TPU v7x, 512 devices: a whole 4x8x8 slice. The times are simulated.
512 devices in a mesh: clus: 64 (over x, z, core), coef: 8 (over y).
Axes of the slice: x: 4, y: 8, z: 8, core: 2. Of those that a mesh axis runs over, the one named last changes fastest.
Arguments:
- density: bfloat16 [1024, 128, 256], P('clus', 'coef'), may hold values from -6 to 6
- near_list: int32 [1024, 9], P('clus'), may hold values from 0 to 1023, as said below
- far_list: int32 [128, 27], P('clus'), may hold values from 0 to 127
- near_blocks: bfloat16 [1024, 9, 128, 128], P('clus', None, 'coef'), may hold values from -0.1875 to 0.1875
- basis: bfloat16 [1024, 128, 64], P('clus', 'coef'), may hold values from -0.5 to 0.5
- transfer: bfloat16 [1024, 64, 64], P('clus'), may hold values from -0.25 to 0.25
- coupling: bfloat16 [128, 27, 64, 64], P('clus', None, None, 'coef'), may hold values from -0.15625 to 0.15625
Outputs:
- first: bfloat16 [1024, 128, 256], P('clus', 'coef')
- second: bfloat16 [1024, 128, 256], P('clus', 'coef')
Inputs may be any that keep to these rules, and one draw needn't show every extreme that they name: near_list[i, 0] is i itself; every entry differs from its row's cluster i by at most 4, and entries i + 4 and i - 4 appear wherever they lie in range.
All inputs are finite; a program needn't handle non-finite values.
Results may differ from a plain program's by a relative error of at most 0.014.
Values may be sent and summed in bfloat16 or wider, within the bound.
No kernel may reach another device: no remote copies, remote signals or barrier semaphores. Data moves between devices by JAX's collectives and lax.ppermute only.
A program may use at most 64 MiB of HBM per device.

v0:
```python
import jax
import jax.numpy as jnp
from jax import lax
from jax.sharding import PartitionSpec as P

CHILD = 8
NWIN = 4


def padded(block, sides, width):
    for axis, dim in sides:
        count = lax.axis_size(axis)
        forward = [(i, i + 1) for i in range(count - 1)]
        backward = [(target, source) for source, target in forward]
        low = lax.ppermute(
            lax.slice_in_dim(block, block.shape[dim] - width, None, axis=dim), axis, forward
        )
        high = lax.ppermute(lax.slice_in_dim(block, 0, width, axis=dim), axis, backward)
        block = jnp.concatenate([low, block, high], axis=dim)
    return block


def near_field(extended, near_list, near_blocks, offset):
    local = near_list - offset
    total = jnp.zeros((near_blocks.shape[0], near_blocks.shape[2], extended.shape[2]), jnp.float32)
    for column in range(near_list.shape[1]):
        picked = jnp.take(extended, local[:, column], axis=0)
        total = total + jnp.einsum(
            "cmn,cnr->cmr", near_blocks[:, column], picked, preferred_element_type=jnp.float32
        )
    return total


def lift_leaves(transfer_rows, coeffs):
    upper = coeffs.astype(jnp.bfloat16)
    lower_bits = (coeffs - upper.astype(jnp.float32)).astype(jnp.bfloat16)
    high_part = jnp.einsum("csq,csr->cqr", transfer_rows, upper, preferred_element_type=jnp.float32)
    return high_part + jnp.einsum(
        "csq,csr->cqr", transfer_rows, lower_bits, preferred_element_type=jnp.float32
    )


def far_middle(parent_part, far_list, coupling):
    parents = parent_part.shape[0]
    vectors = parent_part.shape[2]
    parent_coef = lax.psum_scatter(
        parent_part.astype(jnp.bfloat16), "coef", scatter_dimension=1, tiled=True
    )
    share = parent_coef.shape[1]
    far_count = far_list.shape[1]
    every = lax.all_gather(parent_coef, "clus", axis=0, tiled=True)
    picked = jnp.take(every, far_list.reshape(-1), axis=0).reshape(
        parents, far_count, share, vectors
    )
    coupled = jnp.einsum("pkaq,pkqr->par", coupling, picked, preferred_element_type=jnp.float32)
    return lax.psum(coupled.astype(jnp.bfloat16), "coef")


def split_operator(values, near_list, far_list, near_blocks, basis, transfer, coupling):
    leaves = values.shape[0]
    vectors = values.shape[2]
    rank_full = transfer.shape[1]
    parents = leaves // CHILD
    offset = lax.axis_index("clus") * leaves - NWIN
    whole_rows = lax.all_gather(values, "coef", axis=1, tiled=True)
    extended = padded(whole_rows, (("clus", 0),), NWIN)
    near_part = near_field(extended, near_list, near_blocks, offset)
    up_part = jnp.einsum("cms,cmr->csr", basis, values, preferred_element_type=jnp.float32)
    lifted = lift_leaves(transfer, up_part)
    parent_part = jnp.sum(lifted.reshape(parents, CHILD, rank_full, vectors), axis=1)
    far_coef = far_middle(parent_part, far_list, coupling)
    grouped = transfer.reshape(parents, CHILD, rank_full, rank_full)
    lower = jnp.einsum(
        "pcsq,pqr->pcsr", grouped, far_coef, preferred_element_type=jnp.float32
    ).astype(jnp.bfloat16)
    lower = lower.reshape(leaves, rank_full, vectors)
    far_part = jnp.einsum("cms,csr->cmr", basis, lower, preferred_element_type=jnp.float32)
    return (far_part + near_part).astype(jnp.bfloat16)


def body(density, near_list, far_list, near_blocks, basis, transfer, coupling):
    first = split_operator(density, near_list, far_list, near_blocks, basis, transfer, coupling)
    second = split_operator(first, near_list, far_list, near_blocks, basis, transfer, coupling)
    return (first, second)


def solution(mesh):
    placed = (
        P("clus", "coef", None),
        P("clus", None),
        P("clus", None),
        P("clus", None, "coef", None),
        P("clus", "coef", None),
        P("clus", None, None),
        P("clus", None, None, "coef"),
    )
    return jax.shard_map(
        body,
        mesh=mesh,
        in_specs=placed,
        out_specs=(P("clus", "coef", None), P("clus", "coef", None)),
        check_vma=False,
    )
```

profile of v0, /device:TPU:1, one launch (start us, length us, event | category | flops | bytes accessed | tf_op | source)
XLA Modules:
  0.0 416.6 jit_solution(5597286829201910890)
XLA Ops:
  11.5 39.1 %reduce-scatter.7.cloned.1.call-done = bf16[8,512]{1,0:T(8,128)(2,1)} async-done(((bf16[64,512]{1,0:T(8,128)(2,1)}), bf16[8,512]{1,0:T(8,128)(2,1)}) %reduce-scatter.7.cloned.1.call-update) | async-done | bytes 8208
  51.3 57.8 %all_gather.12 = bf16[128,8,256]{2,1,0:T(8,128)(2,1)S(1)} all-gather(bf16[2,8,256]{2,1,0:T(8,128)(2,1)S(1)} %copy.57), channel_id=1, replica_groups=mesh['clus'=64,'coef'=8] {'clus'}, dimensions={0}, use_global_device_ids=true | all-gather | bytes 532480 | tf_op jit(solution)/shard_map/all_gather | solution.py:51
  110.8 1.9 fusion.156
  112.7 2.4 collective-permute-start
  115.1 63.3 %all-reduce.3.cloned.1.call-done = bf16[2,64,256]{2,1,0:T(8,128)(2,1)} async-done(((bf16[2,64,256]{2,1,0:T(8,128)(2,1)}), bf16[2,64,256]{2,1,0:T(8,128)(2,1)}) %all-reduce.3.cloned.1.call-update) | async-done | bytes 65552 | tf_op jit(solution)/shard_map/psum | solution.py:56
  179.5 7.6 %collective-permute-start.1 = (bf16[4,128,256]{2,1,0:T(8,128)(2,1)}, bf16[4,128,256]{2,1,0:T(8,128)(2,1)S(1)}, u32[]{:S(2)}, u32[]{:S(2)}) collective-permute-start(bf16[4,128,256]{2,1,0:T(8,128)(2,1)} %get-tuple-element.15), channel_id=1, source_target_pairs={{8,0},{16,8},{24,16},{32,24},{40,32},{48,40},{56,48},{64,56},{72,6... | collective-permute-start | bytes 786440 | tf_op jit(solution)/shard_map/ppermute | solution.py:18
  188.4 4.2 %collective-permute-done.1 = bf16[4,128,256]{2,1,0:T(8,128)(2,1)S(1)} collective-permute-done((bf16[4,128,256]{2,1,0:T(8,128)(2,1)}, bf16[4,128,256]{2,1,0:T(8,128)(2,1)S(1)}, u32[]{:S(2)}, u32[]{:S(2)}) %collective-permute-start.1) | collective-permute-done | bytes 262176 | tf_op jit(solution)/shard_map/ppermute | solution.py:18
  194.2 1.6 gather_fusion.8
  197.5 1.6 gather_fusion.6
  202.3 1.6 gather_fusion.3
  203.9 1.6 gather_fusion.2
  206.1 1.8 fusion.40
  215.5 30.7 %reduce-scatter.9.cloned.1.call-done = bf16[8,512]{1,0:T(8,128)(2,1)} async-done(((bf16[64,512]{1,0:T(8,128)(2,1)}), bf16[8,512]{1,0:T(8,128)(2,1)}) %reduce-scatter.9.cloned.1.call-update) | async-done | bytes 8208
  246.8 57.9 %all_gather.14 = bf16[128,8,256]{2,1,0:T(8,128)(2,1)S(1)} all-gather(bf16[2,8,256]{2,1,0:T(8,128)(2,1)S(1)} %copy.59), channel_id=1, replica_groups=mesh['clus'=64,'coef'=8] {'clus'}, dimensions={0}, use_global_device_ids=true | all-gather | bytes 532480 | tf_op jit(solution)/shard_map/all_gather | solution.py:51
  306.4 1.9 fusion.155
  308.3 2.4 collective-permute-start.2
  310.7 63.5 %all-reduce.5.cloned.1.call-done = bf16[2,64,256]{2,1,0:T(8,128)(2,1)} async-done(((bf16[2,64,256]{2,1,0:T(8,128)(2,1)}), bf16[2,64,256]{2,1,0:T(8,128)(2,1)}) %all-reduce.5.cloned.1.call-update) | async-done | bytes 65552 | tf_op jit(solution)/shard_map/psum | solution.py:56
  375.3 7.6 %collective-permute-start.3 = (bf16[4,128,256]{2,1,0:T(8,128)(2,1)}, bf16[4,128,256]{2,1,0:T(8,128)(2,1)S(1)}, u32[]{:S(2)}, u32[]{:S(2)}) collective-permute-start(bf16[4,128,256]{2,1,0:T(8,128)(2,1)} %get-tuple-element.13), channel_id=1, source_target_pairs={{8,0},{16,8},{24,16},{32,24},{40,32},{48,40},{56,48},{64,56},{72,6... | collective-permute-start | bytes 786440 | tf_op jit(solution)/shard_map/ppermute | solution.py:18
  383.2 5.2 %collective-permute-done.3 = bf16[4,128,256]{2,1,0:T(8,128)(2,1)S(1)} collective-permute-done((bf16[4,128,256]{2,1,0:T(8,128)(2,1)}, bf16[4,128,256]{2,1,0:T(8,128)(2,1)S(1)}, u32[]{:S(2)}, u32[]{:S(2)}) %collective-permute-start.3) | collective-permute-done | bytes 262176 | tf_op jit(solution)/shard_map/ppermute | solution.py:18
  390.0 1.6 gather_fusion.18
  393.2 1.6 gather_fusion.16
  399.6 1.6 gather_fusion.12
  401.9 1.7 fusion.23
  403.6 1.7 fusion.25
  (143 shorter events, 40.0 us)
Async XLA Ops:
  7.2 1.4 copy-start
  7.2 43.5 %reduce-scatter.7.cloned.1.call-start = ((), (), s32[]{:S(2)}) async-start(), calls=%async_computation.6 | async-start | bytes 73728
  8.9 1.9 copy-start.22
  8.9 2.1 copy-start.21
  9.3 100.6 %copy-start.18 = (bf16[2,27,64,8]{2,3,1,0:T(8,128)(2,1)S(1)}, bf16[2,27,64,8]{2,3,1,0:T(8,128)(2,1)}, u32[]{:S(2)}) copy-start(bf16[2,27,64,8]{2,3,1,0:T(8,128)(2,1)} %param.17) | copy-start | bytes 165892
  10.0 100.8 %all-gather.3.cloned.1.call-start = ((), (), s32[]{:S(2)}) async-start(), calls=%async_computation.3 | async-start | bytes 1179648 | tf_op jit(solution)/shard_map/all_gather | solution.py:65
  10.8 167.6 %all-reduce.3.cloned.1.call-start = ((), (), s32[]{:S(2)}) async-start(), calls=%async_computation.2 | async-start | bytes 131072 | tf_op jit(solution)/shard_map/psum | solution.py:56
  109.1 78.0 %copy-start.17 = (bf16[16,16,64]{2,1,0:T(8,128)(2,1)S(1)}, bf16[16,16,64]{2,1,0:T(8,128)(2,1)}, u32[]{:S(2)}) copy-start(bf16[16,16,64]{2,1,0:T(8,128)(2,1)} %param.15) | copy-start | bytes 98308
  110.8 135.4 %reduce-scatter.9.cloned.1.call-start = ((), (), s32[]{:S(2)}) async-start(), calls=%async_computation.7 | async-start | bytes 73728
  110.8 77.5 %copy-start.1 = (bf16[16,128,256]{2,1,0:T(8,128)(2,1)S(1)}, bf16[16,128,256]{2,1,0:T(8,128)(2,1)}, u32[]{:S(2)}) copy-start(bf16[16,128,256]{2,1,0:T(8,128)(2,1)} %all-gather.3.cloned.1.call-done) | copy-start | bytes 3145732
  112.7 74.6 %collective-permute-start = (bf16[4,128,256]{2,1,0:T(8,128)(2,1)S(1)}, bf16[4,128,256]{2,1,0:T(8,128)(2,1)}, u32[]{:S(2)}, u32[]{:S(2)}) collective-permute-start(bf16[4,128,256]{2,1,0:T(8,128)(2,1)S(1)} %get-tuple-element.16), channel_id=1, source_target_pairs={{0,8},{8,16},{16,24},{24,32},{32,40},{40,48},{48,56},{56,64},{64,7... | collective-permute-start | bytes 786440 | tf_op jit(solution)/shard_map/ppermute | solution.py:15
  179.5 13.1 %collective-permute-start.1 = (bf16[4,128,256]{2,1,0:T(8,128)(2,1)}, bf16[4,128,256]{2,1,0:T(8,128)(2,1)S(1)}, u32[]{:S(2)}, u32[]{:S(2)}) collective-permute-start(bf16[4,128,256]{2,1,0:T(8,128)(2,1)} %get-tuple-element.15), channel_id=1, source_target_pairs={{8,0},{16,8},{24,16},{32,24},{40,32},{48,40},{56,48},{64,56},{72,6... | collective-permute-start | bytes 786440 | tf_op jit(solution)/shard_map/ppermute | solution.py:18
  206.1 1.8 copy-start.16
  206.1 3.1 copy-start.15
  206.1 3.1 copy-start.19
  207.9 1.7 copy-start.14
  214.8 91.6 %all-gather.5.cloned.1.call-start = ((), (), s32[]{:S(2)}) async-start(), calls=%async_computation.5 | async-start | bytes 1179648 | tf_op jit(solution)/shard_map/all_gather | solution.py:65
  215.4 158.8 %all-reduce.5.cloned.1.call-start = ((), (), s32[]{:S(2)}) async-start(), calls=%async_computation.4 | async-start | bytes 131072 | tf_op jit(solution)/shard_map/psum | solution.py:56
  306.4 76.7 %copy-start.2 = (bf16[16,128,256]{2,1,0:T(8,128)(2,1)S(1)}, bf16[16,128,256]{2,1,0:T(8,128)(2,1)}, u32[]{:S(2)}) copy-start(bf16[16,128,256]{2,1,0:T(8,128)(2,1)} %all-gather.5.cloned.1.call-done) | copy-start | bytes 3145732
  308.3 74.8 %collective-permute-start.2 = (bf16[4,128,256]{2,1,0:T(8,128)(2,1)S(1)}, bf16[4,128,256]{2,1,0:T(8,128)(2,1)S(1)}, u32[]{:S(2)}, u32[]{:S(2)}) collective-permute-start(bf16[4,128,256]{2,1,0:T(8,128)(2,1)S(1)} %get-tuple-element.14), channel_id=1, source_target_pairs={{0,8},{8,16},{16,24},{24,32},{32,40},{40,48},{48,56},{56,64},{64,7... | collective-permute-start | bytes 786440 | tf_op jit(solution)/shard_map/ppermute | solution.py:15
  375.3 13.1 %collective-permute-start.3 = (bf16[4,128,256]{2,1,0:T(8,128)(2,1)}, bf16[4,128,256]{2,1,0:T(8,128)(2,1)S(1)}, u32[]{:S(2)}, u32[]{:S(2)}) collective-permute-start(bf16[4,128,256]{2,1,0:T(8,128)(2,1)} %get-tuple-element.13), channel_id=1, source_target_pairs={{8,0},{16,8},{24,16},{32,24},{40,32},{48,40},{56,48},{64,56},{72,6... | collective-permute-start | bytes 786440 | tf_op jit(solution)/shard_map/ppermute | solution.py:18
  401.9 3.5 copy-start.9
  401.9 3.5 copy-start.20
  403.6 2.1 copy-start.8
  (9 other events, 11.0 us)
Sparse Core Ops, SparseCore 0:
  11.3 39.2 reduce-scatter.6
  52.7 40.5 all-gather.2
  110.9 67.4 all-reduce.2
  214.9 31.1 reduce-scatter.8
  248.6 40.5 all-gather.4
  306.5 67.6 all-reduce.4
where the time goes:
time: 417 us
  waiting for transfers between devices  207 us (50%)
  blocking collectives  116 us (28%)
  local copies, waits for them, and re-layouts  38.6 us (9%)
  starting transfers between devices  20.3 us (5%)
  matrix products  19.7 us (5%)
  between operations  14.7 us (4%)
    psum x2, waiting for transfers between devices, far_middle(): return lax.psum(coupled.astype(jnp.bfloat16), 'coef')  127 us
    all_gather x2, blocking collectives, far_middle(): every = lax.all_gather(parent_coef, 'clus', axis=0, tiled=True)  116 us
    unnamed x8, waiting for transfers between devices  71 us
    gather x18, local copies, waits for them, and re-layouts, near_field(): picked = jnp.take(extended, local[:, column], axis=0)  26.9 us
    ppermute x2, starting transfers between devices, padded(): lax.ppermute(lax.slice_in_dim(block, 0, width, axis=dim), axis, backward)  15.2 us
    dot_general x18, matrix products, near_field(): jnp.einsum('cmn,cnr->cmr', near_blocks[:, column], picked, preferred_elem...  12.3 us
    ppermute x2, waiting for transfers between devices, padded(): lax.ppermute(lax.slice_in_dim(block, 0, width, axis=dim), axis, backward)  9.39 us
  transfers between devices with their start and end apart: 10, of which 6 were waited for; matrix products, arithmetic and copies ran while one was open for 3% of the time, Pallas kernels for 0%

commit v1 on v0

v1 whole, which is shorter than its diff:
```python
import functools

import jax
import jax.numpy as jnp
from jax import lax
from jax.experimental import pallas as pl
from jax.experimental.pallas import tpu as pltpu
from jax.sharding import Mesh
from jax.sharding import PartitionSpec as P

BF = jnp.bfloat16
F32 = jnp.float32
LEAVES = 16
ROWS = 16
PANEL = 128
RANK = 64
COLS = 32
PACK = 4
GROUPS = LEAVES // PACK
NEAR_K = 9
FAR_K = 27
NWIN = 4
SHARES = 8
PLANE = 32
VEC0 = 0
PAR0 = VEC0 + GROUPS * ROWS
U0 = PAR0 + 32
CPL0 = U0 + LEAVES // 2 * ROWS
SENT = CPL0 + FAR_K * 8
CLUS = ("x", "z", "core")
TOP = (((0,), (0,)), ((), ()))


def dot(a, b):
    return jnp.dot(a, b, preferred_element_type=F32)


def dot_top(a, b):
    return lax.dot_general(a, b, TOP, preferred_element_type=F32)


def lane_group(shape):
    return lax.broadcasted_iota(jnp.int32, shape, len(shape) - 1) // COLS


def spread(rows):
    rows = rows + pltpu.roll(rows, 64, 1)
    return rows + pltpu.roll(rows, 32, 1)


def pack_parents(first, second):
    group = lane_group((32, 128))
    low = jnp.where(group == 0, first[:32], first[32:])
    high = jnp.where(group == 2, second[:32], second[32:])
    return jnp.where(group < 2, low, high).astype(BF)


def prepare_kernel(d_ref, b_ref, t_ref, c_ref, out_ref):
    u = [dot(b_ref[i], t_ref[i]) for i in range(LEAVES)]
    for m in range(LEAVES // 2):
        pair = jnp.concatenate([u[2 * m], u[2 * m + 1]], axis=1).astype(BF)
        for s in range(SHARES):
            out_ref[s, U0 + ROWS * m : U0 + ROWS * (m + 1), :] = pair
    part = []
    for p in range(2):
        rows = jnp.concatenate(u[8 * p : 8 * p + 8], axis=0).astype(BF)
        part.append(dot_top(rows, d_ref[8 * p : 8 * p + 8].reshape(8 * ROWS, 256)))
    for s in range(SHARES):
        cut = slice(COLS * s, COLS * (s + 1))
        pieces = [part[0][:32, cut], part[0][32:, cut], part[1][:32, cut], part[1][32:, cut]]
        out_ref[s, PAR0 : PAR0 + 32, :] = jnp.concatenate(pieces, axis=1).astype(BF)
        for g in range(GROUPS):
            pieces = [d_ref[PACK * g + l][:, cut] for l in range(PACK)]
            out_ref[s, VEC0 + ROWS * g : VEC0 + ROWS * (g + 1), :] = jnp.concatenate(pieces, axis=1)
    both = jnp.concatenate([c_ref[0].astype(F32), c_ref[1].astype(F32)], axis=2)
    both = both.reshape(FAR_K * 8, 128).astype(BF)
    for s in range(SHARES):
        out_ref[s, CPL0:SENT, :] = both


def parent_kernel(recv_ref, out_ref):
    total = jnp.sum(recv_ref[...].astype(F32), axis=0).astype(BF)
    out_ref[...] = jnp.broadcast_to(total[None], out_ref.shape)


def coupled_kernel(far_ref, pc_ref, recv_ref, out_ref, c_scr, rhs_scr):
    for y in range(SHARES):
        rows = recv_ref[y, CPL0:SENT, :].astype(F32).reshape(FAR_K, 8, 128)
        c_scr[:, 8 * y : 8 * y + 8, :] = rows
    low = c_scr[:, :32, :].reshape(FAR_K * 32, 128).astype(BF)
    high = c_scr[:, 32:, :].reshape(FAR_K * 32, 128).astype(BF)
    side = lax.broadcasted_iota(jnp.int32, (32, 128), 1) // 64
    even = lane_group((RANK, 128)) % 2 == 0
    for p in range(2):
        for k in range(FAR_K):
            parent = far_ref[p, k]
            tile = pc_ref[(parent // 2) % 2, parent // 4]
            rhs_scr[32 * k : 32 * (k + 1), :] = jnp.where(side == parent % 2, tile, jnp.zeros_like(tile))
        rhs = rhs_scr[...]
        acc0 = dot_top(low, rhs)[64 * p : 64 * (p + 1)]
        acc1 = dot_top(high, rhs)[64 * p : 64 * (p + 1)]
        out_ref[p] = spread(jnp.where(even, acc0, acc1)).astype(BF)


def apply_kernel(last, near_idx, *refs):
    if last:
        near_ref, vec_ref, lo_ref, hi_ref, u_ref, c_ref, own_ref, out_ref, v_scr = refs
    else:
        near_ref, vec_ref, lo_ref, hi_ref, u_ref, c_ref, out_ref, pc_ref, v_scr, acc_scr = refs
    g = pl.program_id(0)

    @pl.when(g == 0)
    def _():
        for group in range(GROUPS + 2):
            if group == 0:
                tile = lo_ref[...]
            elif group == GROUPS + 1:
                tile = hi_ref[...]
            elif last:
                tile = vec_ref[:, group - 1]
            else:
                tile = vec_ref[:, ROWS * (group - 1) : ROWS * group, :]
            tile = tile.reshape(PANEL, 128)
            for l in range(PACK):
                v_scr[PACK * group + l] = tile[:, COLS * l : COLS * (l + 1)]
        if not last:
            acc_scr[...] = jnp.zeros_like(acc_scr)

    cols = []
    for l in range(PACK):
        i = PACK * g + l
        lhs = jnp.concatenate([near_ref[:, l, k].reshape(PANEL, PANEL) for k in range(NEAR_K)], axis=1)
        rhs = jnp.concatenate([v_scr[near_idx[i, k]] for k in range(NEAR_K)], axis=0)
        cols.append(dot(lhs, rhs))
    base = pl.multiple_of(U0 + 2 * ROWS * g, ROWS)
    u = u_ref[:, pl.ds(base, 2 * ROWS), :]
    u = jnp.concatenate([u[:, :ROWS].reshape(PANEL, 128), u[:, ROWS:].reshape(PANEL, 128)], axis=1)
    coef = c_ref[g // 2].astype(F32)
    group = lane_group((RANK, 128))
    blocks = [jnp.where(group == l, coef, 0.0) for l in range(PACK)]
    far = dot(u, jnp.concatenate(blocks, axis=0).astype(BF))
    res = (jnp.concatenate(cols, axis=1) + far).astype(BF)
    tile = res.reshape(SHARES, ROWS, 128)
    if last:
        out_ref[:, 0, 0] = own_ref[:, 0]
        out_ref[:, 1, 0] = tile
        return
    out_ref[:, 0] = tile
    x = dot_top(u, res)
    y = jnp.zeros((RANK, 128), F32)
    for l in range(PACK):
        y = y + jnp.where(group == l, x[RANK * l : RANK * (l + 1)], 0.0)
    acc_scr[g // 2] = acc_scr[g // 2] + y

    @pl.when(g == GROUPS - 1)
    def _():
        packed = pack_parents(spread(acc_scr[0]), spread(acc_scr[1]))
        pc_ref[...] = jnp.broadcast_to(packed[None], pc_ref.shape)


def finish_kernel(recv_ref, first_ref, second_ref):
    for o, ref in enumerate((first_ref, second_ref)):
        for g in range(GROUPS):
            for b in range(2):
                tiles = [recv_ref[PACK * b + s, o, g] for s in range(PACK)]
                for l in range(PACK):
                    cut = slice(COLS * l, COLS * (l + 1))
                    ref[PACK * g + l, :, 128 * b : 128 * (b + 1)] = jnp.concatenate([t[:, cut] for t in tiles], axis=1)


def vmem(n):
    return [pl.BlockSpec(memory_space=pltpu.VMEM)] * n


def cost(flops, nbytes):
    return pl.CostEstimate(flops=flops, bytes_accessed=nbytes, transcendentals=0)


def prepare(density, basis, transfer, coupling):
    return pl.pallas_call(
        prepare_kernel,
        out_shape=jax.ShapeDtypeStruct((SHARES, SENT, 128), BF),
        in_specs=vmem(4),
        out_specs=vmem(1)[0],
        cost_estimate=cost(40_000_000, 1_500_000),
        name="prepare",
    )(density, basis, transfer, jnp.swapaxes(coupling, 2, 3))


def first_parents(recv):
    return pl.pallas_call(
        parent_kernel,
        grid=(1,),
        out_shape=jax.ShapeDtypeStruct((PLANE, 32, 128), BF),
        in_specs=[pl.BlockSpec((SHARES, 32, 128), lambda i: (0, PAR0 // 32, 0))],
        out_specs=pl.BlockSpec((PLANE, 32, 128), lambda i: (0, 0, 0)),
        cost_estimate=cost(100_000, 350_000),
        name="parents",
    )(recv)


def couple(far_list, every, recv):
    return pl.pallas_call(
        coupled_kernel,
        out_shape=jax.ShapeDtypeStruct((2, RANK, 128), BF),
        in_specs=[pl.BlockSpec(memory_space=pltpu.SMEM)] + vmem(2),
        out_specs=vmem(1)[0],
        scratch_shapes=[pltpu.VMEM((FAR_K, RANK, 128), F32), pltpu.VMEM((FAR_K * 32, 128), BF)],
        cost_estimate=cost(100_000_000, 1_500_000),
        name="couple",
    )(far_list, every, recv)


def apply(near_idx, near, vec, low, high, recv, coef, own=None):
    last = own is not None
    whole = lambda *shape: pl.BlockSpec(shape, lambda g, idx: (0,) * len(shape))
    share = pl.BlockSpec((SHARES, 1, ROWS, 128), lambda g, idx: (0, g, 0, 0))
    in_specs = [
        pl.BlockSpec((SHARES, PACK, NEAR_K, ROWS, PANEL), lambda g, idx: (0, g, 0, 0, 0)),
        whole(SHARES, GROUPS, ROWS, 128) if last else whole(SHARES, SENT, 128),
        whole(SHARES, ROWS, 128),
        whole(SHARES, ROWS, 128),
        whole(SHARES, SENT, 128),
        whole(2, RANK, 128),
    ]
    scratch = [pltpu.VMEM((LEAVES + 2 * NWIN, PANEL, COLS), BF)]
    operands = [near, vec, low, high, recv, coef]
    if last:
        in_specs.append(share)
        operands.append(own)
        out_shape = jax.ShapeDtypeStruct((SHARES, 2, GROUPS, ROWS, 128), BF)
        out_specs = pl.BlockSpec((SHARES, 2, 1, ROWS, 128), lambda g, idx: (0, 0, g, 0, 0))
    else:
        scratch.append(pltpu.VMEM((2, RANK, 128), F32))
        out_shape = (
            jax.ShapeDtypeStruct((SHARES, GROUPS, ROWS, 128), BF),
            jax.ShapeDtypeStruct((PLANE, 32, 128), BF),
        )
        out_specs = (share, whole(PLANE, 32, 128))
    return pl.pallas_call(
        functools.partial(apply_kernel, last),
        grid_spec=pltpu.PrefetchScalarGridSpec(
            num_scalar_prefetch=1,
            grid=(GROUPS,),
            in_specs=in_specs,
            out_specs=out_specs,
            scratch_shapes=scratch,
        ),
        out_shape=out_shape,
        cost_estimate=cost(300_000_000, 6_000_000),
        name="apply_last" if last else "apply_first",
    )(near_idx, *operands)


def finish(recv):
    out = jax.ShapeDtypeStruct((LEAVES, ROWS, 256), BF)
    return pl.pallas_call(
        finish_kernel,
        out_shape=(out, out),
        in_specs=vmem(1),
        out_specs=tuple(vmem(2)),
        cost_estimate=cost(100_000, 600_000),
        name="finish",
    )(recv)


def gather_parents(packed):
    plane = lax.all_to_all(packed, ("x", "z"), 0, 0)
    return lax.all_gather(plane, "core", axis=0)


def halo(bottom, top):
    count = 64
    forward = [(i, i + 1) for i in range(count - 1)]
    backward = [(target, source) for source, target in forward]
    return lax.ppermute(top, CLUS, forward), lax.ppermute(bottom, CLUS, backward)


def body(density, near_list, far_list, near_blocks, basis, transfer, coupling):
    near = lax.all_gather(near_blocks, "y", axis=0)
    near_idx = near_list - (lax.axis_index(CLUS) * LEAVES - NWIN)
    near_idx = jnp.clip(near_idx, 0, LEAVES + 2 * NWIN - 1)
    recv = lax.all_to_all(prepare(density, basis, transfer, coupling), "y", 0, 0)
    every = gather_parents(first_parents(recv))
    low, high = halo(recv[:, :ROWS], recv[:, ROWS * (GROUPS - 1) : ROWS * GROUPS])
    coef = couple(far_list, every, recv)
    first, parents = apply(near_idx, near, recv, low, high, recv, coef)
    low, high = halo(first[:, 0], first[:, GROUPS - 1])
    every = gather_parents(parents)
    coef = couple(far_list, every, recv)
    sent = apply(near_idx, near, first, low, high, recv, coef, own=first)
    return finish(lax.all_to_all(sent, "y", 0, 0))


def solution(mesh):
    fine = Mesh(mesh.devices.reshape(4, 8, 2, 8), ("x", "z", "core", "y"))
    placed = (
        P(CLUS, "y", None),
        P(CLUS, None),
        P(CLUS, None),
        P(CLUS, None, "y", None),
        P(CLUS, "y", None),
        P(CLUS, None, None),
        P(CLUS, None, None, "y"),
    )
    return jax.shard_map(
        body,
        mesh=fine,
        in_specs=placed,
        out_specs=(P(CLUS, "y", None), P(CLUS, "y", None)),
        check_vma=False,
    )
```

time: 417 us -> 158 us (0.38)
  waiting for transfers between devices: 207 us -> 6.58 us
  blocking collectives: 116 us -> 59.7 us
  local copies, waits for them, and re-layouts: 38.6 us -> 2.79 us
  starting transfers between devices: 20.3 us -> 46.9 us
  Pallas kernels: 0 us -> 26.3 us
  matrix products: 19.7 us -> 0 us
    psum x2 -> x0, waiting for transfers between devices: 127 us -> none  [far_middle(): return lax.psum(coupled.astype(jnp.bfloat16), 'coef')]
    all_gather x2, blocking collectives: 116 us -> 11.9 us  [gather_parents(): return lax.all_gather(plane, 'core', axis=0)]
    unnamed x8 -> x1, waiting for transfers between devices: 71 us -> 0.68 us
    all_to_all x0 -> x2, blocking collectives: none -> 47.8 us  [the longest x1 32.4 us: body(): lax.all_to_all(prepare(density, basis, transfer, coupling), 'y', 0, 0)]
    all_to_all x0 -> x2, starting transfers between devices: none -> 32.5 us  [gather_parents(): plane = lax.all_to_all(packed, ('x', 'z'), 0, 0)]
    gather x20 -> x0, local copies, waits for them, and re-layouts: 28.1 us -> none  [the longest x18 26.9 us: near_field(): picked = jnp.take(extended, local[:, column], axis=0)]
    pallas_call x0 -> x7, Pallas kernels: none -> 26.3 us  [the longest x2 14.2 us: apply(): pl.pallas_call(functools.partial(apply_kernel, last), grid_spec=pltpu.Pre...]
    dot_general x30 -> x0, matrix products: 19.7 us -> none  [the longest x18 12.3 us: near_field(): jnp.einsum('cmn,cnr->cmr', near_blocks[:, column], picked, preferred_elem...]
  transfers between devices with their start and end apart: 10 -> 7, of which waited for: 6 -> 2; matrix products, arithmetic and copies ran while one was open for 3% -> 1% of each run, Pallas kernels for 0% -> 7%
where the time goes in v1:
time: 158 us; the launch traced here: 157 us
  blocking collectives  59.7 us (38%)
  starting transfers between devices  46.9 us (30%)
  Pallas kernels  26.3 us (17%)
  between operations  14.1 us (9%)
  waiting for transfers between devices  6.58 us (4%)
  local copies, waits for them, and re-layouts  2.79 us (2%)
    all_to_all x2, starting transfers between devices, gather_parents(): plane = lax.all_to_all(packed, ('x', 'z'), 0, 0)  32.5 us
    all_to_all x1, blocking collectives, body(): lax.all_to_all(prepare(density, basis, transfer, coupling), 'y', 0, 0)  32.4 us
    all_to_all x1, blocking collectives, body(): return finish(lax.all_to_all(sent, 'y', 0, 0))  15.4 us
    pallas_call x2, Pallas kernels, apply(): pl.pallas_call(functools.partial(apply_kernel, last), grid_spec=pltpu.Pre...  14.2 us
    all_gather x2, blocking collectives, gather_parents(): return lax.all_gather(plane, 'core', axis=0)  11.9 us
    ppermute x2, starting transfers between devices, halo(): lax.ppermute(top, CLUS, forward)  10.5 us
    pallas_call x2, Pallas kernels, couple(): pl.pallas_call(coupled_kernel, out_shape=jax.ShapeDtypeStruct((2, RANK, 1...  6.21 us
    ppermute x2, starting transfers between devices, halo(): lax.ppermute(bottom, CLUS, backward)  3.84 us
  transfers between devices with their start and end apart: 7, of which 2 were waited for; matrix products, arithmetic and copies ran while one was open for 1% of the time, Pallas kernels for 7%

profile of v1, /device:TPU:1, one launch (start us, length us, event | category | flops | bytes accessed | tf_op | source)
XLA Modules:
  0.0 157.0 jit_solution(9377716649971950034)
XLA Ops:
  7.2 0.7 all-gather.5.cloned.1.call-update
  7.9 2.5 %prepare.1 = bf16[8,440,128]{2,1,0:T(8,128)(2,1)} custom-call(bf16[16,16,256]{2,1,0:T(8,128)(2,1)} %d_ref.1, bf16[16,16,64]{2,1,0:T(8,128)(2,1)} %b_ref.1, bf16[16,64,64]{2,1,0:T(8,128)(2,1)} %t_ref.1, bf16[2,27,8,64]{3,2,1,0:T(8,128)(2,1)} %bitcast.12), custom_call_target="tpu_custom_call" | custom-call | flops 40000000 | bytes 1500000 | tf_op jit(solution)/shard_map/prepare/pallas_call | solution.py:180
  10.4 32.4 %all_to_all.20.recv_ref.refs_1_.refs_4_ = bf16[8,440,128]{2,1,0:T(8,128)(2,1)} all-to-all(bf16[8,440,128]{2,1,0:T(8,128)(2,1)} %prepare.1), channel_id=1, replica_groups=mesh['x'=4,'z'=8,'core'=2,'y'=8] {'y'}, dimensions={0} | all-to-all | bytes 1802240 | tf_op jit(solution)/shard_map/all_to_all | solution.py:283
  42.8 1.6 parents.1
  44.4 19.7 %all-to-all-start.1 = ((bf16[32,32,128]{2,1,0:T(8,128)(2,1)}), bf16[32,32,128]{2,1,0:T(8,128)(2,1)S(1)}, u32[]{:S(2)}, u32[]{:S(2)}) async-start(bf16[32,32,128]{2,1,0:T(8,128)(2,1)} %parents.1), calls=%async_computation.1 | async-start | bytes 524288 | tf_op jit(solution)/shard_map/all_to_all | solution.py:268
  64.6 0.8 fusion
  65.4 6.4 %collective-permute-start = (bf16[8,16,128]{2,1,0:T(8,128)(2,1)S(1)}, bf16[8,16,128]{2,1,0:T(8,128)(2,1)S(1)}, u32[]{:S(2)}, u32[]{:S(2)}) collective-permute-start(bf16[8,16,128]{2,1,0:T(8,128)(2,1)S(1)} %get-tuple-element.7), channel_id=1, source_target_pairs={{0,8},{8,16},{16,24},{24,32},{32,40},{40,48},{48,56},{56,64},{64,7... | collective-permute-start | bytes 98312 | tf_op jit(solution)/shard_map/ppermute | solution.py:276
  71.8 1.9 %collective-permute-start.1 = (bf16[8,16,128]{2,1,0:T(8,128)(2,1)S(1)}, bf16[8,16,128]{2,1,0:T(8,128)(2,1)S(1)}, u32[]{:S(2)}, u32[]{:S(2)}) collective-permute-start(bf16[8,16,128]{2,1,0:T(8,128)(2,1)S(1)} %get-tuple-element.6), channel_id=1, source_target_pairs={{8,0},{16,8},{24,16},{32,24},{40,32},{48,40},{56,48},{64,56},{72,6... | collective-permute-start | bytes 98312 | tf_op jit(solution)/shard_map/ppermute | solution.py:276
  73.8 6.3 %all-gather.1 = bf16[64,32,128]{2,1,0:T(8,128)(2,1)} all-gather(bf16[32,32,128]{2,1,0:T(8,128)(2,1)S(1)} %all-to-all-done.1), channel_id=3, replica_groups=mesh['x'=4,'z'=8,'core'=2,'y'=8] {'core'}, dimensions={0}, use_global_device_ids=true | all-gather | bytes 786432 | tf_op jit(solution)/shard_map/all_gather | solution.py:269
  80.1 3.1 %couple.2.refs_5_ = bf16[2,64,128]{2,1,0:T(8,128)(2,1)} custom-call(s32[2,27]{1,0:T(2,128)} %far_ref.3, bf16[2,32,32,128]{3,2,1,0:T(8,128)(2,1)} %bitcast.10, bf16[8,440,128]{2,1,0:T(8,128)(2,1)} %all_to_all.20.recv_ref.refs_1_.refs_4_), custom_call_target="tpu_custom_call" | custom-call | flops 100000000 | bytes 1500000 | tf_op jit(solution)/shard_map/couple/pallas_call | solution.py:203
  83.2 3.0 %all-gather.5.cloned.1.call-done = bf16[128,9,16,128]{3,2,1,0:T(8,128)(2,1)} async-done(((bf16[16,9,16,128]{3,2,1,0:T(8,128)(2,1)}), bf16[128,9,16,128]{3,2,1,0:T(8,128)(2,1)}) %all-gather.5.cloned.1.call-update) | async-done | bytes 4718608 | tf_op jit(solution)/shard_map/all_gather | solution.py:280
  86.2 7.6 %apply_first.1 = (bf16[8,4,16,128]{3,2,1,0:T(8,128)(2,1)}, bf16[32,32,128]{2,1,0:T(8,128)(2,1)}) custom-call(s32[16,9]{1,0:T(8,128)} %subtract_clamp_fusion.near_idx, bf16[8,16,9,16,128]{4,3,2,1,0:T(8,128)(2,1)} %bitcast.8, bf16[8,440,128]{2,1,0:T(8,128)(2,1)} %all_to_all.20.recv_ref.refs_1_.refs_4_, bf16[8,16,128]{2,1,0:T(8,128)(2,1)} %copy-done, ...), custom_call_target="tpu_custom_call" | custom-call | flops 300000000 | bytes 6000000 | tf_op jit(solution)/shard_map/apply_first/pallas_call | solution.py:240
  93.8 12.9 %all-to-all-start.2 = ((bf16[32,32,128]{2,1,0:T(8,128)(2,1)}), bf16[32,32,128]{2,1,0:T(8,128)(2,1)S(1)}, u32[]{:S(2)}, u32[]{:S(2)}) async-start(bf16[32,32,128]{2,1,0:T(8,128)(2,1)} %get-tuple-element.5), calls=%async_computation.2 | async-start | bytes 524288 | tf_op jit(solution)/shard_map/all_to_all | solution.py:268
  106.7 0.8 slice_bitcast_fusion
  107.5 4.1 %collective-permute-start.2 = (bf16[8,16,128]{2,1,0:T(8,128)(2,1)S(1)}, bf16[8,16,128]{2,1,0:T(8,128)(2,1)S(1)}, u32[]{:S(2)}, u32[]{:S(2)}) collective-permute-start(bf16[8,16,128]{2,1,0:T(8,128)(2,1)S(1)} %get-tuple-element.9), channel_id=1, source_target_pairs={{0,8},{8,16},{16,24},{24,32},{32,40},{40,48},{48,56},{56,64},{64,7... | collective-permute-start | bytes 98312 | tf_op jit(solution)/shard_map/ppermute | solution.py:276
  111.6 1.9 %collective-permute-start.3 = (bf16[8,16,128]{2,1,0:T(8,128)(2,1)S(1)}, bf16[8,16,128]{2,1,0:T(8,128)(2,1)S(1)}, u32[]{:S(2)}, u32[]{:S(2)}) collective-permute-start(bf16[8,16,128]{2,1,0:T(8,128)(2,1)S(1)} %get-tuple-element.8), channel_id=1, source_target_pairs={{8,0},{16,8},{24,16},{32,24},{40,32},{48,40},{56,48},{64,56},{72,6... | collective-permute-start | bytes 98312 | tf_op jit(solution)/shard_map/ppermute | solution.py:276
  113.5 2.9 %all-to-all-done.2 = bf16[32,32,128]{2,1,0:T(8,128)(2,1)S(1)} async-done(((bf16[32,32,128]{2,1,0:T(8,128)(2,1)}), bf16[32,32,128]{2,1,0:T(8,128)(2,1)S(1)}, u32[]{:S(2)}, u32[]{:S(2)}) %all-to-all-start.2) | async-done | bytes 262176 | tf_op jit(solution)/shard_map/all_to_all | solution.py:268
  116.4 5.6 %all-gather.2 = bf16[64,32,128]{2,1,0:T(8,128)(2,1)} all-gather(bf16[32,32,128]{2,1,0:T(8,128)(2,1)S(1)} %all-to-all-done.2), channel_id=4, replica_groups=mesh['x'=4,'z'=8,'core'=2,'y'=8] {'core'}, dimensions={0}, use_global_device_ids=true | all-gather | bytes 786432 | tf_op jit(solution)/shard_map/all_gather | solution.py:269
  122.0 3.1 %couple.3.refs_5_ = bf16[2,64,128]{2,1,0:T(8,128)(2,1)} custom-call(s32[2,27]{1,0:T(2,128)} %far_ref.3, bf16[2,32,32,128]{3,2,1,0:T(8,128)(2,1)} %bitcast.11, bf16[8,440,128]{2,1,0:T(8,128)(2,1)} %all_to_all.20.recv_ref.refs_1_.refs_4_), custom_call_target="tpu_custom_call" | custom-call | flops 100000000 | bytes 1500000 | tf_op jit(solution)/shard_map/couple/pallas_call | solution.py:203
  125.1 0.6 copy-done.1
  125.7 0.6 copy-done.3
  126.3 6.5 %apply_last.1 = bf16[8,2,4,16,128]{4,3,2,1,0:T(8,128)(2,1)} custom-call(s32[16,9]{1,0:T(8,128)} %subtract_clamp_fusion.near_idx, bf16[8,16,9,16,128]{4,3,2,1,0:T(8,128)(2,1)} %bitcast.9, bf16[8,4,16,128]{3,2,1,0:T(8,128)(2,1)} %get-tuple-element.4.refs_1_.refs_6_, bf16[8,16,128]{2,1,0:T(8,128)(2,1)} %copy-done.1, bf16[8,16,128]{2,1,0:T(8,128)(2,1)} %copy-done.3, ...), custom_call_target="tpu_custom_call" | custom-call | flops 300000000 | bytes 6000000 | tf_op jit(solution)/shard_map/apply_last/pallas_call | solution.py:240
  132.9 15.4 %all_to_all.21.recv_ref = bf16[8,2,4,16,128]{4,3,2,1,0:T(8,128)(2,1)} all-to-all(bf16[8,2,4,16,128]{4,3,2,1,0:T(8,128)(2,1)} %apply_last.1), channel_id=1, replica_groups=mesh['x'=4,'z'=8,'core'=2,'y'=8] {'y'}, dimensions={0} | all-to-all | bytes 524288 | tf_op jit(solution)/shard_map/all_to_all | solution.py:292
  148.3 1.9 %finish.1 = (bf16[16,16,256]{2,1,0:T(8,128)(2,1)}, bf16[16,16,256]{2,1,0:T(8,128)(2,1)}) custom-call(bf16[8,2,4,16,128]{4,3,2,1,0:T(8,128)(2,1)} %all_to_all.21.recv_ref), custom_call_target="tpu_custom_call" | custom-call | flops 100000 | bytes 600000 | tf_op jit(solution)/shard_map/finish/pallas_call | solution.py:257
  (15 shorter events, 0.7 us)
Async XLA Ops:
  7.2 56.9 %copy-start.4 = (s32[16,9]{1,0:T(8,128)S(1)}, s32[16,9]{1,0:T(8,128)}, u32[]{:S(2)}) copy-start(s32[16,9]{1,0:T(8,128)} %param.8) | copy-start | bytes 1732
  7.2 79.0 %all-gather.5.cloned.1.call-start = ((), (), s32[]{:S(2)}) async-start(), calls=%async_computation.4 | async-start | bytes 5308416 | tf_op jit(solution)/shard_map/all_gather | solution.py:280
  44.4 29.4 %all-to-all-start.1 = ((bf16[32,32,128]{2,1,0:T(8,128)(2,1)}), bf16[32,32,128]{2,1,0:T(8,128)(2,1)S(1)}, u32[]{:S(2)}, u32[]{:S(2)}) async-start(bf16[32,32,128]{2,1,0:T(8,128)(2,1)} %parents.1), calls=%async_computation.1 | async-start | bytes 524288 | tf_op jit(solution)/shard_map/all_to_all | solution.py:268
  65.4 17.8 %collective-permute-start = (bf16[8,16,128]{2,1,0:T(8,128)(2,1)S(1)}, bf16[8,16,128]{2,1,0:T(8,128)(2,1)S(1)}, u32[]{:S(2)}, u32[]{:S(2)}) collective-permute-start(bf16[8,16,128]{2,1,0:T(8,128)(2,1)S(1)} %get-tuple-element.7), channel_id=1, source_target_pairs={{0,8},{8,16},{16,24},{24,32},{32,40},{40,48},{48,56},{56,64},{64,7... | collective-permute-start | bytes 98312 | tf_op jit(solution)/shard_map/ppermute | solution.py:276
  71.8 11.3 %collective-permute-start.1 = (bf16[8,16,128]{2,1,0:T(8,128)(2,1)S(1)}, bf16[8,16,128]{2,1,0:T(8,128)(2,1)S(1)}, u32[]{:S(2)}, u32[]{:S(2)}) collective-permute-start(bf16[8,16,128]{2,1,0:T(8,128)(2,1)S(1)} %get-tuple-element.6), channel_id=1, source_target_pairs={{8,0},{16,8},{24,16},{32,24},{40,32},{48,40},{56,48},{64,56},{72,6... | collective-permute-start | bytes 98312 | tf_op jit(solution)/shard_map/ppermute | solution.py:276
  83.2 3.0 %copy-start = (bf16[8,16,128]{2,1,0:T(8,128)(2,1)}, bf16[8,16,128]{2,1,0:T(8,128)(2,1)S(1)}, u32[]{:S(2)}) copy-start(bf16[8,16,128]{2,1,0:T(8,128)(2,1)S(1)} %collective-permute-done.refs_2_) | copy-start | bytes 98308
  83.2 3.0 %copy-start.2 = (bf16[8,16,128]{2,1,0:T(8,128)(2,1)}, bf16[8,16,128]{2,1,0:T(8,128)(2,1)S(1)}, u32[]{:S(2)}) copy-start(bf16[8,16,128]{2,1,0:T(8,128)(2,1)S(1)} %collective-permute-done.1.refs_3_) | copy-start | bytes 98308
  93.8 22.6 %all-to-all-start.2 = ((bf16[32,32,128]{2,1,0:T(8,128)(2,1)}), bf16[32,32,128]{2,1,0:T(8,128)(2,1)S(1)}, u32[]{:S(2)}, u32[]{:S(2)}) async-start(bf16[32,32,128]{2,1,0:T(8,128)(2,1)} %get-tuple-element.5), calls=%async_computation.2 | async-start | bytes 524288 | tf_op jit(solution)/shard_map/all_to_all | solution.py:268
  107.5 17.6 %collective-permute-start.2 = (bf16[8,16,128]{2,1,0:T(8,128)(2,1)S(1)}, bf16[8,16,128]{2,1,0:T(8,128)(2,1)S(1)}, u32[]{:S(2)}, u32[]{:S(2)}) collective-permute-start(bf16[8,16,128]{2,1,0:T(8,128)(2,1)S(1)} %get-tuple-element.9), channel_id=1, source_target_pairs={{0,8},{8,16},{16,24},{24,32},{32,40},{40,48},{48,56},{56,64},{64,7... | collective-permute-start | bytes 98312 | tf_op jit(solution)/shard_map/ppermute | solution.py:276
  111.6 13.5 %collective-permute-start.3 = (bf16[8,16,128]{2,1,0:T(8,128)(2,1)S(1)}, bf16[8,16,128]{2,1,0:T(8,128)(2,1)S(1)}, u32[]{:S(2)}, u32[]{:S(2)}) collective-permute-start(bf16[8,16,128]{2,1,0:T(8,128)(2,1)S(1)} %get-tuple-element.8), channel_id=1, source_target_pairs={{8,0},{16,8},{24,16},{32,24},{40,32},{48,40},{56,48},{64,56},{72,6... | collective-permute-start | bytes 98312 | tf_op jit(solution)/shard_map/ppermute | solution.py:276
  125.1 0.6 copy-start.1
  125.7 0.6 copy-start.3
Sparse Core Ops, SparseCore 0:
  10.1 76.1 all-gather.4

commit v2 on v0

v2 whole, which is shorter than its diff:
```python
import jax
import jax.numpy as jnp
from jax import lax
from jax.experimental import pallas as pl
from jax.experimental.pallas import tpu as pltpu
from jax.sharding import Mesh
from jax.sharding import PartitionSpec as P

BF = jnp.bfloat16
F32 = jnp.float32
LEAVES = 16
ROWS = 16
PANEL = 128
RANK = 64
COLS = 32
PACK = 4
GROUPS = LEAVES // PACK
NEAR_K = 9
FAR_K = 27
NWIN = 4
SHARES = 8
PLANE = 32
PAR0 = GROUPS * ROWS
SENT = PAR0 + 32
BAS0 = LEAVES * NEAR_K * ROWS
CPL0 = BAS0 + LEAVES // 2 * ROWS
HELD = CPL0 + FAR_K * 8
HALF = FAR_K * 32
CLUS = ("x", "z", "core")
TOP = (((0,), (0,)), ((), ()))
ANY = pl.BlockSpec(memory_space=pl.ANY)
SMEM = pl.BlockSpec(memory_space=pltpu.SMEM)
VMEM = pl.BlockSpec(memory_space=pltpu.VMEM)


def dot(a, b):
    return jnp.dot(a, b, preferred_element_type=F32)


def dot_top(a, b):
    return lax.dot_general(a, b, TOP, preferred_element_type=F32)


def lane_group(shape):
    return lax.broadcasted_iota(jnp.int32, shape, len(shape) - 1) // COLS


def spread(rows):
    rows = rows + pltpu.roll(rows, 64, 1)
    return rows + pltpu.roll(rows, 32, 1)


def pack_parents(first, second):
    group = lane_group((32, 128))
    low = jnp.where(group == 0, first[:32], first[32:])
    high = jnp.where(group == 2, second[:32], second[32:])
    return jnp.where(group < 2, low, high).astype(BF)


def stack_kernel(near_ref, b_ref, c_ref, out_ref):
    out_ref[:BAS0] = near_ref[...].reshape(BAS0, PANEL)
    for m in range(LEAVES // 2):
        row = BAS0 + ROWS * m
        out_ref[row : row + ROWS] = jnp.concatenate([b_ref[2 * m], b_ref[2 * m + 1]], axis=1)
    both = jnp.concatenate([c_ref[0].astype(F32), c_ref[1].astype(F32)], axis=2)
    out_ref[CPL0:] = both.reshape(FAR_K * 8, 128).astype(BF)


def prepare_kernel(d_ref, b_ref, t_ref, out_ref):
    part = []
    for p in range(2):
        u = [dot(b_ref[i], t_ref[i]) for i in range(8 * p, 8 * p + 8)]
        rows = jnp.concatenate(u, axis=0).astype(BF)
        part.append(dot_top(rows, d_ref[8 * p : 8 * p + 8].reshape(8 * ROWS, 256)))
    for s in range(SHARES):
        cut = slice(COLS * s, COLS * (s + 1))
        pieces = [part[0][:32, cut], part[0][32:, cut], part[1][:32, cut], part[1][32:, cut]]
        out_ref[s, PAR0:SENT, :] = jnp.concatenate(pieces, axis=1).astype(BF)
        for g in range(GROUPS):
            pieces = [d_ref[PACK * g + l][:, cut] for l in range(PACK)]
            out_ref[s, ROWS * g : ROWS * (g + 1), :] = jnp.concatenate(pieces, axis=1)


def parent_kernel(recv_ref, out_ref, bottom_ref, top_ref):
    total = jnp.sum(recv_ref[:, PAR0:SENT, :].astype(F32), axis=0).astype(BF)
    out_ref[...] = jnp.broadcast_to(total[None], out_ref.shape)
    bottom_ref[...] = recv_ref[:, :ROWS, :]
    top_ref[...] = recv_ref[:, PAR0 - ROWS : PAR0, :]


def far_sums(far_ref, pc_ref, cpl, rhs_scr):
    side = lax.broadcasted_iota(jnp.int32, (32, 128), 1) // 64
    even = lane_group((RANK, 128)) % 2 == 0
    sums = []
    for p in range(2):
        for k in range(FAR_K):
            parent = far_ref[p, k]
            tile = pc_ref[(parent // 2) % 2, parent // 4]
            rhs_scr[32 * k : 32 * (k + 1), :] = jnp.where(side == parent % 2, tile, jnp.zeros_like(tile))
        rhs = rhs_scr[...]
        acc0 = dot(cpl[0][RANK * p : RANK * (p + 1)], rhs)
        acc1 = dot(cpl[1][RANK * p : RANK * (p + 1)], rhs)
        sums.append(spread(jnp.where(even, acc0, acc1)).astype(BF).astype(F32))
    return sums


def far_field(u, coef):
    group = lane_group((RANK, 128))
    blocks = [jnp.where(group == l, coef, 0.0) for l in range(PACK)]
    return dot(u, jnp.concatenate(blocks, axis=0).astype(BF))


def near_copies(w_ref, near_scr, sems):
    size = NEAR_K * ROWS
    return [
        pltpu.make_async_copy(w_ref.at[:, pl.ds(size * i, size), :], near_scr.at[i], sems.at[i])
        for i in range(LEAVES)
    ]


def unpack(tiles, v_scr):
    for n, tile in enumerate(tiles):
        for l in range(PACK):
            v_scr[PACK * n + l] = tile[:, COLS * l : COLS * (l + 1)]


def near_field(g, idx_ref, copies, near_scr, v_scr):
    cols = []
    for i in range(PACK * g, PACK * (g + 1)):
        copies[i].wait()
        parts = [near_scr[i, :, ROWS * k : ROWS * (k + 1), :].reshape(PANEL, PANEL) for k in range(NEAR_K)]
        rhs = jnp.concatenate([v_scr[idx_ref[i, k]] for k in range(NEAR_K)], axis=0)
        cols.append(dot(jnp.concatenate(parts, axis=1), rhs))
    return jnp.concatenate(cols, axis=1)


def first_kernel(
    far_ref, idx_ref, pc_ref, w_ref, t_ref, recv_ref, lo_ref, hi_ref,
    out_ref, par_ref, bottom_ref, top_ref, cpl_ref, u_ref,
    near_scr, own_scr, c_scr, rhs_scr, v_scr, sems, own_sem,
):
    own = pltpu.make_async_copy(w_ref.at[:, pl.ds(BAS0, HELD - BAS0), :], own_scr, own_sem)
    own.start()
    copies = near_copies(w_ref, near_scr, sems)
    for copy in copies:
        copy.start()
    tiles = [lo_ref[...]] + [recv_ref[:, ROWS * g : ROWS * (g + 1), :] for g in range(GROUPS)] + [hi_ref[...]]
    unpack([tile.reshape(PANEL, 128) for tile in tiles], v_scr)
    own.wait()
    for y in range(SHARES):
        rows = own_scr[y, CPL0 - BAS0 :, :].astype(F32).reshape(FAR_K, 8, 128)
        c_scr[:, 8 * y : 8 * y + 8, :] = rows
    cpl = [c_scr[:, 32 * h : 32 * (h + 1), :].reshape(HALF, 128).T.astype(BF) for h in range(2)]
    for h in range(2):
        cpl_ref[h] = cpl[h]
    zero = jnp.zeros((RANK, RANK), BF)
    for m in range(LEAVES // 2):
        rows = own_scr[:, ROWS * m : ROWS * (m + 1), :].reshape(PANEL, 128)
        upper = jnp.concatenate([t_ref[2 * m], zero], axis=1)
        lower = jnp.concatenate([zero, t_ref[2 * m + 1]], axis=1)
        pair = dot(rows, jnp.concatenate([upper, lower], axis=0)).astype(BF)
        u_ref[m // 2, :, 128 * (m % 2) : 128 * (m % 2 + 1)] = pair
    coef = far_sums(far_ref, pc_ref, cpl, rhs_scr)
    group = lane_group((RANK, 128))
    parents = [jnp.zeros((RANK, 128), F32), jnp.zeros((RANK, 128), F32)]
    for g in range(GROUPS):
        u = u_ref[g]
        res = (near_field(g, idx_ref, copies, near_scr, v_scr) + far_field(u, coef[g // 2])).astype(BF)
        tile = res.reshape(SHARES, ROWS, 128)
        out_ref[:, g] = tile
        if g == 0:
            bottom_ref[...] = tile
        if g == GROUPS - 1:
            top_ref[...] = tile
        x = dot_top(u, res)
        for l in range(PACK):
            parents[g // 2] += jnp.where(group == l, x[RANK * l : RANK * (l + 1)], 0.0)
    packed = pack_parents(spread(parents[0]), spread(parents[1]))
    par_ref[...] = jnp.broadcast_to(packed[None], par_ref.shape)


def near_kernel(idx_ref, w_ref, vec_ref, lo_ref, hi_ref, out_ref, near_scr, v_scr, sems):
    copies = near_copies(w_ref, near_scr, sems)
    for copy in copies:
        copy.start()
    tiles = [lo_ref[...]] + [vec_ref[:, g] for g in range(GROUPS)] + [hi_ref[...]]
    unpack([tile.reshape(PANEL, 128) for tile in tiles], v_scr)
    for g in range(GROUPS):
        out_ref[g] = near_field(g, idx_ref, copies, near_scr, v_scr)


def last_kernel(far_ref, pc_ref, cpl_ref, u_ref, near_ref, own_ref, out_ref, rhs_scr):
    coef = far_sums(far_ref, pc_ref, (cpl_ref[0], cpl_ref[1]), rhs_scr)
    for g in range(GROUPS):
        res = (near_ref[g] + far_field(u_ref[g], coef[g // 2])).astype(BF)
        out_ref[:, 0, g] = own_ref[:, g]
        out_ref[:, 1, g] = res.reshape(SHARES, ROWS, 128)


def finish_kernel(recv_ref, first_ref, second_ref):
    for o, ref in enumerate((first_ref, second_ref)):
        for g in range(GROUPS):
            for b in range(2):
                tiles = [recv_ref[PACK * b + s, o, g] for s in range(PACK)]
                for l in range(PACK):
                    cut = slice(COLS * l, COLS * (l + 1))
                    ref[PACK * g + l, :, 128 * b : 128 * (b + 1)] = jnp.concatenate([t[:, cut] for t in tiles], axis=1)


def array(*shape, dtype=BF):
    return jax.ShapeDtypeStruct(shape, dtype)


def call(kernel, name, outs, ins, scratch, flops, nbytes, *operands):
    single = not isinstance(outs, tuple)
    return pl.pallas_call(
        kernel,
        out_shape=outs,
        in_specs=ins,
        out_specs=VMEM if single else (VMEM,) * len(outs),
        scratch_shapes=scratch,
        cost_estimate=pl.CostEstimate(flops=flops, bytes_accessed=nbytes, transcendentals=0),
        name=name,
    )(*operands)


def gather_parents(packed):
    plane = lax.all_to_all(packed, ("x", "z"), 0, 0)
    return lax.all_gather(plane, "core", axis=0)


def halo(bottom, top):
    count = 64
    forward = [(i, i + 1) for i in range(count - 1)]
    backward = [(target, source) for source, target in forward]
    return lax.ppermute(top, CLUS, forward), lax.ppermute(bottom, CLUS, backward)


def body(density, near_list, far_list, near_blocks, basis, transfer, coupling):
    share = array(SHARES, ROWS, 128)
    spread_out = array(PLANE, 32, 128)
    near_scratch = pltpu.VMEM((LEAVES, SHARES, NEAR_K * ROWS, PANEL), BF)
    vec_scratch = pltpu.VMEM((LEAVES + 2 * NWIN, PANEL, COLS), BF)
    rhs_scratch = pltpu.VMEM((HALF, 128), BF)
    near_sems = pltpu.SemaphoreType.DMA((LEAVES,))

    mine = call(
        stack_kernel, "stack", array(HELD, PANEL), [VMEM] * 3, [], 0, 1_400_000,
        near_blocks, basis, jnp.swapaxes(coupling, 2, 3),
    )
    held = lax.all_gather(mine, "y", axis=0)
    near_idx = near_list - (lax.axis_index(CLUS) * LEAVES - NWIN)
    near_idx = jnp.clip(near_idx, 0, LEAVES + 2 * NWIN - 1)
    sent = call(
        prepare_kernel, "prepare", array(SHARES, SENT, 128), [VMEM] * 3, [], 40_000_000, 500_000,
        density, basis, transfer,
    )
    recv = lax.all_to_all(sent, "y", 0, 0)
    parents, bottom, top = call(
        parent_kernel, "parents", (spread_out, share, share), [VMEM], [], 100_000, 500_000, recv
    )
    every = gather_parents(parents)
    low, high = halo(bottom, top)
    first, parents, bottom, top, cpl, u = call(
        first_kernel, "first",
        (
            array(SHARES, GROUPS, ROWS, 128), spread_out, share, share,
            array(2, 2 * RANK, HALF), array(GROUPS, PANEL, PACK * RANK),
        ),
        [SMEM, SMEM, VMEM, ANY] + [VMEM] * 4,
        [
            near_scratch,
            pltpu.VMEM((SHARES, HELD - BAS0, 128), BF),
            pltpu.VMEM((FAR_K, RANK, 128), F32),
            rhs_scratch,
            vec_scratch,
            near_sems,
            pltpu.SemaphoreType.DMA,
        ],
        400_000_000, 8_000_000,
        far_list, near_idx, every, held, transfer, recv, low, high,
    )
    plane = lax.all_to_all(parents, ("x", "z"), 0, 0)
    low, high = halo(bottom, top)
    near = call(
        near_kernel, "near", array(GROUPS, PANEL, 128, dtype=F32), [SMEM, ANY] + [VMEM] * 3,
        [near_scratch, vec_scratch, near_sems], 300_000_000, 6_000_000,
        near_idx, held, first, low, high,
    )
    every = lax.all_gather(plane, "core", axis=0)
    sent = call(
        last_kernel, "last", array(SHARES, 2, GROUPS, ROWS, 128), [SMEM] + [VMEM] * 5,
        [rhs_scratch], 100_000_000, 2_000_000,
        far_list, every, cpl, u, near, first,
    )
    out = array(LEAVES, ROWS, 256)
    return call(
        finish_kernel, "finish", (out, out), [VMEM], [], 0, 600_000, lax.all_to_all(sent, "y", 0, 0)
    )


def solution(mesh):
    fine = Mesh(mesh.devices.reshape(4, 8, 2, 8), ("x", "z", "core", "y"))
    placed = (
        P(CLUS, "y", None),
        P(CLUS, None),
        P(CLUS, None),
        P(CLUS, None, "y", None),
        P(CLUS, "y", None),
        P(CLUS, None, None),
        P(CLUS, None, None, "y"),
    )
    return jax.shard_map(
        body,
        mesh=fine,
        in_specs=placed,
        out_specs=(P(CLUS, "y", None), P(CLUS, "y", None)),
        check_vma=False,
    )
```

time: 417 us -> 154 us (0.37)
  waiting for transfers between devices: 207 us -> 29.3 us
  blocking collectives: 116 us -> 41.3 us
  local copies, waits for them, and re-layouts: 38.6 us -> 0.62 us
  Pallas kernels: 0 us -> 28.6 us
  matrix products: 19.7 us -> 0 us
  starting transfers between devices: 20.3 us -> 37.7 us
    psum x2 -> x0, waiting for transfers between devices: 127 us -> none  [far_middle(): return lax.psum(coupled.astype(jnp.bfloat16), 'coef')]
    all_gather x2, blocking collectives: 116 us -> 8.49 us  [the longest x1 6.18 us: gather_parents(): return lax.all_gather(plane, 'core', axis=0)]
    unnamed x8 -> x1, waiting for transfers between devices: 71 us -> 0.02 us
    all_to_all x0 -> x2, blocking collectives: none -> 32.8 us  [the longest x1 16.5 us: body(): recv = lax.all_to_all(sent, 'y', 0, 0)]
    pallas_call x0 -> x7, Pallas kernels: none -> 28.6 us  [call(): pl.pallas_call(kernel, out_shape=outs, in_specs=ins, out_specs=VMEM if si...]
    gather x20 -> x0, local copies, waits for them, and re-layouts: 28.1 us -> none  [the longest x18 26.9 us: near_field(): picked = jnp.take(extended, local[:, column], axis=0)]
    all_gather x2 -> x1, waiting for transfers between devices: 0.04 us -> 25.2 us  [body(): held = lax.all_gather(mine, 'y', axis=0)]
    all_to_all x0 -> x2, starting transfers between devices: none -> 23.6 us  [the longest x1 13.2 us: gather_parents(): plane = lax.all_to_all(packed, ('x', 'z'), 0, 0)]
  transfers between devices with their start and end apart: 10 -> 7, of which waited for: 6 -> 3; matrix products, arithmetic and copies ran while one was open for 3% -> 1% of each run, Pallas kernels for 0% -> 7%
where the time goes in v2:
time: 154 us; the launch traced here: 153 us
  blocking collectives  41.3 us (27%)
  starting transfers between devices  37.7 us (24%)
  waiting for transfers between devices  29.3 us (19%)
  Pallas kernels  28.6 us (19%)
  between operations  14.1 us (9%)
    pallas_call x7, Pallas kernels, call(): pl.pallas_call(kernel, out_shape=outs, in_specs=ins, out_specs=VMEM if si...  28.6 us
    all_gather x1, waiting for transfers between devices, body(): held = lax.all_gather(mine, 'y', axis=0)  25.2 us
    all_to_all x1, blocking collectives, body(): recv = lax.all_to_all(sent, 'y', 0, 0)  16.5 us
    all_to_all x1, blocking collectives, body(): lax.all_to_all(sent, 'y', 0, 0)  16.3 us
    all_to_all x1, starting transfers between devices, gather_parents(): plane = lax.all_to_all(packed, ('x', 'z'), 0, 0)  13.2 us
    all_to_all x1, starting transfers between devices, body(): plane = lax.all_to_all(parents, ('x', 'z'), 0, 0)  10.4 us
    ppermute x2, starting transfers between devices, halo(): lax.ppermute(top, CLUS, forward)  10.3 us
    all_gather x1, blocking collectives, gather_parents(): return lax.all_gather(plane, 'core', axis=0)  6.18 us
  transfers between devices with their start and end apart: 7, of which 3 were waited for; matrix products, arithmetic and copies ran while one was open for 1% of the time, Pallas kernels for 7%

profile of v2, /device:TPU:1, one launch (start us, length us, event | category | flops | bytes accessed | tf_op | source)
XLA Modules:
  0.0 153.0 jit_solution(14434432000539658351)
XLA Ops:
  7.2 0.0 all-gather.5.cloned.1.call-start
  7.2 2.1 %stack.1 = bf16[2648,128]{1,0:T(8,128)(2,1)} custom-call(bf16[16,9,16,128]{3,2,1,0:T(8,128)(2,1)} %near_ref.1, bf16[16,16,64]{2,1,0:T(8,128)(2,1)} %b_ref.3, bf16[2,27,8,64]{3,2,1,0:T(8,128)(2,1)} %bitcast.8), custom_call_target="tpu_custom_call" | custom-call | bytes 1400000 | tf_op jit(solution)/shard_map/stack/pallas_call | solution.py:216
  9.3 0.0 all-gather.5.cloned.1.call-update
  9.3 2.4 %prepare.1 = bf16[8,96,128]{2,1,0:T(8,128)(2,1)} custom-call(bf16[16,16,256]{2,1,0:T(8,128)(2,1)} %d_ref.1, bf16[16,16,64]{2,1,0:T(8,128)(2,1)} %b_ref.3, bf16[16,64,64]{2,1,0:T(8,128)(2,1)} %t_ref.3), custom_call_target="tpu_custom_call" | custom-call | flops 40000000 | bytes 500000 | tf_op jit(solution)/shard_map/prepare/pallas_call | solution.py:216
  11.7 16.5 %all_to_all.20.recv_ref = bf16[8,96,128]{2,1,0:T(8,128)(2,1)} all-to-all(bf16[8,96,128]{2,1,0:T(8,128)(2,1)} %prepare.1), channel_id=1, replica_groups=mesh['x'=4,'z'=8,'core'=2,'y'=8] {'y'}, dimensions={0} | all-to-all | bytes 393216 | tf_op jit(solution)/shard_map/all_to_all | solution.py:258
  28.1 1.6 %parents.1 = (bf16[32,32,128]{2,1,0:T(8,128)(2,1)}, bf16[8,16,128]{2,1,0:T(8,128)(2,1)}, bf16[8,16,128]{2,1,0:T(8,128)(2,1)}) custom-call(bf16[8,96,128]{2,1,0:T(8,128)(2,1)} %all_to_all.20.recv_ref), custom_call_target="tpu_custom_call" | custom-call | flops 100000 | bytes 500000 | tf_op jit(solution)/shard_map/parents/pallas_call | solution.py:216
  29.8 13.2 %all-to-all-start.1 = ((bf16[32,32,128]{2,1,0:T(8,128)(2,1)}), bf16[32,32,128]{2,1,0:T(8,128)(2,1)S(1)}, u32[]{:S(2)}, u32[]{:S(2)}) async-start(bf16[32,32,128]{2,1,0:T(8,128)(2,1)} %get-tuple-element.11), calls=%async_computation.1 | async-start | bytes 524288 | tf_op jit(solution)/shard_map/all_to_all | solution.py:228
  43.0 1.3 subtract_clamp_fusion.idx_ref
  44.3 6.1 %collective-permute-start = (bf16[8,16,128]{2,1,0:T(8,128)(2,1)}, bf16[8,16,128]{2,1,0:T(8,128)(2,1)S(1)}, u32[]{:S(2)}, u32[]{:S(2)}) collective-permute-start(bf16[8,16,128]{2,1,0:T(8,128)(2,1)} %get-tuple-element.12), channel_id=1, source_target_pairs={{0,8},{8,16},{16,24},{24,32},{32,40},{40,48},{48,56},{56,64},{64,7... | collective-permute-start | bytes 98312 | tf_op jit(solution)/shard_map/ppermute | solution.py:236
  50.4 1.9 %collective-permute-start.1 = (bf16[8,16,128]{2,1,0:T(8,128)(2,1)}, bf16[8,16,128]{2,1,0:T(8,128)(2,1)S(1)}, u32[]{:S(2)}, u32[]{:S(2)}) collective-permute-start(bf16[8,16,128]{2,1,0:T(8,128)(2,1)} %get-tuple-element.13), channel_id=1, source_target_pairs={{8,0},{16,8},{24,16},{32,24},{40,32},{48,40},{56,48},{64,56},{72,6... | collective-permute-start | bytes 98312 | tf_op jit(solution)/shard_map/ppermute | solution.py:236
  52.3 0.3 all-to-all-done.1
  52.6 6.2 %all-gather = bf16[64,32,128]{2,1,0:T(8,128)(2,1)} all-gather(bf16[32,32,128]{2,1,0:T(8,128)(2,1)S(1)} %all-to-all-done.1), channel_id=2, replica_groups=mesh['x'=4,'z'=8,'core'=2,'y'=8] {'core'}, dimensions={0}, use_global_device_ids=true | all-gather | bytes 786432 | tf_op jit(solution)/shard_map/all_gather | solution.py:229
  58.8 25.2 %all-gather.5.cloned.1.call-done = bf16[21184,128]{1,0:T(8,128)(2,1)} async-done(((bf16[2648,128]{1,0:T(8,128)(2,1)}), bf16[21184,128]{1,0:T(8,128)(2,1)}) %all-gather.5.cloned.1.call-update) | async-done | bytes 5423120 | tf_op jit(solution)/shard_map/all_gather | solution.py:251
  84.0 10.6 %first.1 = (bf16[8,4,16,128]{3,2,1,0:T(8,128)(2,1)}, bf16[32,32,128]{2,1,0:T(8,128)(2,1)}, bf16[8,16,128]{2,1,0:T(8,128)(2,1)}, bf16[8,16,128]{2,1,0:T(8,128)(2,...) custom-call(s32[2,27]{1,0:T(2,128)} %far_ref.3, s32[16,9]{1,0:T(8,128)} %subtract_clamp_fusion.idx_ref, ...), custom_call_target="tpu_custom_call" | custom-call | flops 400000000 | bytes 8000000 | tf_op jit(solution)/shard_map/first/pallas_call | solution.py:216
  94.6 10.4 %all-to-all-start.2 = ((bf16[32,32,128]{2,1,0:T(8,128)(2,1)}), bf16[32,32,128]{2,1,0:T(8,128)(2,1)S(1)}, u32[]{:S(2)}, u32[]{:S(2)}) async-start(bf16[32,32,128]{2,1,0:T(8,128)(2,1)} %get-tuple-element.14), calls=%async_computation.2 | async-start | bytes 524288 | tf_op jit(solution)/shard_map/all_to_all | solution.py:283
  105.0 4.2 %collective-permute-start.2 = (bf16[8,16,128]{2,1,0:T(8,128)(2,1)}, bf16[8,16,128]{2,1,0:T(8,128)(2,1)S(1)}, u32[]{:S(2)}, u32[]{:S(2)}) collective-permute-start(bf16[8,16,128]{2,1,0:T(8,128)(2,1)} %get-tuple-element.18), channel_id=1, source_target_pairs={{0,8},{8,16},{16,24},{24,32},{32,40},{40,48},{48,56},{56,64},{64,7... | collective-permute-start | bytes 98312 | tf_op jit(solution)/shard_map/ppermute | solution.py:236
  109.2 1.9 %collective-permute-start.3 = (bf16[8,16,128]{2,1,0:T(8,128)(2,1)}, bf16[8,16,128]{2,1,0:T(8,128)(2,1)S(1)}, u32[]{:S(2)}, u32[]{:S(2)}) collective-permute-start(bf16[8,16,128]{2,1,0:T(8,128)(2,1)} %get-tuple-element.19), channel_id=1, source_target_pairs={{8,0},{16,8},{24,16},{32,24},{40,32},{48,40},{56,48},{64,56},{72,6... | collective-permute-start | bytes 98312 | tf_op jit(solution)/shard_map/ppermute | solution.py:236
  111.1 3.8 %collective-permute-done.3.hi_ref = bf16[8,16,128]{2,1,0:T(8,128)(2,1)S(1)} collective-permute-done((bf16[8,16,128]{2,1,0:T(8,128)(2,1)}, bf16[8,16,128]{2,1,0:T(8,128)(2,1)S(1)}, u32[]{:S(2)}, u32[]{:S(2)}) %collective-permute-start.3) | collective-permute-done | bytes 32800 | tf_op jit(solution)/shard_map/ppermute | solution.py:236
  114.9 0.6 copy-done.3
  115.5 6.8 %near.1.near_ref = f32[4,128,128]{2,1,0:T(8,128)} custom-call(s32[16,9]{1,0:T(8,128)} %subtract_clamp_fusion.idx_ref, bf16[8,2648,128]{2,1,0:T(8,128)(2,1)} %bitcast.5, bf16[8,4,16,128]{3,2,1,0:T(8,128)(2,1)} %get-tuple-element.17.vec_ref.own_ref, bf16[8,16,128]{2,1,0:T(8,128)(2,1)} %copy-done.2, bf16[8,16,128]{2,1,0:T(8,128)(2,1)} %copy-done.3), custom_call_target="tpu_custom_call" | custom-call | flops 300000000 | bytes 6000000 | tf_op jit(solution)/shard_map/near/pallas_call | solution.py:216
  122.4 2.3 %all-gather.2 = bf16[64,32,128]{2,1,0:T(8,128)(2,1)} all-gather(bf16[32,32,128]{2,1,0:T(8,128)(2,1)S(1)} %all-to-all-done.2), channel_id=4, replica_groups=mesh['x'=4,'z'=8,'core'=2,'y'=8] {'core'}, dimensions={0}, use_global_device_ids=true | all-gather | bytes 786432 | tf_op jit(solution)/shard_map/all_gather | solution.py:290
  124.7 3.3 %last.1 = bf16[8,2,4,16,128]{4,3,2,1,0:T(8,128)(2,1)} custom-call(s32[2,27]{1,0:T(2,128)} %far_ref.3, bf16[2,32,32,128]{3,2,1,0:T(8,128)(2,1)} %bitcast.6, bf16[2,128,864]{2,1,0:T(8,128)(2,1)} %get-tuple-element.15.cpl_ref, bf16[4,128,256]{2,1,0:T(8,128)(2,1)} %get-tuple-element.16.u_ref, f32[4,128,128]{2,1,0:T(8,128)} %near.1.near_ref, ...), custom_call_target="tpu_custom_call" | custom-call | flops 100000000 | bytes 2000000 | tf_op jit(solution)/shard_map/last/pallas_call | solution.py:216
  128.0 16.3 %all_to_all.21.recv_ref = bf16[8,2,4,16,128]{4,3,2,1,0:T(8,128)(2,1)} all-to-all(bf16[8,2,4,16,128]{4,3,2,1,0:T(8,128)(2,1)} %last.1), channel_id=1, replica_groups=mesh['x'=4,'z'=8,'core'=2,'y'=8] {'y'}, dimensions={0} | all-to-all | bytes 524288 | tf_op jit(solution)/shard_map/all_to_all | solution.py:298
  144.3 1.9 %finish.1 = (bf16[16,16,256]{2,1,0:T(8,128)(2,1)}, bf16[16,16,256]{2,1,0:T(8,128)(2,1)}) custom-call(bf16[8,2,4,16,128]{4,3,2,1,0:T(8,128)(2,1)} %all_to_all.21.recv_ref), custom_call_target="tpu_custom_call" | custom-call | bytes 600000 | tf_op jit(solution)/shard_map/finish/pallas_call | solution.py:216
  (11 shorter events, 0.0 us)
Async XLA Ops:
  7.2 76.8 %all-gather.5.cloned.1.call-start = ((), (), s32[]{:S(2)}) async-start(), calls=%async_computation.4 | async-start | bytes 6100992 | tf_op jit(solution)/shard_map/all_gather | solution.py:251
  29.8 22.8 %all-to-all-start.1 = ((bf16[32,32,128]{2,1,0:T(8,128)(2,1)}), bf16[32,32,128]{2,1,0:T(8,128)(2,1)S(1)}, u32[]{:S(2)}, u32[]{:S(2)}) async-start(bf16[32,32,128]{2,1,0:T(8,128)(2,1)} %get-tuple-element.11), calls=%async_computation.1 | async-start | bytes 524288 | tf_op jit(solution)/shard_map/all_to_all | solution.py:228
  44.3 14.5 %collective-permute-start = (bf16[8,16,128]{2,1,0:T(8,128)(2,1)}, bf16[8,16,128]{2,1,0:T(8,128)(2,1)S(1)}, u32[]{:S(2)}, u32[]{:S(2)}) collective-permute-start(bf16[8,16,128]{2,1,0:T(8,128)(2,1)} %get-tuple-element.12), channel_id=1, source_target_pairs={{0,8},{8,16},{16,24},{24,32},{32,40},{40,48},{48,56},{56,64},{64,7... | collective-permute-start | bytes 98312 | tf_op jit(solution)/shard_map/ppermute | solution.py:236
  50.4 8.4 %collective-permute-start.1 = (bf16[8,16,128]{2,1,0:T(8,128)(2,1)}, bf16[8,16,128]{2,1,0:T(8,128)(2,1)S(1)}, u32[]{:S(2)}, u32[]{:S(2)}) collective-permute-start(bf16[8,16,128]{2,1,0:T(8,128)(2,1)} %get-tuple-element.13), channel_id=1, source_target_pairs={{8,0},{16,8},{24,16},{32,24},{40,32},{48,40},{56,48},{64,56},{72,6... | collective-permute-start | bytes 98312 | tf_op jit(solution)/shard_map/ppermute | solution.py:236
  58.8 25.2 %copy-start = (bf16[8,16,128]{2,1,0:T(8,128)(2,1)}, bf16[8,16,128]{2,1,0:T(8,128)(2,1)S(1)}, u32[]{:S(2)}) copy-start(bf16[8,16,128]{2,1,0:T(8,128)(2,1)S(1)} %collective-permute-done.lo_ref) | copy-start | bytes 98308
  58.8 25.2 %copy-start.1 = (bf16[8,16,128]{2,1,0:T(8,128)(2,1)}, bf16[8,16,128]{2,1,0:T(8,128)(2,1)S(1)}, u32[]{:S(2)}) copy-start(bf16[8,16,128]{2,1,0:T(8,128)(2,1)S(1)} %collective-permute-done.1.hi_ref) | copy-start | bytes 98308
  94.6 27.8 %all-to-all-start.2 = ((bf16[32,32,128]{2,1,0:T(8,128)(2,1)}), bf16[32,32,128]{2,1,0:T(8,128)(2,1)S(1)}, u32[]{:S(2)}, u32[]{:S(2)}) async-start(bf16[32,32,128]{2,1,0:T(8,128)(2,1)} %get-tuple-element.14), calls=%async_computation.2 | async-start | bytes 524288 | tf_op jit(solution)/shard_map/all_to_all | solution.py:283
  105.0 6.1 %collective-permute-start.2 = (bf16[8,16,128]{2,1,0:T(8,128)(2,1)}, bf16[8,16,128]{2,1,0:T(8,128)(2,1)S(1)}, u32[]{:S(2)}, u32[]{:S(2)}) collective-permute-start(bf16[8,16,128]{2,1,0:T(8,128)(2,1)} %get-tuple-element.18), channel_id=1, source_target_pairs={{0,8},{8,16},{16,24},{24,32},{32,40},{40,48},{48,56},{56,64},{64,7... | collective-permute-start | bytes 98312 | tf_op jit(solution)/shard_map/ppermute | solution.py:236
  109.2 5.7 %collective-permute-start.3 = (bf16[8,16,128]{2,1,0:T(8,128)(2,1)}, bf16[8,16,128]{2,1,0:T(8,128)(2,1)S(1)}, u32[]{:S(2)}, u32[]{:S(2)}) collective-permute-start(bf16[8,16,128]{2,1,0:T(8,128)(2,1)} %get-tuple-element.19), channel_id=1, source_target_pairs={{8,0},{16,8},{24,16},{32,24},{40,32},{48,40},{56,48},{64,56},{72,6... | collective-permute-start | bytes 98312 | tf_op jit(solution)/shard_map/ppermute | solution.py:236
  111.1 3.8 %copy-start.2 = (bf16[8,16,128]{2,1,0:T(8,128)(2,1)}, bf16[8,16,128]{2,1,0:T(8,128)(2,1)S(1)}, u32[]{:S(2)}) copy-start(bf16[8,16,128]{2,1,0:T(8,128)(2,1)S(1)} %collective-permute-done.2.lo_ref) | copy-start | bytes 98308
  114.9 0.6 copy-start.3
Sparse Core Ops, SparseCore 0:
  10.1 73.8 all-gather.4

commit v3 on v2

v3 whole, which is shorter than its diff:
```python
import jax
import jax.numpy as jnp
from jax import lax
from jax.experimental import pallas as pl
from jax.experimental.pallas import tpu as pltpu
from jax.sharding import Mesh
from jax.sharding import PartitionSpec as P

BF = jnp.bfloat16
F32 = jnp.float32
LEAVES = 16
ROWS = 16
PANEL = 128
RANK = 64
VECS = 256
COLS = 32
PACK = 4
GROUPS = LEAVES // PACK
NEAR_K = 9
FAR_K = 27
NWIN = 4
WIDE = LEAVES + 2 * NWIN
BAND = 2 * NWIN + 1
SHARES = 8
PLANE = 32
PAIRS = 14
CPL = PAIRS * 8 // ROWS
FULL = WIDE + CPL
HALF = FAR_K * 32
CLUS = ("x", "z", "core")
TOP = (((0,), (0,)), ((), ()))
ANY = pl.BlockSpec(memory_space=pl.ANY)
SMEM = pl.BlockSpec(memory_space=pltpu.SMEM)
VMEM = pl.BlockSpec(memory_space=pltpu.VMEM)


def dot(a, b):
    return jnp.dot(a, b, preferred_element_type=F32)


def dot_top(a, b):
    return lax.dot_general(a, b, TOP, preferred_element_type=F32)


def lane_group(shape):
    return lax.broadcasted_iota(jnp.int32, shape, len(shape) - 1) // COLS


def spread(rows):
    rows = rows + pltpu.roll(rows, 64, 1)
    return rows + pltpu.roll(rows, 32, 1)


def pack_parents(first, second):
    group = lane_group((32, 128))
    low = jnp.where(group == 0, first[:32], first[32:])
    high = jnp.where(group == 2, second[:32], second[32:])
    return jnp.where(group < 2, low, high)


def cut_parents(part, s):
    cut = slice(COLS * s, COLS * (s + 1))
    pieces = [part[0][:32, cut], part[0][32:, cut], part[1][:32, cut], part[1][32:, cut]]
    return jnp.concatenate(pieces, axis=1).astype(BF)


def prepare_kernel(d_ref, b_ref, t_ref, sent_ref, u_ref, ug_ref):
    u = [dot(b_ref[i], t_ref[i]).astype(BF) for i in range(LEAVES)]
    for g in range(GROUPS):
        ug_ref[g] = jnp.concatenate(u[PACK * g : PACK * (g + 1)], axis=1)
    part = []
    for p in range(2):
        rows = jnp.concatenate(u[8 * p : 8 * p + 8], axis=0)
        u_ref[p] = rows
        part.append(dot_top(rows, d_ref[8 * p : 8 * p + 8].reshape(8 * ROWS, VECS)))
    for s in range(SHARES):
        sent_ref[s] = cut_parents(part, s)


def stack_kernel(d_ref, lo_ref, hi_ref, c_ref, out_ref):
    out_ref[:NWIN] = lo_ref[...]
    out_ref[NWIN : NWIN + LEAVES] = d_ref[...]
    out_ref[NWIN + LEAVES : WIDE] = hi_ref[...]
    both = jnp.concatenate([c_ref[0].astype(F32), c_ref[1].astype(F32)], axis=2)
    rest = jnp.concatenate([both[PAIRS:], jnp.zeros((2 * PAIRS - FAR_K, 8, 128), F32)], axis=0)
    both = jnp.concatenate([both[:PAIRS], rest], axis=2)
    out_ref[WIDE:] = both.reshape(CPL, ROWS, VECS).astype(BF)


def parent_kernel(recv_ref, out_ref):
    total = jnp.sum(recv_ref[...].astype(F32), axis=0).astype(BF)
    out_ref[...] = jnp.broadcast_to(total[None], out_ref.shape)


def build_band(idx_ref, near_ref, s_scr):
    s_scr[...] = jnp.zeros_like(s_scr)
    for i in range(LEAVES):
        blocks = [near_ref[i, k].astype(F32) for k in range(NEAR_K)]
        for j in range(i, i + BAND):
            total = jnp.zeros((ROWS, PANEL), F32)
            for k in range(NEAR_K):
                total = total + jnp.where(idx_ref[i, k] == j, blocks[k], 0.0)
            s_scr[j, ROWS * i : ROWS * (i + 1)] = total.astype(BF)
    return jnp.concatenate([s_scr[j] for j in range(WIDE)], axis=1)


def near_kernel(
    idx_ref, near_ref, held_ref, u_ref, ug_ref, order_ref,
    keep_ref, wide_ref, lo_ref, hi_ref, sent_ref,
    s_scr, w_scr, sem,
):
    del order_ref
    copy = pltpu.make_async_copy(held_ref.at[:, pl.ds(0, WIDE)], w_scr, sem)
    copy.start()
    band = build_band(idx_ref, near_ref, s_scr)
    copy.wait()
    res = dot(band, jnp.concatenate([w_scr[:, j].reshape(PANEL, VECS) for j in range(WIDE)], axis=0))
    keep_ref[...] = res.reshape(LEAVES, ROWS, VECS)
    low = res.astype(BF)
    wide = low.reshape(LEAVES, ROWS, VECS)
    wide_ref[:LEAVES] = wide
    wide_ref[LEAVES:] = ug_ref[...]
    lo_ref[:NWIN] = wide[:NWIN]
    lo_ref[NWIN] = ug_ref[0]
    hi_ref[:NWIN] = wide[LEAVES - NWIN :]
    hi_ref[NWIN] = ug_ref[GROUPS - 1]
    part = [dot_top(u_ref[p], low[PANEL * p : PANEL * (p + 1)]) for p in range(2)]
    gram = jnp.concatenate([dot_top(u_ref[p], u_ref[p]) for p in range(2)], axis=1).astype(BF)
    for s in range(SHARES):
        sent_ref[s, :32] = cut_parents(part, s)
        sent_ref[s, 32:] = gram


def widen_kernel(own_ref, lo_ref, hi_ref, out_ref):
    out_ref[:NWIN] = lo_ref[:NWIN]
    out_ref[NWIN : NWIN + LEAVES] = own_ref[:LEAVES]
    out_ref[NWIN + LEAVES : WIDE] = hi_ref[:NWIN]
    out_ref[WIDE] = lo_ref[NWIN]
    out_ref[WIDE + 1 : WIDE + 1 + GROUPS] = own_ref[LEAVES:]
    out_ref[WIDE + 1 + GROUPS] = hi_ref[NWIN]


def second_kernel(idx_ref, near_ref, wide_ref, out_ref, q_ref, s_scr, w_scr, sem):
    copy = pltpu.make_async_copy(wide_ref, w_scr, sem)
    copy.start()
    band = build_band(idx_ref, near_ref, s_scr)
    copy.wait()
    out_ref[...] = dot(band, jnp.concatenate([w_scr[:, j].reshape(PANEL, VECS) for j in range(WIDE)], axis=0))
    parts = []
    for groups in ((0,), (1, 2), (3, 4), (5,)):
        rows = []
        for g in groups:
            u = w_scr[:, WIDE + g].reshape(PANEL, PACK * RANK)
            rows += [u[:, RANK * l : RANK * (l + 1)] for l in range(PACK)]
        cut = band[:, PANEL * PACK * groups[0] : PANEL * PACK * (groups[-1] + 1)]
        parts.append(dot(cut, jnp.concatenate(rows, axis=0)))
    q_ref[...] = jnp.concatenate(parts, axis=1).astype(BF)


def far_sums(far_ref, pc_ref, cpl, rhs_scr):
    side = lax.broadcasted_iota(jnp.int32, (32, 128), 1) // 64
    even = lane_group((RANK, 128)) % 2 == 0
    sums = []
    for p in range(2):
        for k in range(FAR_K):
            parent = far_ref[p, k]
            tile = pc_ref[(parent // 2) % 2, parent // 4]
            rhs_scr[32 * k : 32 * (k + 1), :] = jnp.where(side == parent % 2, tile, jnp.zeros_like(tile))
        rhs = rhs_scr[...]
        acc0 = dot(cpl[0][RANK * p : RANK * (p + 1)], rhs)
        acc1 = dot(cpl[1][RANK * p : RANK * (p + 1)], rhs)
        sums.append(spread(jnp.where(even, acc0, acc1)).astype(BF))
    return sums


def coupling_kernel(held_ref, cpl_ref, w_scr, c_scr, sem):
    copy = pltpu.make_async_copy(held_ref.at[:, pl.ds(WIDE, CPL)], w_scr, sem)
    copy.start()
    copy.wait()
    for y in range(SHARES):
        rows = w_scr[y].astype(F32).reshape(PAIRS, 8, VECS)
        c_scr[:PAIRS, 8 * y : 8 * y + 8, :] = rows[:, :, :128]
        c_scr[PAIRS:, 8 * y : 8 * y + 8, :] = rows[:, :, 128:]
    for h in range(2):
        part = c_scr[:FAR_K, 32 * h : 32 * (h + 1), :]
        cpl_ref[h] = part.reshape(HALF, 128).T.astype(BF)


def middle_kernel(far_ref, pc_ref, cpl_ref, recv_ref, out_ref, tile_ref, rhs_scr):
    coef = far_sums(far_ref, pc_ref, (cpl_ref[0], cpl_ref[1]), rhs_scr)
    tile_ref[...] = pack_parents(coef[0].astype(F32), coef[1].astype(F32)).astype(BF)
    total = jnp.sum(recv_ref[...].astype(F32), axis=0)
    gram = total[32:].astype(BF)
    own = [dot(gram[:, RANK * p : RANK * (p + 1)], coef[p]) for p in range(2)]
    packed = (total[:32] + pack_parents(own[0], own[1])).astype(BF)
    out_ref[...] = jnp.broadcast_to(packed[None], out_ref.shape)


def last_kernel(far_ref, pc_ref, cpl_ref, tile_ref, lo_ref, hi_ref, out_ref, rhs_scr):
    coef = far_sums(far_ref, pc_ref, (cpl_ref[0], cpl_ref[1]), rhs_scr)
    tile = pack_parents(coef[0].astype(F32), coef[1].astype(F32)).astype(BF)
    both = jnp.concatenate([lo_ref[...], tile_ref[...], hi_ref[...], tile], axis=0)
    out_ref[...] = jnp.broadcast_to(both[None], out_ref.shape)


def coefficients(c_ref, kind, p):
    halves = []
    for h in range(2):
        cut = slice(COLS * (2 * p + h), COLS * (2 * p + h + 1))
        pieces = [c_ref[s, 32 * kind : 32 * (kind + 1), cut] for s in range(SHARES)]
        halves.append(jnp.concatenate(pieces, axis=1))
    return jnp.concatenate(halves, axis=0)


def finish_kernel(keep_ref, u_ref, c_ref, near_ref, q_ref, first_ref, second_ref):
    below, above = coefficients(c_ref, 0, 1), coefficients(c_ref, 2, 0)
    own = [coefficients(c_ref, 1, p) for p in range(2)]
    new = [coefficients(c_ref, 3, p) for p in range(2)]
    res = near_ref[...] + dot(q_ref[...], jnp.concatenate([below] + own + [above], axis=0))
    for p in range(2):
        rows = slice(8 * p, 8 * (p + 1))
        far = dot(u_ref[p], own[p]).reshape(8, ROWS, VECS)
        first_ref[rows] = (keep_ref[rows] + far).astype(BF)
        far = dot(u_ref[p], new[p])
        second_ref[rows] = (res[PANEL * p : PANEL * (p + 1)] + far).reshape(8, ROWS, VECS).astype(BF)


def array(*shape, dtype=BF):
    return jax.ShapeDtypeStruct(shape, dtype)


def call(kernel, outs, ins, scratch, flops, nbytes, *operands):
    single = not isinstance(outs, tuple)
    return pl.pallas_call(
        kernel,
        out_shape=outs,
        in_specs=ins,
        out_specs=VMEM if single else (VMEM,) * len(outs),
        scratch_shapes=scratch,
        cost_estimate=pl.CostEstimate(flops=flops, bytes_accessed=nbytes, transcendentals=0),
    )(*operands)


def halo(bottom, top):
    count = 64
    forward = [(i, i + 1) for i in range(count - 1)]
    backward = [(target, source) for source, target in forward]
    return lax.ppermute(top, CLUS, forward), lax.ppermute(bottom, CLUS, backward)


def operator_twice(density, near_list, far_list, near_blocks, basis, transfer, coupling):
    rhs_scratch = pltpu.VMEM((HALF, 128), BF)
    tile = array(32, 128)
    plane_out = array(PLANE, 32, 128)
    cpl_out = array(2, 2 * RANK, HALF)

    low, high = halo(density[:NWIN], density[LEAVES - NWIN :])
    mine = call(
        stack_kernel, array(FULL, ROWS, VECS), [VMEM] * 4, [], 0, 600_000,
        density, low, high, jnp.swapaxes(coupling, 2, 3),
    )
    held = lax.all_gather(mine, "y", axis=0)
    sent, u, ug = call(
        prepare_kernel,
        (array(SHARES, 32, 128), array(2, PANEL, RANK), array(GROUPS, ROWS, PACK * RANK)),
        [VMEM] * 3, [], 40_000_000, 500_000,
        density, basis, transfer,
    )
    recv = lax.all_to_all(sent, "y", 0, 0)
    parents = call(parent_kernel, plane_out, [VMEM], [], 100_000, 300_000, recv)
    plane = lax.all_to_all(parents, ("x", "z"), 0, 0)

    near_idx = near_list - (lax.axis_index(CLUS) * LEAVES - NWIN)
    near_idx = jnp.clip(near_idx, 0, WIDE - 1)
    band_scratch = pltpu.VMEM((WIDE, LEAVES * ROWS, PANEL), BF)
    keep, wide, bottom, top, sent = call(
        near_kernel,
        (
            array(LEAVES, ROWS, VECS, dtype=F32),
            array(LEAVES + GROUPS, ROWS, VECS),
            array(NWIN + 1, ROWS, VECS),
            array(NWIN + 1, ROWS, VECS),
            array(SHARES, 96, 128),
        ),
        [SMEM, VMEM, ANY, VMEM, VMEM, ANY],
        [band_scratch, pltpu.VMEM((SHARES, WIDE, ROWS, VECS), BF), pltpu.SemaphoreType.DMA],
        420_000_000, 4_500_000,
        near_idx, near_blocks, held, u, ug, parents,
    )
    low, high = halo(bottom, top)
    wide = call(
        widen_kernel, array(WIDE + GROUPS + 2, ROWS, VECS), [VMEM] * 3, [], 0, 500_000,
        wide, low, high,
    )
    wide = lax.all_gather(wide, "y", axis=0)
    recv = lax.all_to_all(sent, "y", 0, 0)

    cpl = call(
        coupling_kernel, cpl_out, [ANY],
        [
            pltpu.VMEM((SHARES, CPL, ROWS, VECS), BF),
            pltpu.VMEM((2 * PAIRS, RANK, 128), F32),
            pltpu.SemaphoreType.DMA,
        ],
        0, 1_000_000, held,
    )
    every = lax.all_gather(plane, "core", axis=0)
    parents, own = call(
        middle_kernel, (plane_out, tile), [SMEM] + [VMEM] * 3, [rhs_scratch], 100_000_000, 1_400_000,
        far_list, every, cpl, recv,
    )
    plane = lax.all_to_all(parents, ("x", "z"), 0, 0)
    low, high = halo(own, own)
    every = lax.all_gather(plane, "core", axis=0)
    sent = call(
        last_kernel, array(SHARES, 128, 128), [SMEM] + [VMEM] * 5, [rhs_scratch], 100_000_000, 1_300_000,
        far_list, every, cpl, own, low, high,
    )
    coefs = lax.all_to_all(sent, "y", 0, 0)
    plain, q = call(
        second_kernel,
        (array(LEAVES * ROWS, VECS, dtype=F32), array(LEAVES * ROWS, 4 * RANK)),
        [SMEM, VMEM, ANY],
        [band_scratch, pltpu.VMEM((SHARES, WIDE + GROUPS + 2, ROWS, VECS), BF), pltpu.SemaphoreType.DMA],
        520_000_000, 4_000_000,
        near_idx, near_blocks, wide,
    )
    out = array(LEAVES, ROWS, VECS)
    return call(
        finish_kernel, (out, out), [VMEM] * 5, [], 100_000_000, 2_000_000,
        keep, u, coefs, plain, q,
    )


def solution(mesh):
    fine = Mesh(mesh.devices.reshape(4, 8, 2, 8), ("x", "z", "core", "y"))
    placed = (
        P(CLUS, "y", None),
        P(CLUS, None),
        P(CLUS, None),
        P(CLUS, None, "y", None),
        P(CLUS, "y", None),
        P(CLUS, None, None),
        P(CLUS, None, None, "y"),
    )
    return jax.shard_map(
        operator_twice,
        mesh=fine,
        in_specs=placed,
        out_specs=(P(CLUS, "y", None), P(CLUS, "y", None)),
        check_vma=False,
    )
```

time: 154 us -> 176 us (1.14)
  waiting for transfers between devices: 29.3 us -> 49.3 us
  starting transfers between devices: 37.7 us -> 48.8 us
  blocking collectives: 41.3 us -> 30.8 us
  local copies, waits for them, and re-layouts: 0.62 us -> 4.66 us
  Pallas kernels: 28.6 us -> 26 us
    all_to_all x2 -> x4, waiting for transfers between devices: 0.3 us -> 20.3 us  [the longest x2 10.5 us: operator_twice(): recv = lax.all_to_all(sent, 'y', 0, 0)]
    all_to_all x2 -> x1, blocking collectives: 32.8 us -> 20.2 us  [operator_twice(): plane = lax.all_to_all(parents, ('x', 'z'), 0, 0)]
    ppermute x2 -> x3, starting transfers between devices: 10.3 us -> 19.1 us  [halo(): lax.ppermute(top, CLUS, forward)]
    ppermute x2 -> x3, starting transfers between devices: 3.84 us -> 8.5 us  [halo(): lax.ppermute(bottom, CLUS, backward)]
    unnamed x8 -> x20, local copies, waits for them, and re-layouts: 0.62 us -> 3.88 us
    pallas_call x7 -> x10, Pallas kernels: 28.6 us -> 26 us  [call(): pl.pallas_call(kernel, out_shape=outs, in_specs=ins, out_specs=VMEM if si...]
    all_to_all x2 -> x4, starting transfers between devices: 23.6 us -> 21.1 us  [the longest x2 10.4 us: operator_twice(): recv = lax.all_to_all(sent, 'y', 0, 0)]
    all_gather x2, blocking collectives: 8.49 us -> 10.7 us  [operator_twice(): every = lax.all_gather(plane, 'core', axis=0)]
  transfers between devices with their start and end apart: 7 -> 12, of which waited for: 3 -> 7; matrix products, arithmetic and copies ran while one was open for 1% -> 1% of each run, Pallas kernels for 7% -> 9%
where the time goes in v3:
time: 176 us; the launch traced here: 175 us
  waiting for transfers between devices  49.3 us (28%)
  starting transfers between devices  48.8 us (28%)
  blocking collectives  30.8 us (18%)
  Pallas kernels  26 us (15%)
  between operations  14.2 us (8%)
  local copies, waits for them, and re-layouts  4.66 us (3%)
    pallas_call x10, Pallas kernels, call(): pl.pallas_call(kernel, out_shape=outs, in_specs=ins, out_specs=VMEM if si...  26 us
    all_gather x1, waiting for transfers between devices, operator_twice(): held = lax.all_gather(mine, 'y', axis=0)  24.5 us
    all_to_all x1, blocking collectives, operator_twice(): plane = lax.all_to_all(parents, ('x', 'z'), 0, 0)  20.2 us
    ppermute x3, starting transfers between devices, halo(): lax.ppermute(top, CLUS, forward)  19.1 us
    all_gather x2, blocking collectives, operator_twice(): every = lax.all_gather(plane, 'core', axis=0)  10.7 us
    all_to_all x2, waiting for transfers between devices, operator_twice(): recv = lax.all_to_all(sent, 'y', 0, 0)  10.5 us
    all_to_all x2, starting transfers between devices, operator_twice(): recv = lax.all_to_all(sent, 'y', 0, 0)  10.4 us
    ppermute x3, starting transfers between devices, halo(): lax.ppermute(bottom, CLUS, backward)  8.5 us
  transfers between devices with their start and end apart: 12, of which 7 were waited for; matrix products, arithmetic and copies ran while one was open for 1% of the time, Pallas kernels for 9%

profile of v3, /device:TPU:1, one launch (start us, length us, event | category | flops | bytes accessed | tf_op | source)
XLA Modules:
  0.0 175.1 jit_solution(15197050762756005049)
XLA Ops:
  8.0 5.4 %collective-permute-start = (bf16[4,16,256]{2,1,0:T(8,128)(2,1)S(1)}, bf16[4,16,256]{2,1,0:T(8,128)(2,1)S(1)}, u32[]{:S(2)}, u32[]{:S(2)}) collective-permute-start(bf16[4,16,256]{2,1,0:T(8,128)(2,1)S(1)} %get-tuple-element.27), channel_id=1, source_target_pairs={{0,8},{8,16},{16,24},{24,32},{32,40},{40,48},{48,56},{56,64},{64,7... | collective-permute-start | bytes 98312 | tf_op jit(solution)/shard_map/ppermute | solution.py:248
  13.4 4.7 %collective-permute-start.1 = (bf16[4,16,256]{2,1,0:T(8,128)(2,1)S(1)}, bf16[4,16,256]{2,1,0:T(8,128)(2,1)S(1)}, u32[]{:S(2)}, u32[]{:S(2)}) collective-permute-start(bf16[4,16,256]{2,1,0:T(8,128)(2,1)S(1)} %get-tuple-element.26), channel_id=1, source_target_pairs={{8,0},{16,8},{24,16},{32,24},{40,32},{48,40},{56,48},{64,56},{72,6... | collective-permute-start | bytes 98312 | tf_op jit(solution)/shard_map/ppermute | solution.py:248
  21.3 2.1 %shard_map.87 = (bf16[8,32,128]{2,1,0:T(8,128)(2,1)}, bf16[2,128,64]{2,1,0:T(8,128)(2,1)}, bf16[4,16,256]{2,1,0:T(8,128)(2,1)}) custom-call(bf16[16,16,256]{2,1,0:T(8,128)(2,1)} %d_ref.3, bf16[16,16,64]{2,1,0:T(8,128)(2,1)} %b_ref.1, bf16[16,64,64]{2,1,0:T(8,128)(2,1)} %t_ref.1), custom_call_target="tpu_custom_call" | custom-call | flops 40000000 | bytes 500000 | tf_op jit(solution)/shard_map/pallas_call | solution.py:234
  23.4 6.6 %all-to-all-start = ((bf16[8,32,128]{2,1,0:T(8,128)(2,1)}), bf16[8,32,128]{2,1,0:T(8,128)(2,1)S(1)}, u32[]{:S(2)}, u32[]{:S(2)}) async-start(bf16[8,32,128]{2,1,0:T(8,128)(2,1)} %get-tuple-element.16), calls=%async_computation | async-start | bytes 131072 | tf_op jit(solution)/shard_map/all_to_all | solution.py:269
  31.3 5.9 %all-to-all-done.recv_ref = bf16[8,32,128]{2,1,0:T(8,128)(2,1)S(1)} async-done(((bf16[8,32,128]{2,1,0:T(8,128)(2,1)}), bf16[8,32,128]{2,1,0:T(8,128)(2,1)S(1)}, u32[]{:S(2)}, u32[]{:S(2)}) %all-to-all-start) | async-done | bytes 65568 | tf_op jit(solution)/shard_map/all_to_all | solution.py:269
  39.4 24.5 %all-gather.7.cloned.1.call-done = bf16[248,16,256]{2,1,0:T(8,128)(2,1)} async-done(((bf16[31,16,256]{2,1,0:T(8,128)(2,1)}), bf16[248,16,256]{2,1,0:T(8,128)(2,1)}) %all-gather.7.cloned.1.call-update) | async-done | bytes 2031632 | tf_op jit(solution)/shard_map/all_gather | solution.py:262
  63.9 4.1 %shard_map.89 = (f32[16,16,256]{2,1,0:T(8,128)}, bf16[20,16,256]{2,1,0:T(8,128)(2,1)}, bf16[5,16,256]{2,1,0:T(8,128)(2,1)}, bf16[5,16,256]{2,1,0:T(8,128)(2,1)}, bf16[8,96,128]{2,1,0:T(8,128)(2,1)}) custom-call(s32[16,9]{1,0:T(8,128)} %subtract_clamp_fusion.idx_ref, bf16[16,9,16,128]{3,2,1,0:T(8,128)(2,1)} %near_ref.3, bf16[8,31,16,256]{3,2,1,0:T(8,128)(2,1)} %bitcast.5, ...), custom_call_target="tpu_custom_call" | custom-call | flops 420000000 | bytes 4500000 | tf_op jit(solution)/shard_map/pallas_call | solution.py:234
  68.0 8.1 %collective-permute-start.4 = (bf16[5,16,256]{2,1,0:T(8,128)(2,1)}, bf16[5,16,256]{2,1,0:T(8,128)(2,1)S(1)}, u32[]{:S(2)}, u32[]{:S(2)}) collective-permute-start(bf16[5,16,256]{2,1,0:T(8,128)(2,1)} %get-tuple-element.22), channel_id=1, source_target_pairs={{0,8},{8,16},{16,24},{24,32},{32,40},{40,48},{48,56},{56,64},{64,7... | collective-permute-start | bytes 122888 | tf_op jit(solution)/shard_map/ppermute | solution.py:248
  78.1 3.6 %collective-permute-done.5.hi_ref = bf16[5,16,256]{2,1,0:T(8,128)(2,1)S(1)} collective-permute-done((bf16[5,16,256]{2,1,0:T(8,128)(2,1)}, bf16[5,16,256]{2,1,0:T(8,128)(2,1)S(1)}, u32[]{:S(2)}, u32[]{:S(2)}) %collective-permute-start.5) | collective-permute-done | bytes 40992 | tf_op jit(solution)/shard_map/ppermute | solution.py:248
  84.0 20.2 %all_to_all.25 = bf16[32,32,128]{2,1,0:T(8,128)(2,1)S(1)} all-to-all(bf16[32,32,128]{2,1,0:T(8,128)(2,1)S(1)} %copy-done), channel_id=1, replica_groups=mesh['x'=4,'z'=8,'core'=2,'y'=8] {'x','z'}, dimensions={0} | all-to-all | bytes 524288 | tf_op jit(solution)/shard_map/all_to_all | solution.py:271
  104.1 3.9 %all-to-all-start.2 = ((bf16[8,96,128]{2,1,0:T(8,128)(2,1)}), bf16[8,96,128]{2,1,0:T(8,128)(2,1)S(1)}, u32[]{:S(2)}, u32[]{:S(2)}) async-start(bf16[8,96,128]{2,1,0:T(8,128)(2,1)} %get-tuple-element.18), calls=%async_computation.2 | async-start | bytes 393216 | tf_op jit(solution)/shard_map/all_to_all | solution.py:296
  108.0 4.5 %all-gather.1 = bf16[64,32,128]{2,1,0:T(8,128)(2,1)} all-gather(bf16[32,32,128]{2,1,0:T(8,128)(2,1)S(1)} %all_to_all.25), channel_id=3, replica_groups=mesh['x'=4,'z'=8,'core'=2,'y'=8] {'core'}, dimensions={0}, use_global_device_ids=true | all-gather | bytes 786432 | tf_op jit(solution)/shard_map/all_gather | solution.py:307
  112.5 2.0 %shard_map.90.cpl_ref = bf16[2,128,864]{2,1,0:T(8,128)(2,1)} custom-call(bf16[8,31,16,256]{3,2,1,0:T(8,128)(2,1)} %bitcast.6), custom_call_target="tpu_custom_call" | custom-call | bytes 1000000 | tf_op jit(solution)/shard_map/pallas_call | solution.py:234
  114.5 4.6 %all-to-all-done.2.recv_ref = bf16[8,96,128]{2,1,0:T(8,128)(2,1)S(1)} async-done(((bf16[8,96,128]{2,1,0:T(8,128)(2,1)}), bf16[8,96,128]{2,1,0:T(8,128)(2,1)S(1)}, u32[]{:S(2)}, u32[]{:S(2)}) %all-to-all-start.2) | async-done | bytes 196640 | tf_op jit(solution)/shard_map/all_to_all | solution.py:296
  119.8 3.1 %shard_map.91 = (bf16[32,32,128]{2,1,0:T(8,128)(2,1)}, bf16[32,128]{1,0:T(8,128)(2,1)}) custom-call(s32[2,27]{1,0:T(2,128)} %far_ref.3, bf16[2,32,32,128]{3,2,1,0:T(8,128)(2,1)} %bitcast.7, bf16[2,128,864]{2,1,0:T(8,128)(2,1)} %shard_map.90.cpl_ref, bf16[8,96,128]{2,1,0:T(8,128)(2,1)} %copy-done.2), custom_call_target="tpu_custom_call" | custom-call | flops 100000000 | bytes 1400000 | tf_op jit(solution)/shard_map/pallas_call | solution.py:234
  122.9 7.3 %all-to-all-start.3 = ((bf16[32,32,128]{2,1,0:T(8,128)(2,1)}), bf16[32,32,128]{2,1,0:T(8,128)(2,1)S(1)}, u32[]{:S(2)}, u32[]{:S(2)}) async-start(bf16[32,32,128]{2,1,0:T(8,128)(2,1)} %get-tuple-element.19), calls=%async_computation.3 | async-start | bytes 524288 | tf_op jit(solution)/shard_map/all_to_all | solution.py:312
  130.2 5.6 %collective-permute-start.2 = (bf16[32,128]{1,0:T(8,128)(2,1)}, bf16[32,128]{1,0:T(8,128)(2,1)S(1)}, u32[]{:S(2)}, u32[]{:S(2)}) collective-permute-start(bf16[32,128]{1,0:T(8,128)(2,1)} %get-tuple-element.20.tile_ref), channel_id=1, source_target_pairs={{0,8},{8,16},{16,24},{24,32},{32,40},{40,48},{48,56},{56,64},{64,7... | collective-permute-start | bytes 24584 | tf_op jit(solution)/shard_map/ppermute | solution.py:248
  137.8 2.1 %all-to-all-done.3 = bf16[32,32,128]{2,1,0:T(8,128)(2,1)S(1)} async-done(((bf16[32,32,128]{2,1,0:T(8,128)(2,1)}), bf16[32,32,128]{2,1,0:T(8,128)(2,1)S(1)}, u32[]{:S(2)}, u32[]{:S(2)}) %all-to-all-start.3) | async-done | bytes 262176 | tf_op jit(solution)/shard_map/all_to_all | solution.py:312
  139.9 6.2 %all-gather.2 = bf16[64,32,128]{2,1,0:T(8,128)(2,1)} all-gather(bf16[32,32,128]{2,1,0:T(8,128)(2,1)S(1)} %all-to-all-done.3), channel_id=4, replica_groups=mesh['x'=4,'z'=8,'core'=2,'y'=8] {'core'}, dimensions={0}, use_global_device_ids=true | all-gather | bytes 786432 | tf_op jit(solution)/shard_map/all_gather | solution.py:314
  146.7 3.0 %shard_map.92 = bf16[8,128,128]{2,1,0:T(8,128)(2,1)} custom-call(s32[2,27]{1,0:T(2,128)} %far_ref.3, bf16[2,32,32,128]{3,2,1,0:T(8,128)(2,1)} %bitcast.8, bf16[2,128,864]{2,1,0:T(8,128)(2,1)} %shard_map.90.cpl_ref, bf16[32,128]{1,0:T(8,128)(2,1)} %get-tuple-element.20.tile_ref, bf16[32,128]{1,0:T(8,128)(2,1)} %copy-done.8, bf16[32,128]{1,0:T(8,128)(2,1)} %copy-done.9), custom_call_target="tpu_custom_call" | custom-call | flops 100000000 | bytes 1300000 | tf_op jit(solution)/shard_map/pallas_call | solution.py:234
  149.6 3.4 %all-to-all-start.4 = ((bf16[8,128,128]{2,1,0:T(8,128)(2,1)}), bf16[8,128,128]{2,1,0:T(8,128)(2,1)S(1)}, u32[]{:S(2)}, u32[]{:S(2)}) async-start(bf16[8,128,128]{2,1,0:T(8,128)(2,1)} %shard_map.92), calls=%async_computation.4 | async-start | bytes 524288 | tf_op jit(solution)/shard_map/all_to_all | solution.py:319
  153.1 4.4 %shard_map.94 = (f32[256,256]{1,0:T(8,128)}, bf16[256,256]{1,0:T(8,128)(2,1)}) custom-call(s32[16,9]{1,0:T(8,128)} %subtract_clamp_fusion.idx_ref, bf16[16,9,16,128]{3,2,1,0:T(8,128)(2,1)} %near_ref.3, bf16[8,30,16,256]{3,2,1,0:T(8,128)(2,1)} %bitcast.9), custom_call_target="tpu_custom_call" | custom-call | flops 520000000 | bytes 4000000 | tf_op jit(solution)/shard_map/pallas_call | solution.py:234
  157.5 7.8 %all-to-all-done.4.c_ref = bf16[8,128,128]{2,1,0:T(8,128)(2,1)S(1)} async-done(((bf16[8,128,128]{2,1,0:T(8,128)(2,1)}), bf16[8,128,128]{2,1,0:T(8,128)(2,1)S(1)}, u32[]{:S(2)}, u32[]{:S(2)}) %all-to-all-start.4) | async-done | bytes 262176 | tf_op jit(solution)/shard_map/all_to_all | solution.py:319
  166.0 2.3 %shard_map.95 = (bf16[16,16,256]{2,1,0:T(8,128)(2,1)}, bf16[16,16,256]{2,1,0:T(8,128)(2,1)}) custom-call(f32[16,16,256]{2,1,0:T(8,128)} %get-tuple-element.17.keep_ref, bf16[2,128,64]{2,1,0:T(8,128)(2,1)} %get-tuple-element.14.u_ref, bf16[8,128,128]{2,1,0:T(8,128)(2,1)} %copy-done.1, f32[256,256]{1,0:T(8,128)} %get-tuple-element.24.near_ref, ...), custom_call_target="tpu_custom_call" | custom-call | flops 100000000 | bytes 2000000 | tf_op jit(solution)/shard_map/pallas_call | solution.py:234
  (37 shorter events, 15.8 us)
Async XLA Ops:
  7.2 56.7 %all-gather.7.cloned.1.call-start = ((), (), s32[]{:S(2)}) async-start(), calls=%async_computation.5 | async-start | bytes 2285568 | tf_op jit(solution)/shard_map/all_gather | solution.py:262
  8.0 10.0 %collective-permute-start = (bf16[4,16,256]{2,1,0:T(8,128)(2,1)S(1)}, bf16[4,16,256]{2,1,0:T(8,128)(2,1)S(1)}, u32[]{:S(2)}, u32[]{:S(2)}) collective-permute-start(bf16[4,16,256]{2,1,0:T(8,128)(2,1)S(1)} %get-tuple-element.27), channel_id=1, source_target_pairs={{0,8},{8,16},{16,24},{24,32},{32,40},{40,48},{48,56},{56,64},{64,7... | collective-permute-start | bytes 98312 | tf_op jit(solution)/shard_map/ppermute | solution.py:248
  13.4 5.5 %collective-permute-start.1 = (bf16[4,16,256]{2,1,0:T(8,128)(2,1)S(1)}, bf16[4,16,256]{2,1,0:T(8,128)(2,1)S(1)}, u32[]{:S(2)}, u32[]{:S(2)}) collective-permute-start(bf16[4,16,256]{2,1,0:T(8,128)(2,1)S(1)} %get-tuple-element.26), channel_id=1, source_target_pairs={{8,0},{16,8},{24,16},{32,24},{40,32},{48,40},{56,48},{64,56},{72,6... | collective-permute-start | bytes 98312 | tf_op jit(solution)/shard_map/ppermute | solution.py:248
  18.0 0.8 copy-start.6
  18.9 0.6 copy-start.7
  23.4 13.8 %all-to-all-start = ((bf16[8,32,128]{2,1,0:T(8,128)(2,1)}), bf16[8,32,128]{2,1,0:T(8,128)(2,1)S(1)}, u32[]{:S(2)}, u32[]{:S(2)}) async-start(bf16[8,32,128]{2,1,0:T(8,128)(2,1)} %get-tuple-element.16), calls=%async_computation | async-start | bytes 131072 | tf_op jit(solution)/shard_map/all_to_all | solution.py:269
  30.0 123.1 %all-gather.9.cloned.1.call-start = ((), (), s32[]{:S(2)}) async-start(), calls=%async_computation.6 | async-start | bytes 2211840 | tf_op jit(solution)/shard_map/all_gather | solution.py:295
  37.2 0.6 copy-start.3
  39.4 44.5 %copy-start = (bf16[32,32,128]{2,1,0:T(8,128)(2,1)S(1)}, bf16[32,32,128]{2,1,0:T(8,128)(2,1)}, u32[]{:S(2)}) copy-start(bf16[32,32,128]{2,1,0:T(8,128)(2,1)} %shard_map.88.order_ref) | copy-start | bytes 786436
  68.0 10.0 %collective-permute-start.4 = (bf16[5,16,256]{2,1,0:T(8,128)(2,1)}, bf16[5,16,256]{2,1,0:T(8,128)(2,1)S(1)}, u32[]{:S(2)}, u32[]{:S(2)}) collective-permute-start(bf16[5,16,256]{2,1,0:T(8,128)(2,1)} %get-tuple-element.22), channel_id=1, source_target_pairs={{0,8},{8,16},{16,24},{24,32},{32,40},{40,48},{48,56},{56,64},{64,7... | collective-permute-start | bytes 122888 | tf_op jit(solution)/shard_map/ppermute | solution.py:248
  76.1 5.5 %collective-permute-start.5 = (bf16[5,16,256]{2,1,0:T(8,128)(2,1)}, bf16[5,16,256]{2,1,0:T(8,128)(2,1)S(1)}, u32[]{:S(2)}, u32[]{:S(2)}) collective-permute-start(bf16[5,16,256]{2,1,0:T(8,128)(2,1)} %get-tuple-element.23), channel_id=1, source_target_pairs={{8,0},{16,8},{24,16},{32,24},{40,32},{48,40},{56,48},{64,56},{72,6... | collective-permute-start | bytes 122888 | tf_op jit(solution)/shard_map/ppermute | solution.py:248
  78.1 3.6 %copy-start.4 = (bf16[5,16,256]{2,1,0:T(8,128)(2,1)}, bf16[5,16,256]{2,1,0:T(8,128)(2,1)S(1)}, u32[]{:S(2)}) copy-start(bf16[5,16,256]{2,1,0:T(8,128)(2,1)S(1)} %collective-permute-done.4.lo_ref) | copy-start | bytes 122884
  81.6 0.6 copy-start.5
  104.1 15.0 %all-to-all-start.2 = ((bf16[8,96,128]{2,1,0:T(8,128)(2,1)}), bf16[8,96,128]{2,1,0:T(8,128)(2,1)S(1)}, u32[]{:S(2)}, u32[]{:S(2)}) async-start(bf16[8,96,128]{2,1,0:T(8,128)(2,1)} %get-tuple-element.18), calls=%async_computation.2 | async-start | bytes 393216 | tf_op jit(solution)/shard_map/all_to_all | solution.py:296
  119.1 0.7 copy-start.2
  122.9 17.0 %all-to-all-start.3 = ((bf16[32,32,128]{2,1,0:T(8,128)(2,1)}), bf16[32,32,128]{2,1,0:T(8,128)(2,1)S(1)}, u32[]{:S(2)}, u32[]{:S(2)}) async-start(bf16[32,32,128]{2,1,0:T(8,128)(2,1)} %get-tuple-element.19), calls=%async_computation.3 | async-start | bytes 524288 | tf_op jit(solution)/shard_map/all_to_all | solution.py:312
  130.2 15.8 %collective-permute-start.2 = (bf16[32,128]{1,0:T(8,128)(2,1)}, bf16[32,128]{1,0:T(8,128)(2,1)S(1)}, u32[]{:S(2)}, u32[]{:S(2)}) collective-permute-start(bf16[32,128]{1,0:T(8,128)(2,1)} %get-tuple-element.20.tile_ref), channel_id=1, source_target_pairs={{0,8},{8,16},{16,24},{24,32},{32,40},{40,48},{48,56},{56,64},{64,7... | collective-permute-start | bytes 24584 | tf_op jit(solution)/shard_map/ppermute | solution.py:248
  135.9 10.2 %collective-permute-start.3 = (bf16[32,128]{1,0:T(8,128)(2,1)}, bf16[32,128]{1,0:T(8,128)(2,1)S(1)}, u32[]{:S(2)}, u32[]{:S(2)}) collective-permute-start(bf16[32,128]{1,0:T(8,128)(2,1)} %get-tuple-element.20.tile_ref), channel_id=1, source_target_pairs={{8,0},{16,8},{24,16},{32,24},{40,32},{48,40},{56,48},{64,56},{72,6... | collective-permute-start | bytes 24584 | tf_op jit(solution)/shard_map/ppermute | solution.py:248
  146.1 0.6 copy-start.8
  146.1 0.6 copy-start.9
  149.6 15.7 %all-to-all-start.4 = ((bf16[8,128,128]{2,1,0:T(8,128)(2,1)}), bf16[8,128,128]{2,1,0:T(8,128)(2,1)S(1)}, u32[]{:S(2)}, u32[]{:S(2)}) async-start(bf16[8,128,128]{2,1,0:T(8,128)(2,1)} %shard_map.92), calls=%async_computation.4 | async-start | bytes 524288 | tf_op jit(solution)/shard_map/all_to_all | solution.py:319
  165.3 0.7 copy-start.1
Sparse Core Ops, SparseCore 0:
  21.4 42.4 all-gather.6
  84.1 40.3 all-gather.8

commit v4 on v3

--- a/solution.py
+++ b/solution.py
@@ -25,7 +25,7 @@
 PLANE = 32
 PAIRS = 14
 CPL = PAIRS * 8 // ROWS
-FULL = WIDE + CPL
+FULL = 16
 HALF = FAR_K * 32
 CLUS = ("x", "z", "core")
 TOP = (((0,), (0,)), ((), ()))
@@ -64,66 +64,74 @@
     return jnp.concatenate(pieces, axis=1).astype(BF)
 
 
-def prepare_kernel(d_ref, b_ref, t_ref, sent_ref, u_ref, ug_ref):
+def prepare_kernel(d_ref, b_ref, t_ref, c_ref, sent_ref, u_ref, uc_ref):
     u = [dot(b_ref[i], t_ref[i]).astype(BF) for i in range(LEAVES)]
-    for g in range(GROUPS):
-        ug_ref[g] = jnp.concatenate(u[PACK * g : PACK * (g + 1)], axis=1)
     part = []
     for p in range(2):
         rows = jnp.concatenate(u[8 * p : 8 * p + 8], axis=0)
         u_ref[p] = rows
         part.append(dot_top(rows, d_ref[8 * p : 8 * p + 8].reshape(8 * ROWS, VECS)))
     for s in range(SHARES):
-        sent_ref[s] = cut_parents(part, s)
-
-
-def stack_kernel(d_ref, lo_ref, hi_ref, c_ref, out_ref):
-    out_ref[:NWIN] = lo_ref[...]
-    out_ref[NWIN : NWIN + LEAVES] = d_ref[...]
-    out_ref[NWIN + LEAVES : WIDE] = hi_ref[...]
+        tile = cut_parents(part, s)
+        sent_ref[s, :LEAVES] = d_ref[...]
+        sent_ref[s, LEAVES] = jnp.concatenate([tile[:ROWS], tile[ROWS:]], axis=1)
+    for g in range(GROUPS):
+        uc_ref[g] = jnp.concatenate(u[PACK * g : PACK * (g + 1)], axis=1)
     both = jnp.concatenate([c_ref[0].astype(F32), c_ref[1].astype(F32)], axis=2)
     rest = jnp.concatenate([both[PAIRS:], jnp.zeros((2 * PAIRS - FAR_K, 8, 128), F32)], axis=0)
-    both = jnp.concatenate([both[:PAIRS], rest], axis=2)
-    out_ref[WIDE:] = both.reshape(CPL, ROWS, VECS).astype(BF)
-
-
-def parent_kernel(recv_ref, out_ref):
-    total = jnp.sum(recv_ref[...].astype(F32), axis=0).astype(BF)
+    both = jnp.concatenate([both[:PAIRS], rest], axis=2).reshape(CPL, ROWS, VECS).astype(BF)
+    uc_ref[GROUPS : GROUPS + CPL] = both
+    uc_ref[GROUPS + CPL :] = jnp.zeros((FULL - GROUPS - CPL, ROWS, VECS), BF)
+
+
+def parent_kernel(recv_ref, out_ref, scr, sem):
+    move = pltpu.make_async_copy(recv_ref.at[:, LEAVES], scr, sem)
+    move.start()
+    move.wait()
+    total = jnp.sum(scr[...].astype(F32), axis=0).astype(BF)
+    total = jnp.concatenate([total[:, :128], total[:, 128:]], axis=0)
     out_ref[...] = jnp.broadcast_to(total[None], out_ref.shape)
 
 
 def build_band(idx_ref, near_ref, s_scr):
+    offset = lax.axis_index(CLUS) * LEAVES - NWIN
     s_scr[...] = jnp.zeros_like(s_scr)
     for i in range(LEAVES):
         blocks = [near_ref[i, k].astype(F32) for k in range(NEAR_K)]
         for j in range(i, i + BAND):
             total = jnp.zeros((ROWS, PANEL), F32)
             for k in range(NEAR_K):
-                total = total + jnp.where(idx_ref[i, k] == j, blocks[k], 0.0)
+                total = total + jnp.where(idx_ref[i, k] == j + offset, blocks[k], 0.0)
             s_scr[j, ROWS * i : ROWS * (i + 1)] = total.astype(BF)
     return jnp.concatenate([s_scr[j] for j in range(WIDE)], axis=1)
 
 
+def fetch(pairs, sems):
+    moves = [pltpu.make_async_copy(src, dst, sems.at[n]) for n, (src, dst) in enumerate(pairs)]
+    for move in moves:
+        move.start()
+    return moves
+
+
+def leaf_rows(w_scr):
+    return jnp.concatenate([w_scr[:, j].reshape(PANEL, VECS) for j in range(WIDE)], axis=0)
+
+
 def near_kernel(
-    idx_ref, near_ref, held_ref, u_ref, ug_ref, order_ref,
-    keep_ref, wide_ref, lo_ref, hi_ref, sent_ref,
-    s_scr, w_scr, sem,
+    idx_ref, near_ref, lo_ref, own_ref, hi_ref, u_ref,
+    keep_ref, low_ref, sent_ref,
+    s_scr, w_scr, sems,
 ):
-    del order_ref
-    copy = pltpu.make_async_copy(held_ref.at[:, pl.ds(0, WIDE)], w_scr, sem)
-    copy.start()
+    top = NWIN + LEAVES
+    pairs = ((lo_ref, w_scr.at[:, :NWIN]), (own_ref.at[:, :LEAVES], w_scr.at[:, NWIN:top]), (hi_ref, w_scr.at[:, top:]))
+    moves = fetch(pairs, sems)
     band = build_band(idx_ref, near_ref, s_scr)
-    copy.wait()
-    res = dot(band, jnp.concatenate([w_scr[:, j].reshape(PANEL, VECS) for j in range(WIDE)], axis=0))
+    for move in moves:
+        move.wait()
+    res = dot(band, leaf_rows(w_scr))
     keep_ref[...] = res.reshape(LEAVES, ROWS, VECS)
     low = res.astype(BF)
-    wide = low.reshape(LEAVES, ROWS, VECS)
-    wide_ref[:LEAVES] = wide
-    wide_ref[LEAVES:] = ug_ref[...]
-    lo_ref[:NWIN] = wide[:NWIN]
-    lo_ref[NWIN] = ug_ref[0]
-    hi_ref[:NWIN] = wide[LEAVES - NWIN :]
-    hi_ref[NWIN] = ug_ref[GROUPS - 1]
+    low_ref[...] = low.reshape(LEAVES, ROWS, VECS)
     part = [dot_top(u_ref[p], low[PANEL * p : PANEL * (p + 1)]) for p in range(2)]
     gram = jnp.concatenate([dot_top(u_ref[p], u_ref[p]) for p in range(2)], axis=1).astype(BF)
     for s in range(SHARES):
@@ -131,21 +139,24 @@
         sent_ref[s, 32:] = gram
 
 
-def widen_kernel(own_ref, lo_ref, hi_ref, out_ref):
-    out_ref[:NWIN] = lo_ref[:NWIN]
-    out_ref[NWIN : NWIN + LEAVES] = own_ref[:LEAVES]
-    out_ref[NWIN + LEAVES : WIDE] = hi_ref[:NWIN]
-    out_ref[WIDE] = lo_ref[NWIN]
-    out_ref[WIDE + 1 : WIDE + 1 + GROUPS] = own_ref[LEAVES:]
-    out_ref[WIDE + 1 + GROUPS] = hi_ref[NWIN]
-
-
-def second_kernel(idx_ref, near_ref, wide_ref, out_ref, q_ref, s_scr, w_scr, sem):
-    copy = pltpu.make_async_copy(wide_ref, w_scr, sem)
-    copy.start()
+def second_kernel(
+    idx_ref, near_ref, lo_ref, own_ref, hi_ref, ulo_ref, uc_ref, uhi_ref,
+    out_ref, q_ref, s_scr, w_scr, sems,
+):
+    top = NWIN + LEAVES
+    pairs = (
+        (lo_ref, w_scr.at[:, :NWIN]),
+        (own_ref, w_scr.at[:, NWIN:top]),
+        (hi_ref, w_scr.at[:, top:WIDE]),
+        (ulo_ref.at[:SHARES], w_scr.at[:, WIDE]),
+        (uc_ref.at[:, :GROUPS], w_scr.at[:, WIDE + 1 : WIDE + 1 + GROUPS]),
+        (uhi_ref.at[:SHARES], w_scr.at[:, WIDE + 1 + GROUPS]),
+    )
+    moves = fetch(pairs, sems)
     band = build_band(idx_ref, near_ref, s_scr)
-    copy.wait()
-    out_ref[...] = dot(band, jnp.concatenate([w_scr[:, j].reshape(PANEL, VECS) for j in range(WIDE)], axis=0))
+    for move in moves:
+        move.wait()
+    out_ref[...] = dot(band, leaf_rows(w_scr))
     parts = []
     for groups in ((0,), (1, 2), (3, 4), (5,)):
         rows = []
@@ -174,7 +185,7 @@
 
 
 def coupling_kernel(held_ref, cpl_ref, w_scr, c_scr, sem):
-    copy = pltpu.make_async_copy(held_ref.at[:, pl.ds(WIDE, CPL)], w_scr, sem)
+    copy = pltpu.make_async_copy(held_ref.at[:, pl.ds(GROUPS, CPL)], w_scr, sem)
     copy.start()
     copy.wait()
     for y in range(SHARES):
@@ -186,9 +197,25 @@
         cpl_ref[h] = part.reshape(HALF, 128).T.astype(BF)
 
 
-def middle_kernel(far_ref, pc_ref, cpl_ref, recv_ref, out_ref, tile_ref, rhs_scr):
+def fold(tile):
+    return jnp.concatenate([tile[:ROWS], tile[ROWS:]], axis=1)
+
+
+def unfold(slab):
+    return jnp.concatenate([slab[:, :128], slab[:, 128:]], axis=0)
+
+
+def middle_kernel(
+    far_ref, pc_ref, cpl_ref, recv_ref, held_ref, out_ref, bottom_ref, top_ref, rhs_scr, u_scr, sems
+):
+    pairs = ((held_ref.at[:, 0], u_scr.at[0]), (held_ref.at[:, GROUPS - 1], u_scr.at[1]))
+    moves = fetch(pairs, sems)
     coef = far_sums(far_ref, pc_ref, (cpl_ref[0], cpl_ref[1]), rhs_scr)
-    tile_ref[...] = pack_parents(coef[0].astype(F32), coef[1].astype(F32)).astype(BF)
+    slab = fold(pack_parents(coef[0].astype(F32), coef[1].astype(F32)).astype(BF))
+    for n, ref in enumerate((bottom_ref, top_ref)):
+        moves[n].wait()
+        ref[:SHARES] = u_scr[n]
+        ref[SHARES] = slab
     total = jnp.sum(recv_ref[...].astype(F32), axis=0)
     gram = total[32:].astype(BF)
     own = [dot(gram[:, RANK * p : RANK * (p + 1)], coef[p]) for p in range(2)]
@@ -196,10 +223,11 @@
     out_ref[...] = jnp.broadcast_to(packed[None], out_ref.shape)
 
 
-def last_kernel(far_ref, pc_ref, cpl_ref, tile_ref, lo_ref, hi_ref, out_ref, rhs_scr):
+def last_kernel(far_ref, pc_ref, cpl_ref, own_ref, lo_ref, hi_ref, out_ref, rhs_scr):
     coef = far_sums(far_ref, pc_ref, (cpl_ref[0], cpl_ref[1]), rhs_scr)
     tile = pack_parents(coef[0].astype(F32), coef[1].astype(F32)).astype(BF)
-    both = jnp.concatenate([lo_ref[...], tile_ref[...], hi_ref[...], tile], axis=0)
+    both = [unfold(ref[SHARES]) for ref in (lo_ref, own_ref, hi_ref)] + [tile]
+    both = jnp.concatenate(both, axis=0)
     out_ref[...] = jnp.broadcast_to(both[None], out_ref.shape)
 
 
@@ -248,52 +276,49 @@
     return lax.ppermute(top, CLUS, forward), lax.ppermute(bottom, CLUS, backward)
 
 
+def exchange(values, axis):
+    return lax.all_to_all(values, axis, 0, 0)
+
+
 def operator_twice(density, near_list, far_list, near_blocks, basis, transfer, coupling):
     rhs_scratch = pltpu.VMEM((HALF, 128), BF)
-    tile = array(32, 128)
+    band_scratch = pltpu.VMEM((WIDE, LEAVES * ROWS, PANEL), BF)
     plane_out = array(PLANE, 32, 128)
     cpl_out = array(2, 2 * RANK, HALF)
-
-    low, high = halo(density[:NWIN], density[LEAVES - NWIN :])
-    mine = call(
-        stack_kernel, array(FULL, ROWS, VECS), [VMEM] * 4, [], 0, 600_000,
-        density, low, high, jnp.swapaxes(coupling, 2, 3),
-    )
-    held = lax.all_gather(mine, "y", axis=0)
-    sent, u, ug = call(
+    sent, u, uc = call(
         prepare_kernel,
-        (array(SHARES, 32, 128), array(2, PANEL, RANK), array(GROUPS, ROWS, PACK * RANK)),
-        [VMEM] * 3, [], 40_000_000, 500_000,
-        density, basis, transfer,
-    )
-    recv = lax.all_to_all(sent, "y", 0, 0)
-    parents = call(parent_kernel, plane_out, [VMEM], [], 100_000, 300_000, recv)
-    plane = lax.all_to_all(parents, ("x", "z"), 0, 0)
-
-    near_idx = near_list - (lax.axis_index(CLUS) * LEAVES - NWIN)
-    near_idx = jnp.clip(near_idx, 0, WIDE - 1)
-    band_scratch = pltpu.VMEM((WIDE, LEAVES * ROWS, PANEL), BF)
-    keep, wide, bottom, top, sent = call(
+        (
+            array(SHARES, LEAVES + 1, ROWS, VECS),
+            array(2, PANEL, RANK),
+            array(FULL, ROWS, VECS),
+        ),
+        [VMEM] * 4, [], 40_000_000, 1_700_000,
+        density, basis, transfer, jnp.swapaxes(coupling, 2, 3),
+    )
+    held = lax.all_gather(uc, "y", axis=0)
+    whole = exchange(sent, "y")
+    parents = call(
+        parent_kernel, plane_out, [ANY],
+        [pltpu.VMEM((SHARES, ROWS, VECS), BF), pltpu.SemaphoreType.DMA], 100_000, 300_000,
+        whole,
+    )
+    plane = exchange(parents, ("x", "z"))
+
+    low, high = halo(whole[:, :NWIN], whole[:, LEAVES - NWIN : LEAVES])
+    keep, wide, sent = call(
         near_kernel,
         (
             array(LEAVES, ROWS, VECS, dtype=F32),
-            array(LEAVES + GROUPS, ROWS, VECS),
-            array(NWIN + 1, ROWS, VECS),
-            array(NWIN + 1, ROWS, VECS),
+            array(LEAVES, ROWS, VECS),
             array(SHARES, 96, 128),
         ),
-        [SMEM, VMEM, ANY, VMEM, VMEM, ANY],
-        [band_scratch, pltpu.VMEM((SHARES, WIDE, ROWS, VECS), BF), pltpu.SemaphoreType.DMA],
+        [SMEM, VMEM, ANY, ANY, ANY, VMEM],
+        [band_scratch, pltpu.VMEM((SHARES, WIDE, ROWS, VECS), BF), pltpu.SemaphoreType.DMA((3,))],
         420_000_000, 4_500_000,
-        near_idx, near_blocks, held, u, ug, parents,
-    )
-    low, high = halo(bottom, top)
-    wide = call(
-        widen_kernel, array(WIDE + GROUPS + 2, ROWS, VECS), [VMEM] * 3, [], 0, 500_000,
-        wide, low, high,
+        near_list, near_blocks, low, whole, high, u,
     )
     wide = lax.all_gather(wide, "y", axis=0)
-    recv = lax.all_to_all(sent, "y", 0, 0)
+    recv = exchange(sent, "y")
 
     cpl = call(
         coupling_kernel, cpl_out, [ANY],
@@ -305,25 +330,34 @@
         0, 1_000_000, held,
     )
     every = lax.all_gather(plane, "core", axis=0)
-    parents, own = call(
-        middle_kernel, (plane_out, tile), [SMEM] + [VMEM] * 3, [rhs_scratch], 100_000_000, 1_400_000,
-        far_list, every, cpl, recv,
-    )
-    plane = lax.all_to_all(parents, ("x", "z"), 0, 0)
-    low, high = halo(own, own)
+    payload = array(SHARES + 1, ROWS, VECS)
+    parents, bottom, top = call(
+        middle_kernel, (plane_out, payload, payload),
+        [SMEM] + [VMEM] * 3 + [ANY],
+        [rhs_scratch, pltpu.VMEM((2, SHARES, ROWS, VECS), BF), pltpu.SemaphoreType.DMA((2,))],
+        100_000_000, 1_700_000,
+        far_list, every, cpl, recv, held,
+    )
+    plane = exchange(parents, ("x", "z"))
+    below, above = halo(bottom, top)
     every = lax.all_gather(plane, "core", axis=0)
     sent = call(
         last_kernel, array(SHARES, 128, 128), [SMEM] + [VMEM] * 5, [rhs_scratch], 100_000_000, 1_300_000,
-        far_list, every, cpl, own, low, high,
-    )
-    coefs = lax.all_to_all(sent, "y", 0, 0)
+        far_list, every, cpl, bottom, below, above,
+    )
+    coefs = exchange(sent, "y")
+    low, high = halo(wide[:, :NWIN], wide[:, LEAVES - NWIN :])
     plain, q = call(
         second_kernel,
         (array(LEAVES * ROWS, VECS, dtype=F32), array(LEAVES * ROWS, 4 * RANK)),
-        [SMEM, VMEM, ANY],
-        [band_scratch, pltpu.VMEM((SHARES, WIDE + GROUPS + 2, ROWS, VECS), BF), pltpu.SemaphoreType.DMA],
+        [SMEM, VMEM] + [ANY] * 6,
+        [
+            band_scratch,
+            pltpu.VMEM((SHARES, WIDE + GROUPS + 2, ROWS, VECS), BF),
+            pltpu.SemaphoreType.DMA((6,)),
+        ],
         520_000_000, 4_000_000,
-        near_idx, near_blocks, wide,
+        near_list, near_blocks, low, wide, high, below, held, above,
     )
     out = array(LEAVES, ROWS, VECS)
     return call(

time: 176 us -> 169 us (0.960)
  starting transfers between devices: 48.8 us -> 39.6 us
  blocking collectives: 30.8 us -> 36.3 us
  Pallas kernels: 26 us -> 23.4 us
    all_gather x1, waiting for transfers between devices: 24.5 us -> 0.02 us  [operator_twice(): held = lax.all_gather(uc, 'y', axis=0)]
    all_to_all x4, waiting for transfers between devices: 20.3 us -> 37.6 us  [exchange(): return lax.all_to_all(values, axis, 0, 0)]
    all_to_all x1, blocking collectives: 20.2 us -> 28.2 us  [exchange(): return lax.all_to_all(values, axis, 0, 0)]
    ppermute x3, starting transfers between devices: 19.1 us -> 13.3 us  [halo(): lax.ppermute(top, CLUS, forward)]
    ppermute x3, waiting for transfers between devices: 4.4 us -> 9.26 us  [halo(): lax.ppermute(bottom, CLUS, backward)]
    ppermute x3, starting transfers between devices: 8.5 us -> 5.76 us  [halo(): lax.ppermute(bottom, CLUS, backward)]
    ppermute x3, waiting for transfers between devices: 0.01 us -> 2.74 us  [halo(): lax.ppermute(top, CLUS, forward)]
    pallas_call x10 -> x8, Pallas kernels: 26 us -> 23.4 us  [call(): pl.pallas_call(kernel, out_shape=outs, in_specs=ins, out_specs=VMEM if si...]
  transfers between devices with their start and end apart: 12 -> 12, of which waited for: 7 -> 7; matrix products, arithmetic and copies ran while one was open for 1% -> 1% of each run, Pallas kernels for 9% -> 11%
where the time goes in v4:
time: 169 us; the launch traced here: 168 us
  waiting for transfers between devices  50.3 us (30%)
  starting transfers between devices  39.6 us (23%)
  blocking collectives  36.3 us (21%)
  Pallas kernels  23.4 us (14%)
  between operations  14.2 us (8%)
  local copies, waits for them, and re-layouts  4.55 us (3%)
    all_to_all x4, waiting for transfers between devices, exchange(): return lax.all_to_all(values, axis, 0, 0)  37.6 us
    all_to_all x1, blocking collectives, exchange(): return lax.all_to_all(values, axis, 0, 0)  28.2 us
    pallas_call x8, Pallas kernels, call(): pl.pallas_call(kernel, out_shape=outs, in_specs=ins, out_specs=VMEM if si...  23.4 us
    all_to_all x4, starting transfers between devices, exchange(): return lax.all_to_all(values, axis, 0, 0)  20.5 us
    ppermute x3, starting transfers between devices, halo(): lax.ppermute(top, CLUS, forward)  13.3 us
    ppermute x3, waiting for transfers between devices, halo(): lax.ppermute(bottom, CLUS, backward)  9.26 us
    all_gather x2, blocking collectives, operator_twice(): every = lax.all_gather(plane, 'core', axis=0)  8.03 us
    ppermute x3, starting transfers between devices, halo(): lax.ppermute(bottom, CLUS, backward)  5.76 us
  transfers between devices with their start and end apart: 12, of which 7 were waited for; matrix products, arithmetic and copies ran while one was open for 1% of the time, Pallas kernels for 11%

profile of v4, /device:TPU:1, one launch (start us, length us, event | category | flops | bytes accessed | tf_op | source)
XLA Modules:
  0.0 168.3 jit_solution(3336733798116389365)
XLA Ops:
  7.2 2.5 %shard_map.86 = (bf16[8,17,16,256]{3,2,1,0:T(8,128)(2,1)}, bf16[2,128,64]{2,1,0:T(8,128)(2,1)}, bf16[16,16,256]{2,1,0:T(8,128)(2,1)}) custom-call(bf16[16,16,256]{2,1,0:T(8,128)(2,1)} %d_ref.1, bf16[16,16,64]{2,1,0:T(8,128)(2,1)} %b_ref.1, bf16[16,64,64]{2,1,0:T(8,128)(2,1)} %t_ref.1, bf16[2,27,8,64]{3,2,1,0:T(8,128)(2,1)} %bitcast.12), custom_call_target="tpu_custom_call" | custom-call | flops 40000000 | bytes 1700000 | tf_op jit(solution)/shard_map/pallas_call | solution.py:262
  9.7 7.6 %all-to-all-start = ((bf16[8,17,16,256]{3,2,1,0:T(8,128)(2,1)}), bf16[8,17,16,256]{3,2,1,0:T(8,128)(2,1)S(1)}, u32[]{:S(2)}, u32[]{:S(2)}) async-start(bf16[8,17,16,256]{3,2,1,0:T(8,128)(2,1)} %get-tuple-element.13), calls=%async_computation | async-start | bytes 2228224 | tf_op jit(solution)/shard_map/all_to_all | solution.py:280
  18.1 28.2 %all-to-all-done.own_ref.recv_ref = bf16[8,17,16,256]{3,2,1,0:T(8,128)(2,1)S(1)} async-done(((bf16[8,17,16,256]{3,2,1,0:T(8,128)(2,1)}), bf16[8,17,16,256]{3,2,1,0:T(8,128)(2,1)S(1)}, u32[]{:S(2)}, u32[]{:S(2)}) %all-to-all-start) | async-done | bytes 1114144 | tf_op jit(solution)/shard_map/all_to_all | solution.py:280
  46.4 5.2 %collective-permute-start = (bf16[8,4,16,256]{3,2,1,0:T(8,128)(2,1)S(1)}, bf16[8,4,16,256]{3,2,1,0:T(8,128)(2,1)S(1)}, u32[]{:S(2)}, u32[]{:S(2)}) collective-permute-start(bf16[8,4,16,256]{3,2,1,0:T(8,128)(2,1)S(1)} %get-tuple-element.25), channel_id=1, source_target_pairs={{0,8},{8,16},{16,24},{24,32},{32,40},{40,48},{48,56},{56,64},{64,7... | collective-permute-start | bytes 786440 | tf_op jit(solution)/shard_map/ppermute | solution.py:276
  51.6 1.9 %collective-permute-start.1 = (bf16[8,4,16,256]{3,2,1,0:T(8,128)(2,1)S(1)}, bf16[8,4,16,256]{3,2,1,0:T(8,128)(2,1)S(1)}, u32[]{:S(2)}, u32[]{:S(2)}) collective-permute-start(bf16[8,4,16,256]{3,2,1,0:T(8,128)(2,1)S(1)} %get-tuple-element.24), channel_id=1, source_target_pairs={{8,0},{16,8},{24,16},{32,24},{40,32},{48,40},{56,48},{64,56},{72,6... | collective-permute-start | bytes 786440 | tf_op jit(solution)/shard_map/ppermute | solution.py:276
  54.9 4.8 %collective-permute-done.1.hi_ref = bf16[8,4,16,256]{3,2,1,0:T(8,128)(2,1)S(1)} collective-permute-done((bf16[8,4,16,256]{3,2,1,0:T(8,128)(2,1)S(1)}, bf16[8,4,16,256]{3,2,1,0:T(8,128)(2,1)S(1)}, u32[]{:S(2)}, u32[]{:S(2)}) %collective-permute-start.1) | collective-permute-done | bytes 262176 | tf_op jit(solution)/shard_map/ppermute | solution.py:276
  60.4 4.0 %shard_map.87 = (f32[16,16,256]{2,1,0:T(8,128)}, bf16[16,16,256]{2,1,0:T(8,128)(2,1)}, bf16[8,96,128]{2,1,0:T(8,128)(2,1)}) custom-call(s32[16,9]{1,0:T(8,128)} %idx_ref.3, bf16[16,9,16,128]{3,2,1,0:T(8,128)(2,1)} %near_ref.3, bf16[8,4,16,256]{3,2,1,0:T(8,128)(2,1)} %copy-done.6, bf16[8,17,16,256]{3,2,1,0:T(8,128)(2,1)} %copy-done, ...), custom_call_target="tpu_custom_call" | custom-call | flops 420000000 | bytes 4500000 | tf_op jit(solution)/shard_map/pallas_call | solution.py:262
  66.0 28.2 %all_to_all.25 = bf16[32,32,128]{2,1,0:T(8,128)(2,1)S(1)} all-to-all(bf16[32,32,128]{2,1,0:T(8,128)(2,1)} %shard_map.88), channel_id=1, replica_groups=mesh['x'=4,'z'=8,'core'=2,'y'=8] {'x','z'}, dimensions={0} | all-to-all | bytes 524288 | tf_op jit(solution)/shard_map/all_to_all | solution.py:280
  94.2 3.4 %all-to-all-start.2 = ((bf16[8,96,128]{2,1,0:T(8,128)(2,1)}), bf16[8,96,128]{2,1,0:T(8,128)(2,1)S(1)}, u32[]{:S(2)}, u32[]{:S(2)}) async-start(bf16[8,96,128]{2,1,0:T(8,128)(2,1)} %get-tuple-element.17), calls=%async_computation.2 | async-start | bytes 393216 | tf_op jit(solution)/shard_map/all_to_all | solution.py:280
  97.7 2.0 %shard_map.89.cpl_ref = bf16[2,128,864]{2,1,0:T(8,128)(2,1)} custom-call(bf16[8,16,16,256]{3,2,1,0:T(8,128)(2,1)} %bitcast.5), custom_call_target="tpu_custom_call" | custom-call | bytes 1000000 | tf_op jit(solution)/shard_map/pallas_call | solution.py:262
  99.7 2.3 %all-gather = bf16[64,32,128]{2,1,0:T(8,128)(2,1)} all-gather(bf16[32,32,128]{2,1,0:T(8,128)(2,1)S(1)} %all_to_all.25), channel_id=2, replica_groups=mesh['x'=4,'z'=8,'core'=2,'y'=8] {'core'}, dimensions={0}, use_global_device_ids=true | all-gather | bytes 786432 | tf_op jit(solution)/shard_map/all_gather | solution.py:332
  102.0 6.3 %all-to-all-done.2.recv_ref = bf16[8,96,128]{2,1,0:T(8,128)(2,1)S(1)} async-done(((bf16[8,96,128]{2,1,0:T(8,128)(2,1)}), bf16[8,96,128]{2,1,0:T(8,128)(2,1)S(1)}, u32[]{:S(2)}, u32[]{:S(2)}) %all-to-all-start.2) | async-done | bytes 196640 | tf_op jit(solution)/shard_map/all_to_all | solution.py:280
  109.0 3.7 %shard_map.90 = (bf16[32,32,128]{2,1,0:T(8,128)(2,1)}, bf16[9,16,256]{2,1,0:T(8,128)(2,1)}, bf16[9,16,256]{2,1,0:T(8,128)(2,1)}) custom-call(s32[2,27]{1,0:T(2,128)} %far_ref.3, bf16[2,32,32,128]{3,2,1,0:T(8,128)(2,1)} %bitcast.11, bf16[2,128,864]{2,1,0:T(8,128)(2,1)} %shard_map.89.cpl_ref, bf16[8,96,128]{2,1,0:T(8,128)(2,1)} %copy-done.2, ...), custom_call_target="tpu_custom_call" | custom-call | flops 100000000 | bytes 1700000 | tf_op jit(solution)/shard_map/pallas_call | solution.py:262
  112.7 6.0 %all-to-all-start.3 = ((bf16[32,32,128]{2,1,0:T(8,128)(2,1)}), bf16[32,32,128]{2,1,0:T(8,128)(2,1)S(1)}, u32[]{:S(2)}, u32[]{:S(2)}) async-start(bf16[32,32,128]{2,1,0:T(8,128)(2,1)} %get-tuple-element.18), calls=%async_computation.3 | async-start | bytes 524288 | tf_op jit(solution)/shard_map/all_to_all | solution.py:280
  118.7 4.7 %collective-permute-start.2 = (bf16[9,16,256]{2,1,0:T(8,128)(2,1)}, bf16[9,16,256]{2,1,0:T(8,128)(2,1)S(1)}, u32[]{:S(2)}, u32[]{:S(2)}) collective-permute-start(bf16[9,16,256]{2,1,0:T(8,128)(2,1)} %get-tuple-element.20), channel_id=1, source_target_pairs={{0,8},{8,16},{16,24},{24,32},{32,40},{40,48},{48,56},{56,64},{64,7... | collective-permute-start | bytes 221192 | tf_op jit(solution)/shard_map/ppermute | solution.py:276
  125.3 3.0 %all-to-all-done.3 = bf16[32,32,128]{2,1,0:T(8,128)(2,1)S(1)} async-done(((bf16[32,32,128]{2,1,0:T(8,128)(2,1)}), bf16[32,32,128]{2,1,0:T(8,128)(2,1)S(1)}, u32[]{:S(2)}, u32[]{:S(2)}) %all-to-all-start.3) | async-done | bytes 262176 | tf_op jit(solution)/shard_map/all_to_all | solution.py:280
  128.3 5.7 %all-gather.2 = bf16[64,32,128]{2,1,0:T(8,128)(2,1)} all-gather(bf16[32,32,128]{2,1,0:T(8,128)(2,1)S(1)} %all-to-all-done.3), channel_id=4, replica_groups=mesh['x'=4,'z'=8,'core'=2,'y'=8] {'core'}, dimensions={0}, use_global_device_ids=true | all-gather | bytes 786432 | tf_op jit(solution)/shard_map/all_gather | solution.py:343
  134.7 3.0 %shard_map.91 = bf16[8,128,128]{2,1,0:T(8,128)(2,1)} custom-call(s32[2,27]{1,0:T(2,128)} %far_ref.3, bf16[2,32,32,128]{3,2,1,0:T(8,128)(2,1)} %bitcast.10, bf16[2,128,864]{2,1,0:T(8,128)(2,1)} %shard_map.89.cpl_ref, bf16[9,16,256]{2,1,0:T(8,128)(2,1)} %get-tuple-element.19.own_ref, bf16[9,16,256]{2,1,0:T(8,128)(2,1)} %copy-done.3, bf16[9,16,256]{2,1,0:T(8,128)(2,1)} %copy-done.4), custom_call_target="tpu_custom_call" | custom-call | flops 100000000 | bytes 1300000 | tf_op jit(solution)/shard_map/pallas_call | solution.py:262
  137.7 3.4 %all-to-all-start.4 = ((bf16[8,128,128]{2,1,0:T(8,128)(2,1)}), bf16[8,128,128]{2,1,0:T(8,128)(2,1)S(1)}, u32[]{:S(2)}, u32[]{:S(2)}) async-start(bf16[8,128,128]{2,1,0:T(8,128)(2,1)} %shard_map.91), calls=%async_computation.4 | async-start | bytes 524288 | tf_op jit(solution)/shard_map/all_to_all | solution.py:280
  142.2 3.5 %collective-permute-start.4 = (bf16[8,4,16,256]{3,2,1,0:T(8,128)(2,1)S(1)}, bf16[8,4,16,256]{3,2,1,0:T(8,128)(2,1)S(1)}, u32[]{:S(2)}, u32[]{:S(2)}) collective-permute-start(bf16[8,4,16,256]{3,2,1,0:T(8,128)(2,1)S(1)} %get-tuple-element.27), channel_id=1, source_target_pairs={{0,8},{8,16},{16,24},{24,32},{32,40},{40,48},{48,56},{56,64},{64,7... | collective-permute-start | bytes 786440 | tf_op jit(solution)/shard_map/ppermute | solution.py:276
  145.7 1.9 %collective-permute-start.5 = (bf16[8,4,16,256]{3,2,1,0:T(8,128)(2,1)S(1)}, bf16[8,4,16,256]{3,2,1,0:T(8,128)(2,1)S(1)}, u32[]{:S(2)}, u32[]{:S(2)}) collective-permute-start(bf16[8,4,16,256]{3,2,1,0:T(8,128)(2,1)S(1)} %get-tuple-element.26), channel_id=1, source_target_pairs={{8,0},{16,8},{24,16},{32,24},{40,32},{48,40},{56,48},{64,56},{72,6... | collective-permute-start | bytes 786440 | tf_op jit(solution)/shard_map/ppermute | solution.py:276
  149.0 4.5 %collective-permute-done.5.hi_ref = bf16[8,4,16,256]{3,2,1,0:T(8,128)(2,1)S(1)} collective-permute-done((bf16[8,4,16,256]{3,2,1,0:T(8,128)(2,1)S(1)}, bf16[8,4,16,256]{3,2,1,0:T(8,128)(2,1)S(1)}, u32[]{:S(2)}, u32[]{:S(2)}) %collective-permute-start.5) | collective-permute-done | bytes 262176 | tf_op jit(solution)/shard_map/ppermute | solution.py:276
  154.2 4.3 %shard_map.92 = (f32[256,256]{1,0:T(8,128)}, bf16[256,256]{1,0:T(8,128)(2,1)}) custom-call(s32[16,9]{1,0:T(8,128)} %idx_ref.3, bf16[16,9,16,128]{3,2,1,0:T(8,128)(2,1)} %near_ref.3, bf16[8,4,16,256]{3,2,1,0:T(8,128)(2,1)} %copy-done.5, bf16[8,16,16,256]{3,2,1,0:T(8,128)(2,1)} %bitcast.9, bf16[8,4,16,256]{3,2,1,0:T(8,128)(2,1)} %copy-done.7, ...), custom_call_target="tpu_custom_call" | custom-call | flops 520000000 | bytes 4000000 | tf_op jit(solution)/shard_map/pallas_call | solution.py:262
  159.2 2.3 %shard_map.93 = (bf16[16,16,256]{2,1,0:T(8,128)(2,1)}, bf16[16,16,256]{2,1,0:T(8,128)(2,1)}) custom-call(f32[16,16,256]{2,1,0:T(8,128)} %get-tuple-element.15.keep_ref, bf16[2,128,64]{2,1,0:T(8,128)(2,1)} %get-tuple-element.14.u_ref, bf16[8,128,128]{2,1,0:T(8,128)(2,1)} %copy-done.1, f32[256,256]{1,0:T(8,128)} %get-tuple-element.22.near_ref, ...), custom_call_target="tpu_custom_call" | custom-call | flops 100000000 | bytes 2000000 | tf_op jit(solution)/shard_map/pallas_call | solution.py:262
  (33 shorter events, 11.6 us)
Async XLA Ops:
  9.7 36.6 %all-to-all-start = ((bf16[8,17,16,256]{3,2,1,0:T(8,128)(2,1)}), bf16[8,17,16,256]{3,2,1,0:T(8,128)(2,1)S(1)}, u32[]{:S(2)}, u32[]{:S(2)}) async-start(bf16[8,17,16,256]{3,2,1,0:T(8,128)(2,1)} %get-tuple-element.13), calls=%async_computation | async-start | bytes 2228224 | tf_op jit(solution)/shard_map/all_to_all | solution.py:280
  17.4 80.3 %all-gather.7.cloned.1.call-start = ((), (), s32[]{:S(2)}) async-start(), calls=%async_computation.5 | async-start | bytes 1179648 | tf_op jit(solution)/shard_map/all_gather | solution.py:298
  18.1 123.0 %all-gather.9.cloned.1.call-start = ((), (), s32[]{:S(2)}) async-start(), calls=%async_computation.6 | async-start | bytes 1179648 | tf_op jit(solution)/shard_map/all_gather | solution.py:320
  46.4 13.3 %copy-start = (bf16[8,17,16,256]{3,2,1,0:T(8,128)(2,1)}, bf16[8,17,16,256]{3,2,1,0:T(8,128)(2,1)S(1)}, u32[]{:S(2)}) copy-start(bf16[8,17,16,256]{3,2,1,0:T(8,128)(2,1)S(1)} %all-to-all-done.own_ref.recv_ref) | copy-start | bytes 3342340
  46.4 8.5 %collective-permute-start = (bf16[8,4,16,256]{3,2,1,0:T(8,128)(2,1)S(1)}, bf16[8,4,16,256]{3,2,1,0:T(8,128)(2,1)S(1)}, u32[]{:S(2)}, u32[]{:S(2)}) collective-permute-start(bf16[8,4,16,256]{3,2,1,0:T(8,128)(2,1)S(1)} %get-tuple-element.25), channel_id=1, source_target_pairs={{0,8},{8,16},{16,24},{24,32},{32,40},{40,48},{48,56},{56,64},{64,7... | collective-permute-start | bytes 786440 | tf_op jit(solution)/shard_map/ppermute | solution.py:276
  51.6 8.1 %collective-permute-start.1 = (bf16[8,4,16,256]{3,2,1,0:T(8,128)(2,1)S(1)}, bf16[8,4,16,256]{3,2,1,0:T(8,128)(2,1)S(1)}, u32[]{:S(2)}, u32[]{:S(2)}) collective-permute-start(bf16[8,4,16,256]{3,2,1,0:T(8,128)(2,1)S(1)} %get-tuple-element.24), channel_id=1, source_target_pairs={{8,0},{16,8},{24,16},{32,24},{40,32},{48,40},{56,48},{64,56},{72,6... | collective-permute-start | bytes 786440 | tf_op jit(solution)/shard_map/ppermute | solution.py:276
  54.9 4.8 %copy-start.6 = (bf16[8,4,16,256]{3,2,1,0:T(8,128)(2,1)}, bf16[8,4,16,256]{3,2,1,0:T(8,128)(2,1)S(1)}, u32[]{:S(2)}) copy-start(bf16[8,4,16,256]{3,2,1,0:T(8,128)(2,1)S(1)} %collective-permute-done.lo_ref) | copy-start | bytes 786436
  59.7 0.7 copy-start.8
  94.2 14.0 %all-to-all-start.2 = ((bf16[8,96,128]{2,1,0:T(8,128)(2,1)}), bf16[8,96,128]{2,1,0:T(8,128)(2,1)S(1)}, u32[]{:S(2)}, u32[]{:S(2)}) async-start(bf16[8,96,128]{2,1,0:T(8,128)(2,1)} %get-tuple-element.17), calls=%async_computation.2 | async-start | bytes 393216 | tf_op jit(solution)/shard_map/all_to_all | solution.py:280
  108.3 0.7 copy-start.2
  112.7 15.7 %all-to-all-start.3 = ((bf16[32,32,128]{2,1,0:T(8,128)(2,1)}), bf16[32,32,128]{2,1,0:T(8,128)(2,1)S(1)}, u32[]{:S(2)}, u32[]{:S(2)}) async-start(bf16[32,32,128]{2,1,0:T(8,128)(2,1)} %get-tuple-element.18), calls=%async_computation.3 | async-start | bytes 524288 | tf_op jit(solution)/shard_map/all_to_all | solution.py:280
  118.7 15.4 %collective-permute-start.2 = (bf16[9,16,256]{2,1,0:T(8,128)(2,1)}, bf16[9,16,256]{2,1,0:T(8,128)(2,1)S(1)}, u32[]{:S(2)}, u32[]{:S(2)}) collective-permute-start(bf16[9,16,256]{2,1,0:T(8,128)(2,1)} %get-tuple-element.20), channel_id=1, source_target_pairs={{0,8},{8,16},{16,24},{24,32},{32,40},{40,48},{48,56},{56,64},{64,7... | collective-permute-start | bytes 221192 | tf_op jit(solution)/shard_map/ppermute | solution.py:276
  123.4 10.7 %collective-permute-start.3 = (bf16[9,16,256]{2,1,0:T(8,128)(2,1)}, bf16[9,16,256]{2,1,0:T(8,128)(2,1)S(1)}, u32[]{:S(2)}, u32[]{:S(2)}) collective-permute-start(bf16[9,16,256]{2,1,0:T(8,128)(2,1)} %get-tuple-element.19.own_ref), channel_id=1, source_target_pairs={{8,0},{16,8},{24,16},{32,24},{40,32},{48,40},{56,48},{64,56},{72,6... | collective-permute-start | bytes 221192 | tf_op jit(solution)/shard_map/ppermute | solution.py:276
  134.1 0.6 copy-start.3
  134.1 0.6 copy-start.4
  137.7 20.8 %all-to-all-start.4 = ((bf16[8,128,128]{2,1,0:T(8,128)(2,1)}), bf16[8,128,128]{2,1,0:T(8,128)(2,1)S(1)}, u32[]{:S(2)}, u32[]{:S(2)}) async-start(bf16[8,128,128]{2,1,0:T(8,128)(2,1)} %shard_map.91), calls=%async_computation.4 | async-start | bytes 524288 | tf_op jit(solution)/shard_map/all_to_all | solution.py:280
  142.2 6.8 %collective-permute-start.4 = (bf16[8,4,16,256]{3,2,1,0:T(8,128)(2,1)S(1)}, bf16[8,4,16,256]{3,2,1,0:T(8,128)(2,1)S(1)}, u32[]{:S(2)}, u32[]{:S(2)}) collective-permute-start(bf16[8,4,16,256]{3,2,1,0:T(8,128)(2,1)S(1)} %get-tuple-element.27), channel_id=1, source_target_pairs={{0,8},{8,16},{16,24},{24,32},{32,40},{40,48},{48,56},{56,64},{64,7... | collective-permute-start | bytes 786440 | tf_op jit(solution)/shard_map/ppermute | solution.py:276
  145.7 7.8 %collective-permute-start.5 = (bf16[8,4,16,256]{3,2,1,0:T(8,128)(2,1)S(1)}, bf16[8,4,16,256]{3,2,1,0:T(8,128)(2,1)S(1)}, u32[]{:S(2)}, u32[]{:S(2)}) collective-permute-start(bf16[8,4,16,256]{3,2,1,0:T(8,128)(2,1)S(1)} %get-tuple-element.26), channel_id=1, source_target_pairs={{8,0},{16,8},{24,16},{32,24},{40,32},{48,40},{56,48},{64,56},{72,6... | collective-permute-start | bytes 786440 | tf_op jit(solution)/shard_map/ppermute | solution.py:276
  149.0 4.5 %copy-start.5 = (bf16[8,4,16,256]{3,2,1,0:T(8,128)(2,1)}, bf16[8,4,16,256]{3,2,1,0:T(8,128)(2,1)S(1)}, u32[]{:S(2)}) copy-start(bf16[8,4,16,256]{3,2,1,0:T(8,128)(2,1)S(1)} %collective-permute-done.4.lo_ref) | copy-start | bytes 786436
  153.5 0.7 copy-start.7
  158.5 0.7 copy-start.1
Sparse Core Ops, SparseCore 0:
  20.8 43.9 all-gather.6
  67.5 40.3 all-gather.8

commit v5 on v4

--- a/solution.py
+++ b/solution.py
@@ -119,7 +119,7 @@
 
 def near_kernel(
     idx_ref, near_ref, lo_ref, own_ref, hi_ref, u_ref,
-    keep_ref, low_ref, sent_ref,
+    keep_ref, low_ref, bottom_ref, top_ref, sent_ref,
     s_scr, w_scr, sems,
 ):
     top = NWIN + LEAVES
@@ -131,7 +131,10 @@
     res = dot(band, leaf_rows(w_scr))
     keep_ref[...] = res.reshape(LEAVES, ROWS, VECS)
     low = res.astype(BF)
-    low_ref[...] = low.reshape(LEAVES, ROWS, VECS)
+    rows = low.reshape(LEAVES, ROWS, VECS)
+    low_ref[...] = rows
+    bottom_ref[...] = rows[:NWIN]
+    top_ref[...] = rows[LEAVES - NWIN :]
     part = [dot_top(u_ref[p], low[PANEL * p : PANEL * (p + 1)]) for p in range(2)]
     gram = jnp.concatenate([dot_top(u_ref[p], u_ref[p]) for p in range(2)], axis=1).astype(BF)
     for s in range(SHARES):
@@ -139,15 +142,18 @@
         sent_ref[s, 32:] = gram
 
 
+def widen_kernel(lo_ref, own_ref, hi_ref, out_ref):
+    out_ref[:NWIN] = lo_ref[...]
+    out_ref[NWIN : NWIN + LEAVES] = own_ref[...]
+    out_ref[NWIN + LEAVES :] = hi_ref[...]
+
+
 def second_kernel(
-    idx_ref, near_ref, lo_ref, own_ref, hi_ref, ulo_ref, uc_ref, uhi_ref,
+    idx_ref, near_ref, own_ref, ulo_ref, uc_ref, uhi_ref,
     out_ref, q_ref, s_scr, w_scr, sems,
 ):
-    top = NWIN + LEAVES
     pairs = (
-        (lo_ref, w_scr.at[:, :NWIN]),
-        (own_ref, w_scr.at[:, NWIN:top]),
-        (hi_ref, w_scr.at[:, top:WIDE]),
+        (own_ref, w_scr.at[:, :WIDE]),
         (ulo_ref.at[:SHARES], w_scr.at[:, WIDE]),
         (uc_ref.at[:, :GROUPS], w_scr.at[:, WIDE + 1 : WIDE + 1 + GROUPS]),
         (uhi_ref.at[:SHARES], w_scr.at[:, WIDE + 1 + GROUPS]),
@@ -206,9 +212,14 @@
 
 
 def middle_kernel(
-    far_ref, pc_ref, cpl_ref, recv_ref, held_ref, out_ref, bottom_ref, top_ref, rhs_scr, u_scr, sems
+    far_ref, pc_ref, cpl_ref, recv_ref, held_ref, out_ref, bottom_ref, top_ref,
+    rhs_scr, u_scr, recv_scr, sems,
 ):
-    pairs = ((held_ref.at[:, 0], u_scr.at[0]), (held_ref.at[:, GROUPS - 1], u_scr.at[1]))
+    pairs = (
+        (held_ref.at[:, 0], u_scr.at[0]),
+        (held_ref.at[:, GROUPS - 1], u_scr.at[1]),
+        (recv_ref, recv_scr),
+    )
     moves = fetch(pairs, sems)
     coef = far_sums(far_ref, pc_ref, (cpl_ref[0], cpl_ref[1]), rhs_scr)
     slab = fold(pack_parents(coef[0].astype(F32), coef[1].astype(F32)).astype(BF))
@@ -216,17 +227,22 @@
         moves[n].wait()
         ref[:SHARES] = u_scr[n]
         ref[SHARES] = slab
-    total = jnp.sum(recv_ref[...].astype(F32), axis=0)
+    moves[2].wait()
+    total = jnp.sum(recv_scr[...].astype(F32), axis=0)
     gram = total[32:].astype(BF)
     own = [dot(gram[:, RANK * p : RANK * (p + 1)], coef[p]) for p in range(2)]
     packed = (total[:32] + pack_parents(own[0], own[1])).astype(BF)
     out_ref[...] = jnp.broadcast_to(packed[None], out_ref.shape)
 
 
-def last_kernel(far_ref, pc_ref, cpl_ref, own_ref, lo_ref, hi_ref, out_ref, rhs_scr):
+def last_kernel(far_ref, pc_ref, cpl_ref, own_ref, lo_ref, hi_ref, out_ref, rhs_scr, t_scr, sems):
+    pairs = [(ref.at[SHARES], t_scr.at[n]) for n, ref in enumerate((lo_ref, own_ref, hi_ref))]
+    moves = fetch(pairs, sems)
     coef = far_sums(far_ref, pc_ref, (cpl_ref[0], cpl_ref[1]), rhs_scr)
     tile = pack_parents(coef[0].astype(F32), coef[1].astype(F32)).astype(BF)
-    both = [unfold(ref[SHARES]) for ref in (lo_ref, own_ref, hi_ref)] + [tile]
+    for move in moves:
+        move.wait()
+    both = [unfold(t_scr[n]) for n in range(3)] + [tile]
     both = jnp.concatenate(both, axis=0)
     out_ref[...] = jnp.broadcast_to(both[None], out_ref.shape)
 
@@ -240,7 +256,11 @@
     return jnp.concatenate(halves, axis=0)
 
 
-def finish_kernel(keep_ref, u_ref, c_ref, near_ref, q_ref, first_ref, second_ref):
+def finish_kernel(
+    keep_ref, u_ref, recv_ref, near_ref, q_ref, first_ref, second_ref, c_ref, sems
+):
+    for move in fetch(((recv_ref, c_ref),), sems):
+        move.wait()
     below, above = coefficients(c_ref, 0, 1), coefficients(c_ref, 2, 0)
     own = [coefficients(c_ref, 1, p) for p in range(2)]
     new = [coefficients(c_ref, 3, p) for p in range(2)]
@@ -295,8 +315,9 @@
         [VMEM] * 4, [], 40_000_000, 1_700_000,
         density, basis, transfer, jnp.swapaxes(coupling, 2, 3),
     )
+    whole = exchange(sent, "y")
+    uc, whole = lax.optimization_barrier((uc, whole))
     held = lax.all_gather(uc, "y", axis=0)
-    whole = exchange(sent, "y")
     parents = call(
         parent_kernel, plane_out, [ANY],
         [pltpu.VMEM((SHARES, ROWS, VECS), BF), pltpu.SemaphoreType.DMA], 100_000, 300_000,
@@ -305,11 +326,13 @@
     plane = exchange(parents, ("x", "z"))
 
     low, high = halo(whole[:, :NWIN], whole[:, LEAVES - NWIN : LEAVES])
-    keep, wide, sent = call(
+    keep, wide, bottom, top, sent = call(
         near_kernel,
         (
             array(LEAVES, ROWS, VECS, dtype=F32),
             array(LEAVES, ROWS, VECS),
+            array(NWIN, ROWS, VECS),
+            array(NWIN, ROWS, VECS),
             array(SHARES, 96, 128),
         ),
         [SMEM, VMEM, ANY, ANY, ANY, VMEM],
@@ -317,8 +340,10 @@
         420_000_000, 4_500_000,
         near_list, near_blocks, low, whole, high, u,
     )
+    recv = exchange(sent, "y")
+    low, high = halo(bottom, top)
+    wide = call(widen_kernel, array(WIDE, ROWS, VECS), [VMEM] * 3, [], 0, 400_000, low, wide, high)
     wide = lax.all_gather(wide, "y", axis=0)
-    recv = exchange(sent, "y")
 
     cpl = call(
         coupling_kernel, cpl_out, [ANY],
@@ -333,8 +358,13 @@
     payload = array(SHARES + 1, ROWS, VECS)
     parents, bottom, top = call(
         middle_kernel, (plane_out, payload, payload),
-        [SMEM] + [VMEM] * 3 + [ANY],
-        [rhs_scratch, pltpu.VMEM((2, SHARES, ROWS, VECS), BF), pltpu.SemaphoreType.DMA((2,))],
+        [SMEM] + [VMEM] * 2 + [ANY] * 2,
+        [
+            rhs_scratch,
+            pltpu.VMEM((2, SHARES, ROWS, VECS), BF),
+            pltpu.VMEM((SHARES, 96, 128), BF),
+            pltpu.SemaphoreType.DMA((3,)),
+        ],
         100_000_000, 1_700_000,
         far_list, every, cpl, recv, held,
     )
@@ -342,26 +372,29 @@
     below, above = halo(bottom, top)
     every = lax.all_gather(plane, "core", axis=0)
     sent = call(
-        last_kernel, array(SHARES, 128, 128), [SMEM] + [VMEM] * 5, [rhs_scratch], 100_000_000, 1_300_000,
+        last_kernel, array(SHARES, 128, 128), [SMEM] + [VMEM] * 2 + [ANY] * 3,
+        [rhs_scratch, pltpu.VMEM((3, ROWS, VECS), BF), pltpu.SemaphoreType.DMA((3,))],
+        100_000_000, 1_300_000,
         far_list, every, cpl, bottom, below, above,
     )
     coefs = exchange(sent, "y")
-    low, high = halo(wide[:, :NWIN], wide[:, LEAVES - NWIN :])
     plain, q = call(
         second_kernel,
         (array(LEAVES * ROWS, VECS, dtype=F32), array(LEAVES * ROWS, 4 * RANK)),
-        [SMEM, VMEM] + [ANY] * 6,
+        [SMEM, VMEM] + [ANY] * 4,
         [
             band_scratch,
             pltpu.VMEM((SHARES, WIDE + GROUPS + 2, ROWS, VECS), BF),
-            pltpu.SemaphoreType.DMA((6,)),
+            pltpu.SemaphoreType.DMA((4,)),
         ],
         520_000_000, 4_000_000,
-        near_list, near_blocks, low, wide, high, below, held, above,
+        near_list, near_blocks, wide, below, held, above,
     )
     out = array(LEAVES, ROWS, VECS)
     return call(
-        finish_kernel, (out, out), [VMEM] * 5, [], 100_000_000, 2_000_000,
+        finish_kernel, (out, out), [VMEM] * 2 + [ANY] + [VMEM] * 2,
+        [pltpu.VMEM((SHARES, 128, 128), BF), pltpu.SemaphoreType.DMA((1,))],
+        100_000_000, 2_000_000,
         keep, u, coefs, plain, q,
     )
 

time: 169 us -> 174 us (1.030)
  blocking collectives: 36.3 us -> 67.7 us
  waiting for transfers between devices: 50.3 us -> 26.9 us
  starting transfers between devices: 39.6 us -> 34.3 us
  Pallas kernels: 23.4 us -> 26.4 us
    all_to_all x1 -> x2, blocking collectives: 28.2 us -> 58.2 us  [exchange(): return lax.all_to_all(values, axis, 0, 0)]
    all_to_all x4 -> x3, waiting for transfers between devices: 37.6 us -> 17 us  [exchange(): return lax.all_to_all(values, axis, 0, 0)]
    all_to_all x4 -> x3, starting transfers between devices: 20.5 us -> 13.1 us  [exchange(): return lax.all_to_all(values, axis, 0, 0)]
    pallas_call x8 -> x9, Pallas kernels: 23.4 us -> 26.4 us  [call(): pl.pallas_call(kernel, out_shape=outs, in_specs=ins, out_specs=VMEM if si...]
  transfers between devices with their start and end apart: 12 -> 11, of which waited for: 7 -> 6; matrix products, arithmetic and copies ran while one was open for 1% -> 0% of each run, Pallas kernels for 11% -> 12%
where the time goes in v5:
time: 174 us; the launch traced here: 173 us
  blocking collectives  67.7 us (39%)
  starting transfers between devices  34.3 us (20%)
  waiting for transfers between devices  26.9 us (15%)
  Pallas kernels  26.4 us (15%)
  between operations  14.2 us (8%)
  local copies, waits for them, and re-layouts  3.39 us (2%)
    all_to_all x2, blocking collectives, exchange(): return lax.all_to_all(values, axis, 0, 0)  58.2 us
    pallas_call x9, Pallas kernels, call(): pl.pallas_call(kernel, out_shape=outs, in_specs=ins, out_specs=VMEM if si...  26.4 us
    all_to_all x3, waiting for transfers between devices, exchange(): return lax.all_to_all(values, axis, 0, 0)  17 us
    ppermute x3, starting transfers between devices, halo(): lax.ppermute(top, CLUS, forward)  14.8 us
    all_to_all x3, starting transfers between devices, exchange(): return lax.all_to_all(values, axis, 0, 0)  13.1 us
    all_gather x2, blocking collectives, operator_twice(): every = lax.all_gather(plane, 'core', axis=0)  9.43 us
    ppermute x3, waiting for transfers between devices, halo(): lax.ppermute(bottom, CLUS, backward)  8.52 us
    ppermute x3, starting transfers between devices, halo(): lax.ppermute(bottom, CLUS, backward)  6.24 us
  transfers between devices with their start and end apart: 11, of which 6 were waited for; matrix products, arithmetic and copies ran while one was open for 0% of the time, Pallas kernels for 12%

profile of v5, /device:TPU:1, one launch (start us, length us, event | category | flops | bytes accessed | tf_op | source)
XLA Modules:
  0.0 172.8 jit_solution(3949448776248631173)
XLA Ops:
  7.2 2.5 %shard_map.86 = (bf16[8,17,16,256]{3,2,1,0:T(8,128)(2,1)}, bf16[2,128,64]{2,1,0:T(8,128)(2,1)}, bf16[16,16,256]{2,1,0:T(8,128)(2,1)}) custom-call(bf16[16,16,256]{2,1,0:T(8,128)(2,1)} %d_ref.1, bf16[16,16,64]{2,1,0:T(8,128)(2,1)} %b_ref.1, bf16[16,64,64]{2,1,0:T(8,128)(2,1)} %t_ref.1, bf16[2,27,8,64]{3,2,1,0:T(8,128)(2,1)} %bitcast.11), custom_call_target="tpu_custom_call" | custom-call | flops 40000000 | bytes 1700000 | tf_op jit(solution)/shard_map/pallas_call | solution.py:282
  9.8 34.7 %all_to_all.25.own_ref.recv_ref = bf16[8,17,16,256]{3,2,1,0:T(8,128)(2,1)S(1)} all-to-all(bf16[8,17,16,256]{3,2,1,0:T(8,128)(2,1)} %get-tuple-element.18), channel_id=1, replica_groups=mesh['x'=4,'z'=8,'core'=2,'y'=8] {'y'}, dimensions={0} | all-to-all | bytes 2228224 | tf_op jit(solution)/shard_map/all_to_all | solution.py:300
  44.5 8.0 %collective-permute-start = (bf16[8,4,16,256]{3,2,1,0:T(8,128)(2,1)S(1)}, bf16[8,4,16,256]{3,2,1,0:T(8,128)(2,1)S(1)}, u32[]{:S(2)}, u32[]{:S(2)}) collective-permute-start(bf16[8,4,16,256]{3,2,1,0:T(8,128)(2,1)S(1)} %get-tuple-element.33), channel_id=1, source_target_pairs={{0,8},{8,16},{16,24},{24,32},{32,40},{40,48},{48,56},{56,64},{64,7... | collective-permute-start | bytes 786440 | tf_op jit(solution)/shard_map/ppermute | solution.py:296
  52.5 1.9 %collective-permute-start.1 = (bf16[8,4,16,256]{3,2,1,0:T(8,128)(2,1)S(1)}, bf16[8,4,16,256]{3,2,1,0:T(8,128)(2,1)S(1)}, u32[]{:S(2)}, u32[]{:S(2)}) collective-permute-start(bf16[8,4,16,256]{3,2,1,0:T(8,128)(2,1)S(1)} %get-tuple-element.32), channel_id=1, source_target_pairs={{8,0},{16,8},{24,16},{32,24},{40,32},{48,40},{56,48},{64,56},{72,6... | collective-permute-start | bytes 786440 | tf_op jit(solution)/shard_map/ppermute | solution.py:296
  55.8 4.4 %collective-permute-done.1.hi_ref = bf16[8,4,16,256]{3,2,1,0:T(8,128)(2,1)S(1)} collective-permute-done((bf16[8,4,16,256]{3,2,1,0:T(8,128)(2,1)S(1)}, bf16[8,4,16,256]{3,2,1,0:T(8,128)(2,1)S(1)}, u32[]{:S(2)}, u32[]{:S(2)}) %collective-permute-start.1) | collective-permute-done | bytes 262176 | tf_op jit(solution)/shard_map/ppermute | solution.py:296
  60.9 4.0 %shard_map.87 = (f32[16,16,256]{2,1,0:T(8,128)}, bf16[16,16,256]{2,1,0:T(8,128)(2,1)}, bf16[4,16,256]{2,1,0:T(8,128)(2,1)}, bf16[4,16,256]{2,1,0:T(8,128)(2,1)}, bf16[8,96,128]{2,1,0:T(8,128)(2,1)}) custom-call(s32[16,9]{1,0:T(8,128)} %idx_ref.3, bf16[16,9,16,128]{3,2,1,0:T(8,128)(2,1)} %near_ref.3, bf16[8,4,16,256]{3,2,1,0:T(8,128)(2,1)} %copy-done.5, ...), custom_call_target="tpu_custom_call" | custom-call | flops 420000000 | bytes 4500000 | tf_op jit(solution)/shard_map/pallas_call | solution.py:282
  64.9 1.9 %collective-permute-start.4 = (bf16[4,16,256]{2,1,0:T(8,128)(2,1)}, bf16[4,16,256]{2,1,0:T(8,128)(2,1)S(1)}, u32[]{:S(2)}, u32[]{:S(2)}) collective-permute-start(bf16[4,16,256]{2,1,0:T(8,128)(2,1)} %get-tuple-element.27), channel_id=1, source_target_pairs={{0,8},{8,16},{16,24},{24,32},{32,40},{40,48},{48,56},{56,64},{64,7... | collective-permute-start | bytes 98312 | tf_op jit(solution)/shard_map/ppermute | solution.py:296
  66.9 2.4 %collective-permute-start.5 = (bf16[4,16,256]{2,1,0:T(8,128)(2,1)}, bf16[4,16,256]{2,1,0:T(8,128)(2,1)S(1)}, u32[]{:S(2)}, u32[]{:S(2)}) collective-permute-start(bf16[4,16,256]{2,1,0:T(8,128)(2,1)} %get-tuple-element.29), channel_id=1, source_target_pairs={{8,0},{16,8},{24,16},{32,24},{40,32},{48,40},{56,48},{64,56},{72,6... | collective-permute-start | bytes 98312 | tf_op jit(solution)/shard_map/ppermute | solution.py:296
  69.3 4.1 %collective-permute-done.5.hi_ref = bf16[4,16,256]{2,1,0:T(8,128)(2,1)S(1)} collective-permute-done((bf16[4,16,256]{2,1,0:T(8,128)(2,1)}, bf16[4,16,256]{2,1,0:T(8,128)(2,1)S(1)}, u32[]{:S(2)}, u32[]{:S(2)}) %collective-permute-start.5) | collective-permute-done | bytes 32800 | tf_op jit(solution)/shard_map/ppermute | solution.py:296
  77.2 23.6 %all_to_all.26 = bf16[32,32,128]{2,1,0:T(8,128)(2,1)S(1)} all-to-all(bf16[32,32,128]{2,1,0:T(8,128)(2,1)} %shard_map.88), channel_id=1, replica_groups=mesh['x'=4,'z'=8,'core'=2,'y'=8] {'x','z'}, dimensions={0} | all-to-all | bytes 524288 | tf_op jit(solution)/shard_map/all_to_all | solution.py:300
  100.8 3.4 %all-to-all-start.2 = ((bf16[8,96,128]{2,1,0:T(8,128)(2,1)}), bf16[8,96,128]{2,1,0:T(8,128)(2,1)S(1)}, u32[]{:S(2)}, u32[]{:S(2)}) async-start(bf16[8,96,128]{2,1,0:T(8,128)(2,1)} %get-tuple-element.23), calls=%async_computation.2 | async-start | bytes 393216 | tf_op jit(solution)/shard_map/all_to_all | solution.py:300
  104.2 3.6 %all-gather = bf16[64,32,128]{2,1,0:T(8,128)(2,1)} all-gather(bf16[32,32,128]{2,1,0:T(8,128)(2,1)S(1)} %all_to_all.26), channel_id=2, replica_groups=mesh['x'=4,'z'=8,'core'=2,'y'=8] {'core'}, dimensions={0}, use_global_device_ids=true | all-gather | bytes 786432 | tf_op jit(solution)/shard_map/all_gather | solution.py:357
  107.8 2.0 %shard_map.89.cpl_ref = bf16[2,128,864]{2,1,0:T(8,128)(2,1)} custom-call(bf16[8,16,16,256]{3,2,1,0:T(8,128)(2,1)} %bitcast.5), custom_call_target="tpu_custom_call" | custom-call | bytes 1000000 | tf_op jit(solution)/shard_map/pallas_call | solution.py:282
  109.8 6.3 %all-to-all-done.2.recv_ref = bf16[8,96,128]{2,1,0:T(8,128)(2,1)S(1)} async-done(((bf16[8,96,128]{2,1,0:T(8,128)(2,1)}), bf16[8,96,128]{2,1,0:T(8,128)(2,1)S(1)}, u32[]{:S(2)}, u32[]{:S(2)}) %all-to-all-start.2) | async-done | bytes 196640 | tf_op jit(solution)/shard_map/all_to_all | solution.py:300
  116.8 3.8 %shard_map.90 = (bf16[32,32,128]{2,1,0:T(8,128)(2,1)}, bf16[9,16,256]{2,1,0:T(8,128)(2,1)}, bf16[9,16,256]{2,1,0:T(8,128)(2,1)}) custom-call(s32[2,27]{1,0:T(2,128)} %far_ref.3, bf16[2,32,32,128]{3,2,1,0:T(8,128)(2,1)} %bitcast.9, bf16[2,128,864]{2,1,0:T(8,128)(2,1)} %shard_map.89.cpl_ref, bf16[8,96,128]{2,1,0:T(8,128)(2,1)} %copy-done.2, ...), custom_call_target="tpu_custom_call" | custom-call | flops 100000000 | bytes 1700000 | tf_op jit(solution)/shard_map/pallas_call | solution.py:282
  120.6 6.3 %all-to-all-start.3 = ((bf16[32,32,128]{2,1,0:T(8,128)(2,1)}), bf16[32,32,128]{2,1,0:T(8,128)(2,1)S(1)}, u32[]{:S(2)}, u32[]{:S(2)}) async-start(bf16[32,32,128]{2,1,0:T(8,128)(2,1)} %get-tuple-element.24), calls=%async_computation.3 | async-start | bytes 524288 | tf_op jit(solution)/shard_map/all_to_all | solution.py:300
  126.9 5.0 %collective-permute-start.2 = (bf16[9,16,256]{2,1,0:T(8,128)(2,1)}, bf16[9,16,256]{2,1,0:T(8,128)(2,1)S(1)}, u32[]{:S(2)}, u32[]{:S(2)}) collective-permute-start(bf16[9,16,256]{2,1,0:T(8,128)(2,1)} %get-tuple-element.26), channel_id=1, source_target_pairs={{0,8},{8,16},{16,24},{24,32},{32,40},{40,48},{48,56},{56,64},{64,7... | collective-permute-start | bytes 221192 | tf_op jit(solution)/shard_map/ppermute | solution.py:296
  133.8 2.8 %all-to-all-done.3 = bf16[32,32,128]{2,1,0:T(8,128)(2,1)S(1)} async-done(((bf16[32,32,128]{2,1,0:T(8,128)(2,1)}), bf16[32,32,128]{2,1,0:T(8,128)(2,1)S(1)}, u32[]{:S(2)}, u32[]{:S(2)}) %all-to-all-start.3) | async-done | bytes 262176 | tf_op jit(solution)/shard_map/all_to_all | solution.py:300
  136.6 5.8 %all-gather.2 = bf16[64,32,128]{2,1,0:T(8,128)(2,1)} all-gather(bf16[32,32,128]{2,1,0:T(8,128)(2,1)S(1)} %all-to-all-done.3), channel_id=4, replica_groups=mesh['x'=4,'z'=8,'core'=2,'y'=8] {'core'}, dimensions={0}, use_global_device_ids=true | all-gather | bytes 786432 | tf_op jit(solution)/shard_map/all_gather | solution.py:373
  143.1 3.3 %shard_map.91 = bf16[8,128,128]{2,1,0:T(8,128)(2,1)} custom-call(s32[2,27]{1,0:T(2,128)} %far_ref.3, bf16[2,32,32,128]{3,2,1,0:T(8,128)(2,1)} %bitcast.8, bf16[2,128,864]{2,1,0:T(8,128)(2,1)} %shard_map.89.cpl_ref, bf16[9,16,256]{2,1,0:T(8,128)(2,1)} %get-tuple-element.25.own_ref, bf16[9,16,256]{2,1,0:T(8,128)(2,1)} %copy-done.3, bf16[9,16,256]{2,1,0:T(8,128)(2,1)} %copy-done.4), custom_call_target="tpu_custom_call" | custom-call | flops 100000000 | bytes 1300000 | tf_op jit(solution)/shard_map/pallas_call | solution.py:282
  146.4 3.4 %all-to-all-start.4 = ((bf16[8,128,128]{2,1,0:T(8,128)(2,1)}), bf16[8,128,128]{2,1,0:T(8,128)(2,1)S(1)}, u32[]{:S(2)}, u32[]{:S(2)}) async-start(bf16[8,128,128]{2,1,0:T(8,128)(2,1)} %shard_map.91), calls=%async_computation.4 | async-start | bytes 524288 | tf_op jit(solution)/shard_map/all_to_all | solution.py:300
  149.9 4.3 %shard_map.93 = (f32[256,256]{1,0:T(8,128)}, bf16[256,256]{1,0:T(8,128)(2,1)}) custom-call(s32[16,9]{1,0:T(8,128)} %idx_ref.3, bf16[16,9,16,128]{3,2,1,0:T(8,128)(2,1)} %near_ref.3, bf16[8,24,16,256]{3,2,1,0:T(8,128)(2,1)} %bitcast.10, bf16[9,16,256]{2,1,0:T(8,128)(2,1)} %copy-done.3, bf16[8,16,16,256]{3,2,1,0:T(8,128)(2,1)} %bitcast.7, ...), custom_call_target="tpu_custom_call" | custom-call | flops 520000000 | bytes 4000000 | tf_op jit(solution)/shard_map/pallas_call | solution.py:282
  154.2 7.9 %all-to-all-done.4.recv_ref = bf16[8,128,128]{2,1,0:T(8,128)(2,1)S(1)} async-done(((bf16[8,128,128]{2,1,0:T(8,128)(2,1)}), bf16[8,128,128]{2,1,0:T(8,128)(2,1)S(1)}, u32[]{:S(2)}, u32[]{:S(2)}) %all-to-all-start.4) | async-done | bytes 262176 | tf_op jit(solution)/shard_map/all_to_all | solution.py:300
  162.8 3.2 %shard_map.94 = (bf16[16,16,256]{2,1,0:T(8,128)(2,1)}, bf16[16,16,256]{2,1,0:T(8,128)(2,1)}) custom-call(f32[16,16,256]{2,1,0:T(8,128)} %get-tuple-element.21.keep_ref, bf16[2,128,64]{2,1,0:T(8,128)(2,1)} %get-tuple-element.20.u_ref, bf16[8,128,128]{2,1,0:T(8,128)(2,1)} %copy-done.1, f32[256,256]{1,0:T(8,128)} %get-tuple-element.30.near_ref, ...), custom_call_target="tpu_custom_call" | custom-call | flops 100000000 | bytes 2000000 | tf_op jit(solution)/shard_map/pallas_call | solution.py:282
  (32 shorter events, 10.0 us)
Async XLA Ops:
  7.2 100.6 %all-gather.7.cloned.1.call-start = ((), (), s32[]{:S(2)}) async-start(), calls=%async_computation.5 | async-start | bytes 1179648 | tf_op jit(solution)/shard_map/all_gather | solution.py:320
  44.4 15.8 %copy-start = (bf16[8,17,16,256]{3,2,1,0:T(8,128)(2,1)}, bf16[8,17,16,256]{3,2,1,0:T(8,128)(2,1)S(1)}, u32[]{:S(2)}) copy-start(bf16[8,17,16,256]{3,2,1,0:T(8,128)(2,1)S(1)} %all_to_all.25.own_ref.recv_ref) | copy-start | bytes 3342340
  44.4 105.5 %all-gather.9.cloned.1.call-start = ((), (), s32[]{:S(2)}) async-start(), calls=%async_computation.6 | async-start | bytes 1769472 | tf_op jit(solution)/shard_map/all_gather | solution.py:346
  44.5 11.3 %collective-permute-start = (bf16[8,4,16,256]{3,2,1,0:T(8,128)(2,1)S(1)}, bf16[8,4,16,256]{3,2,1,0:T(8,128)(2,1)S(1)}, u32[]{:S(2)}, u32[]{:S(2)}) collective-permute-start(bf16[8,4,16,256]{3,2,1,0:T(8,128)(2,1)S(1)} %get-tuple-element.33), channel_id=1, source_target_pairs={{0,8},{8,16},{16,24},{24,32},{32,40},{40,48},{48,56},{56,64},{64,7... | collective-permute-start | bytes 786440 | tf_op jit(solution)/shard_map/ppermute | solution.py:296
  52.5 7.7 %collective-permute-start.1 = (bf16[8,4,16,256]{3,2,1,0:T(8,128)(2,1)S(1)}, bf16[8,4,16,256]{3,2,1,0:T(8,128)(2,1)S(1)}, u32[]{:S(2)}, u32[]{:S(2)}) collective-permute-start(bf16[8,4,16,256]{3,2,1,0:T(8,128)(2,1)S(1)} %get-tuple-element.32), channel_id=1, source_target_pairs={{8,0},{16,8},{24,16},{32,24},{40,32},{48,40},{56,48},{64,56},{72,6... | collective-permute-start | bytes 786440 | tf_op jit(solution)/shard_map/ppermute | solution.py:296
  55.8 4.4 %copy-start.5 = (bf16[8,4,16,256]{3,2,1,0:T(8,128)(2,1)}, bf16[8,4,16,256]{3,2,1,0:T(8,128)(2,1)S(1)}, u32[]{:S(2)}) copy-start(bf16[8,4,16,256]{3,2,1,0:T(8,128)(2,1)S(1)} %collective-permute-done.lo_ref) | copy-start | bytes 786436
  60.2 0.7 copy-start.6
  64.9 4.3 %collective-permute-start.4 = (bf16[4,16,256]{2,1,0:T(8,128)(2,1)}, bf16[4,16,256]{2,1,0:T(8,128)(2,1)S(1)}, u32[]{:S(2)}, u32[]{:S(2)}) collective-permute-start(bf16[4,16,256]{2,1,0:T(8,128)(2,1)} %get-tuple-element.27), channel_id=1, source_target_pairs={{0,8},{8,16},{16,24},{24,32},{32,40},{40,48},{48,56},{56,64},{64,7... | collective-permute-start | bytes 98312 | tf_op jit(solution)/shard_map/ppermute | solution.py:296
  66.9 6.6 %collective-permute-start.5 = (bf16[4,16,256]{2,1,0:T(8,128)(2,1)}, bf16[4,16,256]{2,1,0:T(8,128)(2,1)S(1)}, u32[]{:S(2)}, u32[]{:S(2)}) collective-permute-start(bf16[4,16,256]{2,1,0:T(8,128)(2,1)} %get-tuple-element.29), channel_id=1, source_target_pairs={{8,0},{16,8},{24,16},{32,24},{40,32},{48,40},{56,48},{64,56},{72,6... | collective-permute-start | bytes 98312 | tf_op jit(solution)/shard_map/ppermute | solution.py:296
  69.3 4.1 %copy-start.7 = (bf16[4,16,256]{2,1,0:T(8,128)(2,1)}, bf16[4,16,256]{2,1,0:T(8,128)(2,1)S(1)}, u32[]{:S(2)}) copy-start(bf16[4,16,256]{2,1,0:T(8,128)(2,1)S(1)} %collective-permute-done.4.lo_ref) | copy-start | bytes 98308
  73.4 0.6 copy-start.8
  100.8 15.3 %all-to-all-start.2 = ((bf16[8,96,128]{2,1,0:T(8,128)(2,1)}), bf16[8,96,128]{2,1,0:T(8,128)(2,1)S(1)}, u32[]{:S(2)}, u32[]{:S(2)}) async-start(bf16[8,96,128]{2,1,0:T(8,128)(2,1)} %get-tuple-element.23), calls=%async_computation.2 | async-start | bytes 393216 | tf_op jit(solution)/shard_map/all_to_all | solution.py:300
  116.1 0.7 copy-start.2
  120.6 16.0 %all-to-all-start.3 = ((bf16[32,32,128]{2,1,0:T(8,128)(2,1)}), bf16[32,32,128]{2,1,0:T(8,128)(2,1)S(1)}, u32[]{:S(2)}, u32[]{:S(2)}) async-start(bf16[32,32,128]{2,1,0:T(8,128)(2,1)} %get-tuple-element.24), calls=%async_computation.3 | async-start | bytes 524288 | tf_op jit(solution)/shard_map/all_to_all | solution.py:300
  126.9 15.5 %collective-permute-start.2 = (bf16[9,16,256]{2,1,0:T(8,128)(2,1)}, bf16[9,16,256]{2,1,0:T(8,128)(2,1)S(1)}, u32[]{:S(2)}, u32[]{:S(2)}) collective-permute-start(bf16[9,16,256]{2,1,0:T(8,128)(2,1)} %get-tuple-element.26), channel_id=1, source_target_pairs={{0,8},{8,16},{16,24},{24,32},{32,40},{40,48},{48,56},{56,64},{64,7... | collective-permute-start | bytes 221192 | tf_op jit(solution)/shard_map/ppermute | solution.py:296
  131.9 10.5 %collective-permute-start.3 = (bf16[9,16,256]{2,1,0:T(8,128)(2,1)}, bf16[9,16,256]{2,1,0:T(8,128)(2,1)S(1)}, u32[]{:S(2)}, u32[]{:S(2)}) collective-permute-start(bf16[9,16,256]{2,1,0:T(8,128)(2,1)} %get-tuple-element.25.own_ref), channel_id=1, source_target_pairs={{8,0},{16,8},{24,16},{32,24},{40,32},{48,40},{56,48},{64,56},{72,6... | collective-permute-start | bytes 221192 | tf_op jit(solution)/shard_map/ppermute | solution.py:296
  142.4 0.6 copy-start.3
  142.4 0.7 copy-start.4
  146.4 15.7 %all-to-all-start.4 = ((bf16[8,128,128]{2,1,0:T(8,128)(2,1)}), bf16[8,128,128]{2,1,0:T(8,128)(2,1)S(1)}, u32[]{:S(2)}, u32[]{:S(2)}) async-start(bf16[8,128,128]{2,1,0:T(8,128)(2,1)} %shard_map.91), calls=%async_computation.4 | async-start | bytes 524288 | tf_op jit(solution)/shard_map/all_to_all | solution.py:300
  162.1 0.7 copy-start.1
Sparse Core Ops, SparseCore 0:
  44.6 38.7 all-gather.6
  85.4 44.1 all-gather.8

commit v6 on v2

--- a/solution.py
+++ b/solution.py
@@ -1,3 +1,5 @@
+import functools
+
 import jax
 import jax.numpy as jnp
 from jax import lax
@@ -26,6 +28,7 @@
 CPL0 = BAS0 + LEAVES // 2 * ROWS
 HELD = CPL0 + FAR_K * 8
 HALF = FAR_K * 32
+FLIGHT = 4
 CLUS = ("x", "z", "core")
 TOP = (((0,), (0,)), ((), ()))
 ANY = pl.BlockSpec(memory_space=pl.ANY)
@@ -110,28 +113,24 @@
     return dot(u, jnp.concatenate(blocks, axis=0).astype(BF))
 
 
-def near_copies(w_ref, near_scr, sems):
+def near_copies(w_ref, near_scr, sems, leaves):
     size = NEAR_K * ROWS
     return [
-        pltpu.make_async_copy(w_ref.at[:, pl.ds(size * i, size), :], near_scr.at[i], sems.at[i])
-        for i in range(LEAVES)
+        pltpu.make_async_copy(w_ref.at[:, pl.ds(size * i, size), :], near_scr.at[n], sems.at[n])
+        for n, i in enumerate(leaves)
     ]
 
 
-def unpack(tiles, v_scr):
+def unpack(start, tiles, v_scr):
     for n, tile in enumerate(tiles):
         for l in range(PACK):
-            v_scr[PACK * n + l] = tile[:, COLS * l : COLS * (l + 1)]
-
-
-def near_field(g, idx_ref, copies, near_scr, v_scr):
-    cols = []
-    for i in range(PACK * g, PACK * (g + 1)):
-        copies[i].wait()
-        parts = [near_scr[i, :, ROWS * k : ROWS * (k + 1), :].reshape(PANEL, PANEL) for k in range(NEAR_K)]
-        rhs = jnp.concatenate([v_scr[idx_ref[i, k]] for k in range(NEAR_K)], axis=0)
-        cols.append(dot(jnp.concatenate(parts, axis=1), rhs))
-    return jnp.concatenate(cols, axis=1)
+            v_scr[PACK * (start + n) + l] = tile[:, COLS * l : COLS * (l + 1)]
+
+
+def near_leaf(i, n, idx_ref, near_scr, v_scr):
+    parts = [near_scr[n, :, ROWS * k : ROWS * (k + 1), :].reshape(PANEL, PANEL) for k in range(NEAR_K)]
+    rhs = jnp.concatenate([v_scr[idx_ref[i, k]] for k in range(NEAR_K)], axis=0)
+    return dot(jnp.concatenate(parts, axis=1), rhs)
 
 
 def first_kernel(
@@ -141,12 +140,12 @@
 ):
     own = pltpu.make_async_copy(w_ref.at[:, pl.ds(BAS0, HELD - BAS0), :], own_scr, own_sem)
     own.start()
-    copies = near_copies(w_ref, near_scr, sems)
+    tiles = [lo_ref[...]] + [recv_ref[:, ROWS * g : ROWS * (g + 1), :] for g in range(GROUPS)] + [hi_ref[...]]
+    unpack(0, [tile.reshape(PANEL, 128) for tile in tiles], v_scr)
+    own.wait()
+    copies = near_copies(w_ref, near_scr, sems, range(LEAVES))
     for copy in copies:
         copy.start()
-    tiles = [lo_ref[...]] + [recv_ref[:, ROWS * g : ROWS * (g + 1), :] for g in range(GROUPS)] + [hi_ref[...]]
-    unpack([tile.reshape(PANEL, 128) for tile in tiles], v_scr)
-    own.wait()
     for y in range(SHARES):
         rows = own_scr[y, CPL0 - BAS0 :, :].astype(F32).reshape(FAR_K, 8, 128)
         c_scr[:, 8 * y : 8 * y + 8, :] = rows
@@ -165,7 +164,11 @@
     parents = [jnp.zeros((RANK, 128), F32), jnp.zeros((RANK, 128), F32)]
     for g in range(GROUPS):
         u = u_ref[g]
-        res = (near_field(g, idx_ref, copies, near_scr, v_scr) + far_field(u, coef[g // 2])).astype(BF)
+        cols = []
+        for i in range(PACK * g, PACK * (g + 1)):
+            copies[i].wait()
+            cols.append(near_leaf(i, i, idx_ref, near_scr, v_scr))
+        res = (jnp.concatenate(cols, axis=1) + far_field(u, coef[g // 2])).astype(BF)
         tile = res.reshape(SHARES, ROWS, 128)
         out_ref[:, g] = tile
         if g == 0:
@@ -179,20 +182,32 @@
     par_ref[...] = jnp.broadcast_to(packed[None], par_ref.shape)
 
 
-def near_kernel(idx_ref, w_ref, vec_ref, lo_ref, hi_ref, out_ref, near_scr, v_scr, sems):
-    copies = near_copies(w_ref, near_scr, sems)
-    for copy in copies:
+def near_kernel(groups, idx_ref, w_ref, *refs):
+    *tile_refs, out_ref, near_scr, v_scr, sems = refs
+    leaves = [i for g in groups for i in range(PACK * g, PACK * (g + 1))]
+    copies = near_copies(w_ref, near_scr, sems, leaves)
+    for copy in copies[:FLIGHT]:
         copy.start()
-    tiles = [lo_ref[...]] + [vec_ref[:, g] for g in range(GROUPS)] + [hi_ref[...]]
-    unpack([tile.reshape(PANEL, 128) for tile in tiles], v_scr)
-    for g in range(GROUPS):
-        out_ref[g] = near_field(g, idx_ref, copies, near_scr, v_scr)
-
-
-def last_kernel(far_ref, pc_ref, cpl_ref, u_ref, near_ref, own_ref, out_ref, rhs_scr):
+    tiles = [tile_refs[0][:, g] for g in range(GROUPS)]
+    unpack(1, [tile.reshape(PANEL, 128) for tile in tiles], v_scr)
+    if len(tile_refs) > 1:
+        unpack(0, [tile_refs[1][...].reshape(PANEL, 128)], v_scr)
+        unpack(GROUPS + 1, [tile_refs[2][...].reshape(PANEL, 128)], v_scr)
+    cols = []
+    for n, i in enumerate(leaves):
+        copies[n].wait()
+        if n + FLIGHT < len(leaves):
+            copies[n + FLIGHT].start()
+        cols.append(near_leaf(i, n, idx_ref, near_scr, v_scr))
+    for n in range(len(groups)):
+        out_ref[n] = jnp.concatenate(cols[PACK * n : PACK * (n + 1)], axis=1)
+
+
+def last_kernel(far_ref, pc_ref, cpl_ref, u_ref, mid_ref, edge_ref, own_ref, out_ref, rhs_scr):
     coef = far_sums(far_ref, pc_ref, (cpl_ref[0], cpl_ref[1]), rhs_scr)
     for g in range(GROUPS):
-        res = (near_ref[g] + far_field(u_ref[g], coef[g // 2])).astype(BF)
+        near = mid_ref[g - 1] if 0 < g < GROUPS - 1 else edge_ref[g // (GROUPS - 1)]
+        res = (near + far_field(u_ref[g], coef[g // 2])).astype(BF)
         out_ref[:, 0, g] = own_ref[:, g]
         out_ref[:, 1, g] = res.reshape(SHARES, ROWS, 128)
 
@@ -211,7 +226,7 @@
     return jax.ShapeDtypeStruct(shape, dtype)
 
 
-def call(kernel, name, outs, ins, scratch, flops, nbytes, *operands):
+def call(kernel, outs, ins, scratch, flops, nbytes, *operands):
     single = not isinstance(outs, tuple)
     return pl.pallas_call(
         kernel,
@@ -220,13 +235,11 @@
         out_specs=VMEM if single else (VMEM,) * len(outs),
         scratch_shapes=scratch,
         cost_estimate=pl.CostEstimate(flops=flops, bytes_accessed=nbytes, transcendentals=0),
-        name=name,
     )(*operands)
 
 
-def gather_parents(packed):
-    plane = lax.all_to_all(packed, ("x", "z"), 0, 0)
-    return lax.all_gather(plane, "core", axis=0)
+def exchange(values):
+    return lax.all_to_all(values, ("x", "z"), 0, 0)
 
 
 def halo(bottom, top):
@@ -236,7 +249,7 @@
     return lax.ppermute(top, CLUS, forward), lax.ppermute(bottom, CLUS, backward)
 
 
-def body(density, near_list, far_list, near_blocks, basis, transfer, coupling):
+def operator_twice(density, near_list, far_list, near_blocks, basis, transfer, coupling):
     share = array(SHARES, ROWS, 128)
     spread_out = array(PLANE, 32, 128)
     near_scratch = pltpu.VMEM((LEAVES, SHARES, NEAR_K * ROWS, PANEL), BF)
@@ -245,24 +258,24 @@
     near_sems = pltpu.SemaphoreType.DMA((LEAVES,))
 
     mine = call(
-        stack_kernel, "stack", array(HELD, PANEL), [VMEM] * 3, [], 0, 1_400_000,
+        stack_kernel, array(HELD, PANEL), [VMEM] * 3, [], 0, 1_400_000,
         near_blocks, basis, jnp.swapaxes(coupling, 2, 3),
     )
     held = lax.all_gather(mine, "y", axis=0)
     near_idx = near_list - (lax.axis_index(CLUS) * LEAVES - NWIN)
     near_idx = jnp.clip(near_idx, 0, LEAVES + 2 * NWIN - 1)
     sent = call(
-        prepare_kernel, "prepare", array(SHARES, SENT, 128), [VMEM] * 3, [], 40_000_000, 500_000,
+        prepare_kernel, array(SHARES, SENT, 128), [VMEM] * 3, [], 40_000_000, 500_000,
         density, basis, transfer,
     )
     recv = lax.all_to_all(sent, "y", 0, 0)
     parents, bottom, top = call(
-        parent_kernel, "parents", (spread_out, share, share), [VMEM], [], 100_000, 500_000, recv
-    )
-    every = gather_parents(parents)
+        parent_kernel, (spread_out, share, share), [VMEM], [], 100_000, 500_000, recv
+    )
+    every = lax.all_gather(exchange(parents), "core", axis=0)
     low, high = halo(bottom, top)
     first, parents, bottom, top, cpl, u = call(
-        first_kernel, "first",
+        first_kernel,
         (
             array(SHARES, GROUPS, ROWS, 128), spread_out, share, share,
             array(2, 2 * RANK, HALF), array(GROUPS, PANEL, PACK * RANK),
@@ -280,23 +293,32 @@
         400_000_000, 8_000_000,
         far_list, near_idx, every, held, transfer, recv, low, high,
     )
-    plane = lax.all_to_all(parents, ("x", "z"), 0, 0)
+    plane = exchange(parents)
     low, high = halo(bottom, top)
-    near = call(
-        near_kernel, "near", array(GROUPS, PANEL, 128, dtype=F32), [SMEM, ANY] + [VMEM] * 3,
-        [near_scratch, vec_scratch, near_sems], 300_000_000, 6_000_000,
+    half = array(GROUPS // 2, PANEL, 128, dtype=F32)
+    half_scratch = [
+        pltpu.VMEM((LEAVES // 2, SHARES, NEAR_K * ROWS, PANEL), BF),
+        vec_scratch,
+        pltpu.SemaphoreType.DMA((LEAVES // 2,)),
+    ]
+    mid = call(
+        functools.partial(near_kernel, (1, 2)), half, [SMEM, ANY, VMEM],
+        half_scratch, 150_000_000, 3_000_000,
+        near_idx, held, first,
+    )
+    edge = call(
+        functools.partial(near_kernel, (0, 3)), half, [SMEM, ANY] + [VMEM] * 3,
+        half_scratch, 150_000_000, 3_000_000,
         near_idx, held, first, low, high,
     )
     every = lax.all_gather(plane, "core", axis=0)
     sent = call(
-        last_kernel, "last", array(SHARES, 2, GROUPS, ROWS, 128), [SMEM] + [VMEM] * 5,
+        last_kernel, array(SHARES, 2, GROUPS, ROWS, 128), [SMEM] + [VMEM] * 6,
         [rhs_scratch], 100_000_000, 2_000_000,
-        far_list, every, cpl, u, near, first,
+        far_list, every, cpl, u, mid, edge, first,
     )
     out = array(LEAVES, ROWS, 256)
-    return call(
-        finish_kernel, "finish", (out, out), [VMEM], [], 0, 600_000, lax.all_to_all(sent, "y", 0, 0)
-    )
+    return call(finish_kernel, (out, out), [VMEM], [], 0, 600_000, lax.all_to_all(sent, "y", 0, 0))
 
 
 def solution(mesh):
@@ -311,7 +333,7 @@
         P(CLUS, None, None, "y"),
     )
     return jax.shard_map(
-        body,
+        operator_twice,
         mesh=fine,
         in_specs=placed,
         out_specs=(P(CLUS, "y", None), P(CLUS, "y", None)),

time: 154 us -> 154 us (level)
  waiting for transfers between devices: 29.3 us -> 25.5 us
  Pallas kernels: 28.6 us -> 30.5 us
    ppermute x2, waiting for transfers between devices: 3.79 us -> 0.01 us  [halo(): lax.ppermute(bottom, CLUS, backward)]
    pallas_call x7 -> x8, Pallas kernels: 28.6 us -> 30.5 us  [call(): pl.pallas_call(kernel, out_shape=outs, in_specs=ins, out_specs=VMEM if si...]
  transfers between devices with their start and end apart: 7 -> 7, of which waited for: 3 -> 2; matrix products, arithmetic and copies ran while one was open for 1% -> 1% of each run, Pallas kernels for 7% -> 9%
where the time goes in v6:
time: 154 us; the launch traced here: 152 us
  blocking collectives  41.3 us (27%)
  starting transfers between devices  37.7 us (24%)
  Pallas kernels  30.5 us (20%)
  waiting for transfers between devices  25.5 us (17%)
  between operations  14.2 us (9%)
    pallas_call x8, Pallas kernels, call(): pl.pallas_call(kernel, out_shape=outs, in_specs=ins, out_specs=VMEM if si...  30.5 us
    all_gather x1, waiting for transfers between devices, operator_twice(): held = lax.all_gather(mine, 'y', axis=0)  25.2 us
    all_to_all x2, starting transfers between devices, exchange(): return lax.all_to_all(values, ('x', 'z'), 0, 0)  23.6 us
    all_to_all x1, blocking collectives, operator_twice(): recv = lax.all_to_all(sent, 'y', 0, 0)  16.5 us
    all_to_all x1, blocking collectives, operator_twice(): lax.all_to_all(sent, 'y', 0, 0)  16.3 us
    ppermute x2, starting transfers between devices, halo(): lax.ppermute(top, CLUS, forward)  10.3 us
    all_gather x1, blocking collectives, operator_twice(): every = lax.all_gather(exchange(parents), 'core', axis=0)  6.18 us
    ppermute x2, starting transfers between devices, halo(): lax.ppermute(bottom, CLUS, backward)  3.84 us
  transfers between devices with their start and end apart: 7, of which 2 were waited for; matrix products, arithmetic and copies ran while one was open for 1% of the time, Pallas kernels for 9%

profile of v6, /device:TPU:1, one launch (start us, length us, event | category | flops | bytes accessed | tf_op | source)
XLA Modules:
  0.0 151.7 jit_solution(15248000779619064655)
XLA Ops:
  7.2 0.0 all-gather.5.cloned.1.call-start
  7.2 2.1 %shard_map.88 = bf16[2648,128]{1,0:T(8,128)(2,1)} custom-call(bf16[16,9,16,128]{3,2,1,0:T(8,128)(2,1)} %near_ref.1, bf16[16,16,64]{2,1,0:T(8,128)(2,1)} %b_ref.3, bf16[2,27,8,64]{3,2,1,0:T(8,128)(2,1)} %bitcast.9), custom_call_target="tpu_custom_call" | custom-call | bytes 1400000 | tf_op jit(solution)/shard_map/pallas_call | solution.py:231
  9.3 2.4 %shard_map.86 = bf16[8,96,128]{2,1,0:T(8,128)(2,1)} custom-call(bf16[16,16,256]{2,1,0:T(8,128)(2,1)} %d_ref.1, bf16[16,16,64]{2,1,0:T(8,128)(2,1)} %b_ref.3, bf16[16,64,64]{2,1,0:T(8,128)(2,1)} %t_ref.3), custom_call_target="tpu_custom_call" | custom-call | flops 40000000 | bytes 500000 | tf_op jit(solution)/shard_map/pallas_call | solution.py:231
  11.7 16.5 %all_to_all.20.recv_ref = bf16[8,96,128]{2,1,0:T(8,128)(2,1)} all-to-all(bf16[8,96,128]{2,1,0:T(8,128)(2,1)} %shard_map.86), channel_id=1, replica_groups=mesh['x'=4,'z'=8,'core'=2,'y'=8] {'y'}, dimensions={0} | all-to-all | bytes 393216 | tf_op jit(solution)/shard_map/all_to_all | solution.py:271
  28.1 1.6 %shard_map.87 = (bf16[32,32,128]{2,1,0:T(8,128)(2,1)}, bf16[8,16,128]{2,1,0:T(8,128)(2,1)}, bf16[8,16,128]{2,1,0:T(8,128)(2,1)}) custom-call(bf16[8,96,128]{2,1,0:T(8,128)(2,1)} %all_to_all.20.recv_ref), custom_call_target="tpu_custom_call" | custom-call | flops 100000 | bytes 500000 | tf_op jit(solution)/shard_map/pallas_call | solution.py:231
  29.8 13.2 %all-to-all-start.1 = ((bf16[32,32,128]{2,1,0:T(8,128)(2,1)}), bf16[32,32,128]{2,1,0:T(8,128)(2,1)S(1)}, u32[]{:S(2)}, u32[]{:S(2)}) async-start(bf16[32,32,128]{2,1,0:T(8,128)(2,1)} %get-tuple-element.11), calls=%async_computation.1 | async-start | bytes 524288 | tf_op jit(solution)/shard_map/all_to_all | solution.py:242
  43.0 1.3 subtract_clamp_fusion.idx_ref
  44.3 6.1 %collective-permute-start = (bf16[8,16,128]{2,1,0:T(8,128)(2,1)}, bf16[8,16,128]{2,1,0:T(8,128)(2,1)S(1)}, u32[]{:S(2)}, u32[]{:S(2)}) collective-permute-start(bf16[8,16,128]{2,1,0:T(8,128)(2,1)} %get-tuple-element.12), channel_id=1, source_target_pairs={{0,8},{8,16},{16,24},{24,32},{32,40},{40,48},{48,56},{56,64},{64,7... | collective-permute-start | bytes 98312 | tf_op jit(solution)/shard_map/ppermute | solution.py:249
  50.4 1.9 %collective-permute-start.1 = (bf16[8,16,128]{2,1,0:T(8,128)(2,1)}, bf16[8,16,128]{2,1,0:T(8,128)(2,1)S(1)}, u32[]{:S(2)}, u32[]{:S(2)}) collective-permute-start(bf16[8,16,128]{2,1,0:T(8,128)(2,1)} %get-tuple-element.13), channel_id=1, source_target_pairs={{8,0},{16,8},{24,16},{32,24},{40,32},{48,40},{56,48},{64,56},{72,6... | collective-permute-start | bytes 98312 | tf_op jit(solution)/shard_map/ppermute | solution.py:249
  52.3 0.3 all-to-all-done.1
  52.6 6.2 %all-gather = bf16[64,32,128]{2,1,0:T(8,128)(2,1)} all-gather(bf16[32,32,128]{2,1,0:T(8,128)(2,1)S(1)} %all-to-all-done.1), channel_id=2, replica_groups=mesh['x'=4,'z'=8,'core'=2,'y'=8] {'core'}, dimensions={0}, use_global_device_ids=true | all-gather | bytes 786432 | tf_op jit(solution)/shard_map/all_gather | solution.py:275
  58.8 25.2 %all-gather.5.cloned.1.call-done = bf16[21184,128]{1,0:T(8,128)(2,1)} async-done(((bf16[2648,128]{1,0:T(8,128)(2,1)}), bf16[21184,128]{1,0:T(8,128)(2,1)}) %all-gather.5.cloned.1.call-update) | async-done | bytes 5423120 | tf_op jit(solution)/shard_map/all_gather | solution.py:264
  84.0 9.8 %shard_map.89 = (bf16[8,4,16,128]{3,2,1,0:T(8,128)(2,1)}, bf16[32,32,128]{2,1,0:T(8,128)(2,1)}, bf16[8,16,128]{2,1,0:T(8,128)(2,1)}, bf16[8,16,128]{2,1,0:T(8,12...) custom-call(s32[2,27]{1,0:T(2,128)} %far_ref.3, s32[16,9]{1,0:T(8,128)} %subtract_clamp_fusion.idx_ref, ...), custom_call_target="tpu_custom_call" | custom-call | flops 400000000 | bytes 8000000 | tf_op jit(solution)/shard_map/pallas_call | solution.py:231
  93.8 10.4 %all-to-all-start.2 = ((bf16[32,32,128]{2,1,0:T(8,128)(2,1)}), bf16[32,32,128]{2,1,0:T(8,128)(2,1)S(1)}, u32[]{:S(2)}, u32[]{:S(2)}) async-start(bf16[32,32,128]{2,1,0:T(8,128)(2,1)} %get-tuple-element.14), calls=%async_computation.2 | async-start | bytes 524288 | tf_op jit(solution)/shard_map/all_to_all | solution.py:242
  104.3 4.2 %collective-permute-start.2 = (bf16[8,16,128]{2,1,0:T(8,128)(2,1)}, bf16[8,16,128]{2,1,0:T(8,128)(2,1)S(1)}, u32[]{:S(2)}, u32[]{:S(2)}) collective-permute-start(bf16[8,16,128]{2,1,0:T(8,128)(2,1)} %get-tuple-element.18), channel_id=1, source_target_pairs={{0,8},{8,16},{16,24},{24,32},{32,40},{40,48},{48,56},{56,64},{64,7... | collective-permute-start | bytes 98312 | tf_op jit(solution)/shard_map/ppermute | solution.py:249
  108.5 1.9 %collective-permute-start.3 = (bf16[8,16,128]{2,1,0:T(8,128)(2,1)}, bf16[8,16,128]{2,1,0:T(8,128)(2,1)S(1)}, u32[]{:S(2)}, u32[]{:S(2)}) collective-permute-start(bf16[8,16,128]{2,1,0:T(8,128)(2,1)} %get-tuple-element.19), channel_id=1, source_target_pairs={{8,0},{16,8},{24,16},{32,24},{40,32},{48,40},{56,48},{64,56},{72,6... | collective-permute-start | bytes 98312 | tf_op jit(solution)/shard_map/ppermute | solution.py:249
  110.4 4.7 %shard_map.90.mid_ref = f32[2,128,128]{2,1,0:T(8,128)} custom-call(s32[16,9]{1,0:T(8,128)} %subtract_clamp_fusion.idx_ref, bf16[8,2648,128]{2,1,0:T(8,128)(2,1)} %bitcast.5, bf16[8,4,16,128]{3,2,1,0:T(8,128)(2,1)} %get-tuple-element.17.refs_0_.own_ref), custom_call_target="tpu_custom_call" | custom-call | flops 150000000 | bytes 3000000 | tf_op jit(solution)/shard_map/pallas_call | solution.py:231
  115.1 0.6 copy-done.2
  115.7 0.6 copy-done.3
  116.3 4.7 %shard_map.91.edge_ref = f32[2,128,128]{2,1,0:T(8,128)} custom-call(s32[16,9]{1,0:T(8,128)} %subtract_clamp_fusion.idx_ref, bf16[8,2648,128]{2,1,0:T(8,128)(2,1)} %bitcast.6, bf16[8,4,16,128]{3,2,1,0:T(8,128)(2,1)} %get-tuple-element.17.refs_0_.own_ref, bf16[8,16,128]{2,1,0:T(8,128)(2,1)} %copy-done.2, bf16[8,16,128]{2,1,0:T(8,128)(2,1)} %copy-done.3), custom_call_target="tpu_custom_call" | custom-call | flops 150000000 | bytes 3000000 | tf_op jit(solution)/shard_map/pallas_call | solution.py:231
  121.0 2.3 %all-gather.2 = bf16[64,32,128]{2,1,0:T(8,128)(2,1)} all-gather(bf16[32,32,128]{2,1,0:T(8,128)(2,1)S(1)} %all-to-all-done.2), channel_id=4, replica_groups=mesh['x'=4,'z'=8,'core'=2,'y'=8] {'core'}, dimensions={0}, use_global_device_ids=true | all-gather | bytes 786432 | tf_op jit(solution)/shard_map/all_gather | solution.py:314
  123.3 3.3 %shard_map.92 = bf16[8,2,4,16,128]{4,3,2,1,0:T(8,128)(2,1)} custom-call(s32[2,27]{1,0:T(2,128)} %far_ref.3, bf16[2,32,32,128]{3,2,1,0:T(8,128)(2,1)} %bitcast.7, bf16[2,128,864]{2,1,0:T(8,128)(2,1)} %get-tuple-element.15.cpl_ref, bf16[4,128,256]{2,1,0:T(8,128)(2,1)} %get-tuple-element.16.u_ref, f32[2,128,128]{2,1,0:T(8,128)} %shard_map.90.mid_ref, ...), custom_call_target="tpu_custom_call" | custom-call | flops 100000000 | bytes 2000000 | tf_op jit(solution)/shard_map/pallas_call | solution.py:231
  126.6 16.3 %all_to_all.21.recv_ref = bf16[8,2,4,16,128]{4,3,2,1,0:T(8,128)(2,1)} all-to-all(bf16[8,2,4,16,128]{4,3,2,1,0:T(8,128)(2,1)} %shard_map.92), channel_id=1, replica_groups=mesh['x'=4,'z'=8,'core'=2,'y'=8] {'y'}, dimensions={0} | all-to-all | bytes 524288 | tf_op jit(solution)/shard_map/all_to_all | solution.py:321
  142.9 1.9 %shard_map.93 = (bf16[16,16,256]{2,1,0:T(8,128)(2,1)}, bf16[16,16,256]{2,1,0:T(8,128)(2,1)}) custom-call(bf16[8,2,4,16,128]{4,3,2,1,0:T(8,128)(2,1)} %all_to_all.21.recv_ref), custom_call_target="tpu_custom_call" | custom-call | bytes 600000 | tf_op jit(solution)/shard_map/pallas_call | solution.py:231
  (12 shorter events, 0.0 us)
Async XLA Ops:
  7.2 76.8 %all-gather.5.cloned.1.call-start = ((), (), s32[]{:S(2)}) async-start(), calls=%async_computation.4 | async-start | bytes 6100992 | tf_op jit(solution)/shard_map/all_gather | solution.py:264
  29.8 22.8 %all-to-all-start.1 = ((bf16[32,32,128]{2,1,0:T(8,128)(2,1)}), bf16[32,32,128]{2,1,0:T(8,128)(2,1)S(1)}, u32[]{:S(2)}, u32[]{:S(2)}) async-start(bf16[32,32,128]{2,1,0:T(8,128)(2,1)} %get-tuple-element.11), calls=%async_computation.1 | async-start | bytes 524288 | tf_op jit(solution)/shard_map/all_to_all | solution.py:242
  44.3 14.5 %collective-permute-start = (bf16[8,16,128]{2,1,0:T(8,128)(2,1)}, bf16[8,16,128]{2,1,0:T(8,128)(2,1)S(1)}, u32[]{:S(2)}, u32[]{:S(2)}) collective-permute-start(bf16[8,16,128]{2,1,0:T(8,128)(2,1)} %get-tuple-element.12), channel_id=1, source_target_pairs={{0,8},{8,16},{16,24},{24,32},{32,40},{40,48},{48,56},{56,64},{64,7... | collective-permute-start | bytes 98312 | tf_op jit(solution)/shard_map/ppermute | solution.py:249
  50.4 8.4 %collective-permute-start.1 = (bf16[8,16,128]{2,1,0:T(8,128)(2,1)}, bf16[8,16,128]{2,1,0:T(8,128)(2,1)S(1)}, u32[]{:S(2)}, u32[]{:S(2)}) collective-permute-start(bf16[8,16,128]{2,1,0:T(8,128)(2,1)} %get-tuple-element.13), channel_id=1, source_target_pairs={{8,0},{16,8},{24,16},{32,24},{40,32},{48,40},{56,48},{64,56},{72,6... | collective-permute-start | bytes 98312 | tf_op jit(solution)/shard_map/ppermute | solution.py:249
  58.8 25.2 %copy-start = (bf16[8,16,128]{2,1,0:T(8,128)(2,1)}, bf16[8,16,128]{2,1,0:T(8,128)(2,1)S(1)}, u32[]{:S(2)}) copy-start(bf16[8,16,128]{2,1,0:T(8,128)(2,1)S(1)} %collective-permute-done.lo_ref) | copy-start | bytes 98308
  58.8 25.2 %copy-start.1 = (bf16[8,16,128]{2,1,0:T(8,128)(2,1)}, bf16[8,16,128]{2,1,0:T(8,128)(2,1)S(1)}, u32[]{:S(2)}) copy-start(bf16[8,16,128]{2,1,0:T(8,128)(2,1)S(1)} %collective-permute-done.1.hi_ref) | copy-start | bytes 98308
  93.8 27.1 %all-to-all-start.2 = ((bf16[32,32,128]{2,1,0:T(8,128)(2,1)}), bf16[32,32,128]{2,1,0:T(8,128)(2,1)S(1)}, u32[]{:S(2)}, u32[]{:S(2)}) async-start(bf16[32,32,128]{2,1,0:T(8,128)(2,1)} %get-tuple-element.14), calls=%async_computation.2 | async-start | bytes 524288 | tf_op jit(solution)/shard_map/all_to_all | solution.py:242
  104.3 10.8 %collective-permute-start.2 = (bf16[8,16,128]{2,1,0:T(8,128)(2,1)}, bf16[8,16,128]{2,1,0:T(8,128)(2,1)S(1)}, u32[]{:S(2)}, u32[]{:S(2)}) collective-permute-start(bf16[8,16,128]{2,1,0:T(8,128)(2,1)} %get-tuple-element.18), channel_id=1, source_target_pairs={{0,8},{8,16},{16,24},{24,32},{32,40},{40,48},{48,56},{56,64},{64,7... | collective-permute-start | bytes 98312 | tf_op jit(solution)/shard_map/ppermute | solution.py:249
  108.5 6.6 %collective-permute-start.3 = (bf16[8,16,128]{2,1,0:T(8,128)(2,1)}, bf16[8,16,128]{2,1,0:T(8,128)(2,1)S(1)}, u32[]{:S(2)}, u32[]{:S(2)}) collective-permute-start(bf16[8,16,128]{2,1,0:T(8,128)(2,1)} %get-tuple-element.19), channel_id=1, source_target_pairs={{8,0},{16,8},{24,16},{32,24},{40,32},{48,40},{56,48},{64,56},{72,6... | collective-permute-start | bytes 98312 | tf_op jit(solution)/shard_map/ppermute | solution.py:249
  115.1 0.6 copy-start.2
  115.7 0.6 copy-start.3
Sparse Core Ops, SparseCore 0:
  10.1 73.8 all-gather.4

commit v7 on v2

--- a/solution.py
+++ b/solution.py
@@ -26,6 +26,7 @@
 CPL0 = BAS0 + LEAVES // 2 * ROWS
 HELD = CPL0 + FAR_K * 8
 HALF = FAR_K * 32
+BATCH = 8
 CLUS = ("x", "z", "core")
 TOP = (((0,), (0,)), ((), ()))
 ANY = pl.BlockSpec(memory_space=pl.ANY)
@@ -55,6 +56,13 @@
     low = jnp.where(group == 0, first[:32], first[32:])
     high = jnp.where(group == 2, second[:32], second[32:])
     return jnp.where(group < 2, low, high).astype(BF)
+
+
+def fetch(pairs, sems):
+    moves = [pltpu.make_async_copy(src, dst, sems.at[n]) for n, (src, dst) in enumerate(pairs)]
+    for move in moves:
+        move.start()
+    return moves
 
 
 def stack_kernel(near_ref, b_ref, c_ref, out_ref):
@@ -110,43 +118,49 @@
     return dot(u, jnp.concatenate(blocks, axis=0).astype(BF))
 
 
-def near_copies(w_ref, near_scr, sems):
+def near_copies(w_ref, near_scr, sems, leaves):
     size = NEAR_K * ROWS
     return [
-        pltpu.make_async_copy(w_ref.at[:, pl.ds(size * i, size), :], near_scr.at[i], sems.at[i])
-        for i in range(LEAVES)
+        pltpu.make_async_copy(w_ref.at[:, pl.ds(size * i, size), :], near_scr.at[n], sems.at[n])
+        for n, i in enumerate(leaves)
     ]
 
 
-def unpack(tiles, v_scr):
+def unpack(start, tiles, v_scr):
     for n, tile in enumerate(tiles):
         for l in range(PACK):
-            v_scr[PACK * n + l] = tile[:, COLS * l : COLS * (l + 1)]
-
-
-def near_field(g, idx_ref, copies, near_scr, v_scr):
-    cols = []
-    for i in range(PACK * g, PACK * (g + 1)):
-        copies[i].wait()
-        parts = [near_scr[i, :, ROWS * k : ROWS * (k + 1), :].reshape(PANEL, PANEL) for k in range(NEAR_K)]
-        rhs = jnp.concatenate([v_scr[idx_ref[i, k]] for k in range(NEAR_K)], axis=0)
-        cols.append(dot(jnp.concatenate(parts, axis=1), rhs))
-    return jnp.concatenate(cols, axis=1)
+            v_scr[PACK * (start + n) + l] = tile[:, COLS * l : COLS * (l + 1)]
+
+
+def near_field(idx_ref, copies, near_scr, v_scr):
+    for start in range(0, LEAVES, BATCH):
+        for i in range(start, start + BATCH):
+            copies[i].wait()
+        cols = []
+        for i in range(start, start + BATCH):
+            parts = [near_scr[i, :, ROWS * k : ROWS * (k + 1), :].reshape(PANEL, PANEL) for k in range(NEAR_K)]
+            rhs = jnp.concatenate([v_scr[idx_ref[i, k]] for k in range(NEAR_K)], axis=0)
+            cols.append(dot(jnp.concatenate(parts, axis=1), rhs))
+        for n in range(0, BATCH, PACK):
+            yield jnp.concatenate(cols[n : n + PACK], axis=1)
 
 
 def first_kernel(
-    far_ref, idx_ref, pc_ref, w_ref, t_ref, recv_ref, lo_ref, hi_ref,
-    out_ref, par_ref, bottom_ref, top_ref, cpl_ref, u_ref,
-    near_scr, own_scr, c_scr, rhs_scr, v_scr, sems, own_sem,
+    far_ref, idx_ref, pc_in, w_ref, t_in, recv_ref, lo_ref, hi_ref,
+    out_ref, par_ref, bottom_ref, top_ref, cpl_out, u_out,
+    near_scr, own_scr, c_scr, rhs_scr, v_scr, cpl_ref, u_ref, pc_ref, t_ref, sems, own_sem, side_sems,
 ):
     own = pltpu.make_async_copy(w_ref.at[:, pl.ds(BAS0, HELD - BAS0), :], own_scr, own_sem)
     own.start()
-    copies = near_copies(w_ref, near_scr, sems)
+    sources = fetch(((t_in, t_ref), (pc_in, pc_ref)), side_sems)
+    copies = near_copies(w_ref, near_scr, sems, range(LEAVES))
     for copy in copies:
         copy.start()
     tiles = [lo_ref[...]] + [recv_ref[:, ROWS * g : ROWS * (g + 1), :] for g in range(GROUPS)] + [hi_ref[...]]
-    unpack([tile.reshape(PANEL, 128) for tile in tiles], v_scr)
+    unpack(0, [tile.reshape(PANEL, 128) for tile in tiles], v_scr)
     own.wait()
+    for source in sources:
+        source.wait()
     for y in range(SHARES):
         rows = own_scr[y, CPL0 - BAS0 :, :].astype(F32).reshape(FAR_K, 8, 128)
         c_scr[:, 8 * y : 8 * y + 8, :] = rows
@@ -160,12 +174,13 @@
         lower = jnp.concatenate([zero, t_ref[2 * m + 1]], axis=1)
         pair = dot(rows, jnp.concatenate([upper, lower], axis=0)).astype(BF)
         u_ref[m // 2, :, 128 * (m % 2) : 128 * (m % 2 + 1)] = pair
+    sides = fetch(((cpl_ref, cpl_out), (u_ref, u_out)), side_sems)
     coef = far_sums(far_ref, pc_ref, cpl, rhs_scr)
     group = lane_group((RANK, 128))
     parents = [jnp.zeros((RANK, 128), F32), jnp.zeros((RANK, 128), F32)]
-    for g in range(GROUPS):
+    for g, near in enumerate(near_field(idx_ref, copies, near_scr, v_scr)):
         u = u_ref[g]
-        res = (near_field(g, idx_ref, copies, near_scr, v_scr) + far_field(u, coef[g // 2])).astype(BF)
+        res = (near + far_field(u, coef[g // 2])).astype(BF)
         tile = res.reshape(SHARES, ROWS, 128)
         out_ref[:, g] = tile
         if g == 0:
@@ -177,16 +192,18 @@
             parents[g // 2] += jnp.where(group == l, x[RANK * l : RANK * (l + 1)], 0.0)
     packed = pack_parents(spread(parents[0]), spread(parents[1]))
     par_ref[...] = jnp.broadcast_to(packed[None], par_ref.shape)
+    for side in sides:
+        side.wait()
 
 
 def near_kernel(idx_ref, w_ref, vec_ref, lo_ref, hi_ref, out_ref, near_scr, v_scr, sems):
-    copies = near_copies(w_ref, near_scr, sems)
+    copies = near_copies(w_ref, near_scr, sems, range(LEAVES))
     for copy in copies:
         copy.start()
     tiles = [lo_ref[...]] + [vec_ref[:, g] for g in range(GROUPS)] + [hi_ref[...]]
-    unpack([tile.reshape(PANEL, 128) for tile in tiles], v_scr)
-    for g in range(GROUPS):
-        out_ref[g] = near_field(g, idx_ref, copies, near_scr, v_scr)
+    unpack(0, [tile.reshape(PANEL, 128) for tile in tiles], v_scr)
+    for g, near in enumerate(near_field(idx_ref, copies, near_scr, v_scr)):
+        out_ref[g] = near
 
 
 def last_kernel(far_ref, pc_ref, cpl_ref, u_ref, near_ref, own_ref, out_ref, rhs_scr):
@@ -211,22 +228,20 @@
     return jax.ShapeDtypeStruct(shape, dtype)
 
 
-def call(kernel, name, outs, ins, scratch, flops, nbytes, *operands):
+def call(kernel, outs, ins, scratch, flops, nbytes, *operands, sides=0):
     single = not isinstance(outs, tuple)
     return pl.pallas_call(
         kernel,
         out_shape=outs,
         in_specs=ins,
-        out_specs=VMEM if single else (VMEM,) * len(outs),
+        out_specs=VMEM if single else (VMEM,) * (len(outs) - sides) + (ANY,) * sides,
         scratch_shapes=scratch,
         cost_estimate=pl.CostEstimate(flops=flops, bytes_accessed=nbytes, transcendentals=0),
-        name=name,
     )(*operands)
 
 
-def gather_parents(packed):
-    plane = lax.all_to_all(packed, ("x", "z"), 0, 0)
-    return lax.all_gather(plane, "core", axis=0)
+def exchange(values):
+    return lax.all_to_all(values, ("x", "z"), 0, 0)
 
 
 def halo(bottom, top):
@@ -236,7 +251,7 @@
     return lax.ppermute(top, CLUS, forward), lax.ppermute(bottom, CLUS, backward)
 
 
-def body(density, near_list, far_list, near_blocks, basis, transfer, coupling):
+def operator_twice(density, near_list, far_list, near_blocks, basis, transfer, coupling):
     share = array(SHARES, ROWS, 128)
     spread_out = array(PLANE, 32, 128)
     near_scratch = pltpu.VMEM((LEAVES, SHARES, NEAR_K * ROWS, PANEL), BF)
@@ -245,58 +260,62 @@
     near_sems = pltpu.SemaphoreType.DMA((LEAVES,))
 
     mine = call(
-        stack_kernel, "stack", array(HELD, PANEL), [VMEM] * 3, [], 0, 1_400_000,
+        stack_kernel, array(HELD, PANEL), [VMEM] * 3, [], 0, 1_400_000,
         near_blocks, basis, jnp.swapaxes(coupling, 2, 3),
     )
     held = lax.all_gather(mine, "y", axis=0)
     near_idx = near_list - (lax.axis_index(CLUS) * LEAVES - NWIN)
     near_idx = jnp.clip(near_idx, 0, LEAVES + 2 * NWIN - 1)
     sent = call(
-        prepare_kernel, "prepare", array(SHARES, SENT, 128), [VMEM] * 3, [], 40_000_000, 500_000,
+        prepare_kernel, array(SHARES, SENT, 128), [VMEM] * 3, [], 40_000_000, 500_000,
         density, basis, transfer,
     )
     recv = lax.all_to_all(sent, "y", 0, 0)
     parents, bottom, top = call(
-        parent_kernel, "parents", (spread_out, share, share), [VMEM], [], 100_000, 500_000, recv
-    )
-    every = gather_parents(parents)
+        parent_kernel, (spread_out, share, share), [VMEM], [], 100_000, 500_000, recv
+    )
+    every = lax.all_gather(exchange(parents), "core", axis=0)
     low, high = halo(bottom, top)
     first, parents, bottom, top, cpl, u = call(
-        first_kernel, "first",
+        first_kernel,
         (
             array(SHARES, GROUPS, ROWS, 128), spread_out, share, share,
             array(2, 2 * RANK, HALF), array(GROUPS, PANEL, PACK * RANK),
         ),
-        [SMEM, SMEM, VMEM, ANY] + [VMEM] * 4,
+        [SMEM, SMEM] + [ANY] * 3 + [VMEM] * 3,
         [
             near_scratch,
             pltpu.VMEM((SHARES, HELD - BAS0, 128), BF),
             pltpu.VMEM((FAR_K, RANK, 128), F32),
             rhs_scratch,
             vec_scratch,
+            pltpu.VMEM((2, 2 * RANK, HALF), BF),
+            pltpu.VMEM((GROUPS, PANEL, PACK * RANK), BF),
+            pltpu.VMEM((2, PLANE, 32, 128), BF),
+            pltpu.VMEM((LEAVES, RANK, RANK), BF),
             near_sems,
             pltpu.SemaphoreType.DMA,
+            pltpu.SemaphoreType.DMA((2,)),
         ],
         400_000_000, 8_000_000,
         far_list, near_idx, every, held, transfer, recv, low, high,
-    )
-    plane = lax.all_to_all(parents, ("x", "z"), 0, 0)
+        sides=2,
+    )
+    plane = exchange(parents)
     low, high = halo(bottom, top)
     near = call(
-        near_kernel, "near", array(GROUPS, PANEL, 128, dtype=F32), [SMEM, ANY] + [VMEM] * 3,
+        near_kernel, array(GROUPS, PANEL, 128, dtype=F32), [SMEM, ANY] + [VMEM] * 3,
         [near_scratch, vec_scratch, near_sems], 300_000_000, 6_000_000,
         near_idx, held, first, low, high,
     )
     every = lax.all_gather(plane, "core", axis=0)
     sent = call(
-        last_kernel, "last", array(SHARES, 2, GROUPS, ROWS, 128), [SMEM] + [VMEM] * 5,
+        last_kernel, array(SHARES, 2, GROUPS, ROWS, 128), [SMEM] + [VMEM] * 5,
         [rhs_scratch], 100_000_000, 2_000_000,
         far_list, every, cpl, u, near, first,
     )
     out = array(LEAVES, ROWS, 256)
-    return call(
-        finish_kernel, "finish", (out, out), [VMEM], [], 0, 600_000, lax.all_to_all(sent, "y", 0, 0)
-    )
+    return call(finish_kernel, (out, out), [VMEM], [], 0, 600_000, lax.all_to_all(sent, "y", 0, 0))
 
 
 def solution(mesh):
@@ -311,7 +330,7 @@
         P(CLUS, None, None, "y"),
     )
     return jax.shard_map(
-        body,
+        operator_twice,
         mesh=fine,
         in_specs=placed,
         out_specs=(P(CLUS, "y", None), P(CLUS, "y", None)),

time: 154 us -> 149 us (0.968)
  Pallas kernels: 28.6 us -> 24.3 us
    pallas_call x7, Pallas kernels: 28.6 us -> 24.3 us  [call(): pl.pallas_call(kernel, out_shape=outs, in_specs=ins, out_specs=VMEM if si...]
  transfers between devices with their start and end apart: 7 -> 7, of which waited for: 3 -> 3; matrix products, arithmetic and copies ran while one was open for 1% -> 1% of each run, Pallas kernels for 7% -> 6%
where the time goes in v7:
time: 149 us
  blocking collectives  41.3 us (28%)
  starting transfers between devices  37.7 us (25%)
  waiting for transfers between devices  29.3 us (20%)
  Pallas kernels  24.3 us (16%)
  between operations  14.1 us (9%)
    all_gather x1, waiting for transfers between devices, operator_twice(): held = lax.all_gather(mine, 'y', axis=0)  25.2 us
    pallas_call x7, Pallas kernels, call(): pl.pallas_call(kernel, out_shape=outs, in_specs=ins, out_specs=VMEM if si...  24.3 us
    all_to_all x2, starting transfers between devices, exchange(): return lax.all_to_all(values, ('x', 'z'), 0, 0)  23.6 us
    all_to_all x1, blocking collectives, operator_twice(): recv = lax.all_to_all(sent, 'y', 0, 0)  16.5 us
    all_to_all x1, blocking collectives, operator_twice(): lax.all_to_all(sent, 'y', 0, 0)  16.3 us
    ppermute x2, starting transfers between devices, halo(): lax.ppermute(top, CLUS, forward)  10.3 us
    all_gather x1, blocking collectives, operator_twice(): every = lax.all_gather(exchange(parents), 'core', axis=0)  6.18 us
    ppermute x2, starting transfers between devices, halo(): lax.ppermute(bottom, CLUS, backward)  3.84 us
  transfers between devices with their start and end apart: 7, of which 3 were waited for; matrix products, arithmetic and copies ran while one was open for 1% of the time, Pallas kernels for 6%

profile of v7, /device:TPU:1, one launch (start us, length us, event | category | flops | bytes accessed | tf_op | source)
XLA Modules:
  0.0 148.7 jit_solution(7737473006679485058)
XLA Ops:
  7.2 0.0 all-gather.5.cloned.1.call-start
  7.2 2.1 %shard_map.88 = bf16[2648,128]{1,0:T(8,128)(2,1)} custom-call(bf16[16,9,16,128]{3,2,1,0:T(8,128)(2,1)} %near_ref.1, bf16[16,16,64]{2,1,0:T(8,128)(2,1)} %b_ref.3, bf16[2,27,8,64]{3,2,1,0:T(8,128)(2,1)} %bitcast.8), custom_call_target="tpu_custom_call" | custom-call | bytes 1400000 | tf_op jit(solution)/shard_map/pallas_call | solution.py:233
  9.3 0.0 all-gather.5.cloned.1.call-update
  9.3 2.4 %shard_map.86 = bf16[8,96,128]{2,1,0:T(8,128)(2,1)} custom-call(bf16[16,16,256]{2,1,0:T(8,128)(2,1)} %d_ref.1, bf16[16,16,64]{2,1,0:T(8,128)(2,1)} %b_ref.3, bf16[16,64,64]{2,1,0:T(8,128)(2,1)} %t_in.1), custom_call_target="tpu_custom_call" | custom-call | flops 40000000 | bytes 500000 | tf_op jit(solution)/shard_map/pallas_call | solution.py:233
  11.7 16.5 %all_to_all.20.recv_ref = bf16[8,96,128]{2,1,0:T(8,128)(2,1)} all-to-all(bf16[8,96,128]{2,1,0:T(8,128)(2,1)} %shard_map.86), channel_id=1, replica_groups=mesh['x'=4,'z'=8,'core'=2,'y'=8] {'y'}, dimensions={0} | all-to-all | bytes 393216 | tf_op jit(solution)/shard_map/all_to_all | solution.py:273
  28.1 1.6 %shard_map.87 = (bf16[32,32,128]{2,1,0:T(8,128)(2,1)}, bf16[8,16,128]{2,1,0:T(8,128)(2,1)}, bf16[8,16,128]{2,1,0:T(8,128)(2,1)}) custom-call(bf16[8,96,128]{2,1,0:T(8,128)(2,1)} %all_to_all.20.recv_ref), custom_call_target="tpu_custom_call" | custom-call | flops 100000 | bytes 500000 | tf_op jit(solution)/shard_map/pallas_call | solution.py:233
  29.8 13.2 %all-to-all-start.1 = ((bf16[32,32,128]{2,1,0:T(8,128)(2,1)}), bf16[32,32,128]{2,1,0:T(8,128)(2,1)S(1)}, u32[]{:S(2)}, u32[]{:S(2)}) async-start(bf16[32,32,128]{2,1,0:T(8,128)(2,1)} %get-tuple-element.11), calls=%async_computation.1 | async-start | bytes 524288 | tf_op jit(solution)/shard_map/all_to_all | solution.py:244
  43.0 1.3 subtract_clamp_fusion.idx_ref
  44.3 6.1 %collective-permute-start = (bf16[8,16,128]{2,1,0:T(8,128)(2,1)}, bf16[8,16,128]{2,1,0:T(8,128)(2,1)S(1)}, u32[]{:S(2)}, u32[]{:S(2)}) collective-permute-start(bf16[8,16,128]{2,1,0:T(8,128)(2,1)} %get-tuple-element.12), channel_id=1, source_target_pairs={{0,8},{8,16},{16,24},{24,32},{32,40},{40,48},{48,56},{56,64},{64,7... | collective-permute-start | bytes 98312 | tf_op jit(solution)/shard_map/ppermute | solution.py:251
  50.4 1.9 %collective-permute-start.1 = (bf16[8,16,128]{2,1,0:T(8,128)(2,1)}, bf16[8,16,128]{2,1,0:T(8,128)(2,1)S(1)}, u32[]{:S(2)}, u32[]{:S(2)}) collective-permute-start(bf16[8,16,128]{2,1,0:T(8,128)(2,1)} %get-tuple-element.13), channel_id=1, source_target_pairs={{8,0},{16,8},{24,16},{32,24},{40,32},{48,40},{56,48},{64,56},{72,6... | collective-permute-start | bytes 98312 | tf_op jit(solution)/shard_map/ppermute | solution.py:251
  52.3 0.3 all-to-all-done.1
  52.6 6.2 %all-gather = bf16[64,32,128]{2,1,0:T(8,128)(2,1)} all-gather(bf16[32,32,128]{2,1,0:T(8,128)(2,1)S(1)} %all-to-all-done.1), channel_id=2, replica_groups=mesh['x'=4,'z'=8,'core'=2,'y'=8] {'core'}, dimensions={0}, use_global_device_ids=true | all-gather | bytes 786432 | tf_op jit(solution)/shard_map/all_gather | solution.py:277
  58.8 25.2 %all-gather.5.cloned.1.call-done = bf16[21184,128]{1,0:T(8,128)(2,1)} async-done(((bf16[2648,128]{1,0:T(8,128)(2,1)}), bf16[21184,128]{1,0:T(8,128)(2,1)}) %all-gather.5.cloned.1.call-update) | async-done | bytes 5423120 | tf_op jit(solution)/shard_map/all_gather | solution.py:266
  84.0 8.0 %shard_map.89 = (bf16[8,4,16,128]{3,2,1,0:T(8,128)(2,1)}, bf16[32,32,128]{2,1,0:T(8,128)(2,1)}, bf16[8,16,128]{2,1,0:T(8,128)(2,1)}, bf16[8,16,128]{2,1,0:T(8,12...) custom-call(s32[2,27]{1,0:T(2,128)} %far_ref.3, s32[16,9]{1,0:T(8,128)} %subtract_clamp_fusion.idx_ref, ...), custom_call_target="tpu_custom_call" | custom-call | flops 400000000 | bytes 8000000 | tf_op jit(solution)/shard_map/pallas_call | solution.py:233
  92.0 10.4 %all-to-all-start.2 = ((bf16[32,32,128]{2,1,0:T(8,128)(2,1)}), bf16[32,32,128]{2,1,0:T(8,128)(2,1)S(1)}, u32[]{:S(2)}, u32[]{:S(2)}) async-start(bf16[32,32,128]{2,1,0:T(8,128)(2,1)} %get-tuple-element.14), calls=%async_computation.2 | async-start | bytes 524288 | tf_op jit(solution)/shard_map/all_to_all | solution.py:244
  102.4 4.2 %collective-permute-start.2 = (bf16[8,16,128]{2,1,0:T(8,128)(2,1)}, bf16[8,16,128]{2,1,0:T(8,128)(2,1)S(1)}, u32[]{:S(2)}, u32[]{:S(2)}) collective-permute-start(bf16[8,16,128]{2,1,0:T(8,128)(2,1)} %get-tuple-element.18), channel_id=1, source_target_pairs={{0,8},{8,16},{16,24},{24,32},{32,40},{40,48},{48,56},{56,64},{64,7... | collective-permute-start | bytes 98312 | tf_op jit(solution)/shard_map/ppermute | solution.py:251
  106.6 1.9 %collective-permute-start.3 = (bf16[8,16,128]{2,1,0:T(8,128)(2,1)}, bf16[8,16,128]{2,1,0:T(8,128)(2,1)S(1)}, u32[]{:S(2)}, u32[]{:S(2)}) collective-permute-start(bf16[8,16,128]{2,1,0:T(8,128)(2,1)} %get-tuple-element.19), channel_id=1, source_target_pairs={{8,0},{16,8},{24,16},{32,24},{40,32},{48,40},{56,48},{64,56},{72,6... | collective-permute-start | bytes 98312 | tf_op jit(solution)/shard_map/ppermute | solution.py:251
  108.5 3.8 %collective-permute-done.3.hi_ref = bf16[8,16,128]{2,1,0:T(8,128)(2,1)S(1)} collective-permute-done((bf16[8,16,128]{2,1,0:T(8,128)(2,1)}, bf16[8,16,128]{2,1,0:T(8,128)(2,1)S(1)}, u32[]{:S(2)}, u32[]{:S(2)}) %collective-permute-start.3) | collective-permute-done | bytes 32800 | tf_op jit(solution)/shard_map/ppermute | solution.py:251
  112.3 0.6 copy-done.3
  112.9 5.1 %shard_map.90.near_ref = f32[4,128,128]{2,1,0:T(8,128)} custom-call(s32[16,9]{1,0:T(8,128)} %subtract_clamp_fusion.idx_ref, bf16[8,2648,128]{2,1,0:T(8,128)(2,1)} %bitcast.5, bf16[8,4,16,128]{3,2,1,0:T(8,128)(2,1)} %get-tuple-element.17.vec_ref.own_ref, bf16[8,16,128]{2,1,0:T(8,128)(2,1)} %copy-done.2, bf16[8,16,128]{2,1,0:T(8,128)(2,1)} %copy-done.3), custom_call_target="tpu_custom_call" | custom-call | flops 300000000 | bytes 6000000 | tf_op jit(solution)/shard_map/pallas_call | solution.py:233
  118.0 2.3 %all-gather.2 = bf16[64,32,128]{2,1,0:T(8,128)(2,1)} all-gather(bf16[32,32,128]{2,1,0:T(8,128)(2,1)S(1)} %all-to-all-done.2), channel_id=4, replica_groups=mesh['x'=4,'z'=8,'core'=2,'y'=8] {'core'}, dimensions={0}, use_global_device_ids=true | all-gather | bytes 786432 | tf_op jit(solution)/shard_map/all_gather | solution.py:311
  120.3 3.3 %shard_map.91 = bf16[8,2,4,16,128]{4,3,2,1,0:T(8,128)(2,1)} custom-call(s32[2,27]{1,0:T(2,128)} %far_ref.3, bf16[2,32,32,128]{3,2,1,0:T(8,128)(2,1)} %bitcast.6, bf16[2,128,864]{2,1,0:T(8,128)(2,1)} %get-tuple-element.15.cpl_ref, bf16[4,128,256]{2,1,0:T(8,128)(2,1)} %get-tuple-element.16.u_ref, f32[4,128,128]{2,1,0:T(8,128)} %shard_map.90.near_ref, ...), custom_call_target="tpu_custom_call" | custom-call | flops 100000000 | bytes 2000000 | tf_op jit(solution)/shard_map/pallas_call | solution.py:233
  123.6 16.3 %all_to_all.21.recv_ref = bf16[8,2,4,16,128]{4,3,2,1,0:T(8,128)(2,1)} all-to-all(bf16[8,2,4,16,128]{4,3,2,1,0:T(8,128)(2,1)} %shard_map.91), channel_id=1, replica_groups=mesh['x'=4,'z'=8,'core'=2,'y'=8] {'y'}, dimensions={0} | all-to-all | bytes 524288 | tf_op jit(solution)/shard_map/all_to_all | solution.py:318
  139.9 1.9 %shard_map.92 = (bf16[16,16,256]{2,1,0:T(8,128)(2,1)}, bf16[16,16,256]{2,1,0:T(8,128)(2,1)}) custom-call(bf16[8,2,4,16,128]{4,3,2,1,0:T(8,128)(2,1)} %all_to_all.21.recv_ref), custom_call_target="tpu_custom_call" | custom-call | bytes 600000 | tf_op jit(solution)/shard_map/pallas_call | solution.py:233
  (11 shorter events, 0.0 us)
Async XLA Ops:
  7.2 76.8 %all-gather.5.cloned.1.call-start = ((), (), s32[]{:S(2)}) async-start(), calls=%async_computation.4 | async-start | bytes 6100992 | tf_op jit(solution)/shard_map/all_gather | solution.py:266
  29.8 22.8 %all-to-all-start.1 = ((bf16[32,32,128]{2,1,0:T(8,128)(2,1)}), bf16[32,32,128]{2,1,0:T(8,128)(2,1)S(1)}, u32[]{:S(2)}, u32[]{:S(2)}) async-start(bf16[32,32,128]{2,1,0:T(8,128)(2,1)} %get-tuple-element.11), calls=%async_computation.1 | async-start | bytes 524288 | tf_op jit(solution)/shard_map/all_to_all | solution.py:244
  44.3 14.5 %collective-permute-start = (bf16[8,16,128]{2,1,0:T(8,128)(2,1)}, bf16[8,16,128]{2,1,0:T(8,128)(2,1)S(1)}, u32[]{:S(2)}, u32[]{:S(2)}) collective-permute-start(bf16[8,16,128]{2,1,0:T(8,128)(2,1)} %get-tuple-element.12), channel_id=1, source_target_pairs={{0,8},{8,16},{16,24},{24,32},{32,40},{40,48},{48,56},{56,64},{64,7... | collective-permute-start | bytes 98312 | tf_op jit(solution)/shard_map/ppermute | solution.py:251
  50.4 8.4 %collective-permute-start.1 = (bf16[8,16,128]{2,1,0:T(8,128)(2,1)}, bf16[8,16,128]{2,1,0:T(8,128)(2,1)S(1)}, u32[]{:S(2)}, u32[]{:S(2)}) collective-permute-start(bf16[8,16,128]{2,1,0:T(8,128)(2,1)} %get-tuple-element.13), channel_id=1, source_target_pairs={{8,0},{16,8},{24,16},{32,24},{40,32},{48,40},{56,48},{64,56},{72,6... | collective-permute-start | bytes 98312 | tf_op jit(solution)/shard_map/ppermute | solution.py:251
  58.8 25.2 %copy-start = (bf16[8,16,128]{2,1,0:T(8,128)(2,1)}, bf16[8,16,128]{2,1,0:T(8,128)(2,1)S(1)}, u32[]{:S(2)}) copy-start(bf16[8,16,128]{2,1,0:T(8,128)(2,1)S(1)} %collective-permute-done.lo_ref) | copy-start | bytes 98308
  58.8 25.2 %copy-start.1 = (bf16[8,16,128]{2,1,0:T(8,128)(2,1)}, bf16[8,16,128]{2,1,0:T(8,128)(2,1)S(1)}, u32[]{:S(2)}) copy-start(bf16[8,16,128]{2,1,0:T(8,128)(2,1)S(1)} %collective-permute-done.1.hi_ref) | copy-start | bytes 98308
  92.0 26.0 %all-to-all-start.2 = ((bf16[32,32,128]{2,1,0:T(8,128)(2,1)}), bf16[32,32,128]{2,1,0:T(8,128)(2,1)S(1)}, u32[]{:S(2)}, u32[]{:S(2)}) async-start(bf16[32,32,128]{2,1,0:T(8,128)(2,1)} %get-tuple-element.14), calls=%async_computation.2 | async-start | bytes 524288 | tf_op jit(solution)/shard_map/all_to_all | solution.py:244
  102.4 6.1 %collective-permute-start.2 = (bf16[8,16,128]{2,1,0:T(8,128)(2,1)}, bf16[8,16,128]{2,1,0:T(8,128)(2,1)S(1)}, u32[]{:S(2)}, u32[]{:S(2)}) collective-permute-start(bf16[8,16,128]{2,1,0:T(8,128)(2,1)} %get-tuple-element.18), channel_id=1, source_target_pairs={{0,8},{8,16},{16,24},{24,32},{32,40},{40,48},{48,56},{56,64},{64,7... | collective-permute-start | bytes 98312 | tf_op jit(solution)/shard_map/ppermute | solution.py:251
  106.6 5.7 %collective-permute-start.3 = (bf16[8,16,128]{2,1,0:T(8,128)(2,1)}, bf16[8,16,128]{2,1,0:T(8,128)(2,1)S(1)}, u32[]{:S(2)}, u32[]{:S(2)}) collective-permute-start(bf16[8,16,128]{2,1,0:T(8,128)(2,1)} %get-tuple-element.19), channel_id=1, source_target_pairs={{8,0},{16,8},{24,16},{32,24},{40,32},{48,40},{56,48},{64,56},{72,6... | collective-permute-start | bytes 98312 | tf_op jit(solution)/shard_map/ppermute | solution.py:251
  108.5 3.8 %copy-start.2 = (bf16[8,16,128]{2,1,0:T(8,128)(2,1)}, bf16[8,16,128]{2,1,0:T(8,128)(2,1)S(1)}, u32[]{:S(2)}) copy-start(bf16[8,16,128]{2,1,0:T(8,128)(2,1)S(1)} %collective-permute-done.2.lo_ref) | copy-start | bytes 98308
  112.3 0.6 copy-start.3
Sparse Core Ops, SparseCore 0:
  10.1 73.8 all-gather.4

commit v8 on v7

--- a/solution.py
+++ b/solution.py
@@ -106,9 +106,9 @@
             tile = pc_ref[(parent // 2) % 2, parent // 4]
             rhs_scr[32 * k : 32 * (k + 1), :] = jnp.where(side == parent % 2, tile, jnp.zeros_like(tile))
         rhs = rhs_scr[...]
-        acc0 = dot(cpl[0][RANK * p : RANK * (p + 1)], rhs)
-        acc1 = dot(cpl[1][RANK * p : RANK * (p + 1)], rhs)
-        sums.append(spread(jnp.where(even, acc0, acc1)).astype(BF).astype(F32))
+        rows = slice(RANK * p, RANK * (p + 1))
+        acc = dot(jnp.concatenate([cpl[0][rows], cpl[1][rows]], axis=0), rhs)
+        sums.append(spread(jnp.where(even, acc[:RANK], acc[RANK:])).astype(BF).astype(F32))
     return sums
 
 
@@ -154,13 +154,13 @@
     own.start()
     sources = fetch(((t_in, t_ref), (pc_in, pc_ref)), side_sems)
     copies = near_copies(w_ref, near_scr, sems, range(LEAVES))
-    for copy in copies:
-        copy.start()
     tiles = [lo_ref[...]] + [recv_ref[:, ROWS * g : ROWS * (g + 1), :] for g in range(GROUPS)] + [hi_ref[...]]
     unpack(0, [tile.reshape(PANEL, 128) for tile in tiles], v_scr)
     own.wait()
     for source in sources:
         source.wait()
+    for copy in copies[:BATCH]:
+        copy.start()
     for y in range(SHARES):
         rows = own_scr[y, CPL0 - BAS0 :, :].astype(F32).reshape(FAR_K, 8, 128)
         c_scr[:, 8 * y : 8 * y + 8, :] = rows
@@ -174,6 +174,8 @@
         lower = jnp.concatenate([zero, t_ref[2 * m + 1]], axis=1)
         pair = dot(rows, jnp.concatenate([upper, lower], axis=0)).astype(BF)
         u_ref[m // 2, :, 128 * (m % 2) : 128 * (m % 2 + 1)] = pair
+    for copy in copies[BATCH:]:
+        copy.start()
     sides = fetch(((cpl_ref, cpl_out), (u_ref, u_out)), side_sems)
     coef = far_sums(far_ref, pc_ref, cpl, rhs_scr)
     group = lane_group((RANK, 128))
@@ -198,10 +200,12 @@
 
 def near_kernel(idx_ref, w_ref, vec_ref, lo_ref, hi_ref, out_ref, near_scr, v_scr, sems):
     copies = near_copies(w_ref, near_scr, sems, range(LEAVES))
-    for copy in copies:
+    for copy in copies[:BATCH]:
         copy.start()
     tiles = [lo_ref[...]] + [vec_ref[:, g] for g in range(GROUPS)] + [hi_ref[...]]
     unpack(0, [tile.reshape(PANEL, 128) for tile in tiles], v_scr)
+    for copy in copies[BATCH:]:
+        copy.start()
     for g, near in enumerate(near_field(idx_ref, copies, near_scr, v_scr)):
         out_ref[g] = near
 

time: 149 us -> 150 us (level)
  no operation moved by 1% of the time
where the time goes in v8:
time: 150 us; the launch traced here: 149 us
  blocking collectives  41.3 us (28%)
  starting transfers between devices  37.7 us (25%)
  waiting for transfers between devices  29.3 us (20%)
  Pallas kernels  24.4 us (16%)
  between operations  14.1 us (9%)
    all_gather x1, waiting for transfers between devices, operator_twice(): held = lax.all_gather(mine, 'y', axis=0)  25.2 us
    pallas_call x7, Pallas kernels, call(): pl.pallas_call(kernel, out_shape=outs, in_specs=ins, out_specs=VMEM if si...  24.4 us
    all_to_all x2, starting transfers between devices, exchange(): return lax.all_to_all(values, ('x', 'z'), 0, 0)  23.6 us
    all_to_all x1, blocking collectives, operator_twice(): recv = lax.all_to_all(sent, 'y', 0, 0)  16.5 us
    all_to_all x1, blocking collectives, operator_twice(): lax.all_to_all(sent, 'y', 0, 0)  16.3 us
    ppermute x2, starting transfers between devices, halo(): lax.ppermute(top, CLUS, forward)  10.3 us
    all_gather x1, blocking collectives, operator_twice(): every = lax.all_gather(exchange(parents), 'core', axis=0)  6.18 us
    ppermute x2, starting transfers between devices, halo(): lax.ppermute(bottom, CLUS, backward)  3.84 us
  transfers between devices with their start and end apart: 7, of which 3 were waited for; matrix products, arithmetic and copies ran while one was open for 1% of the time, Pallas kernels for 6%

profile of v8, /device:TPU:1, one launch (start us, length us, event | category | flops | bytes accessed | tf_op | source)
XLA Modules:
  0.0 148.8 jit_solution(7880142100188923940)
XLA Ops:
  7.2 0.0 all-gather.5.cloned.1.call-start
  7.2 2.1 %shard_map.88 = bf16[2648,128]{1,0:T(8,128)(2,1)} custom-call(bf16[16,9,16,128]{3,2,1,0:T(8,128)(2,1)} %near_ref.1, bf16[16,16,64]{2,1,0:T(8,128)(2,1)} %b_ref.3, bf16[2,27,8,64]{3,2,1,0:T(8,128)(2,1)} %bitcast.8), custom_call_target="tpu_custom_call" | custom-call | bytes 1400000 | tf_op jit(solution)/shard_map/pallas_call | solution.py:237
  9.3 0.0 all-gather.5.cloned.1.call-update
  9.3 2.4 %shard_map.86 = bf16[8,96,128]{2,1,0:T(8,128)(2,1)} custom-call(bf16[16,16,256]{2,1,0:T(8,128)(2,1)} %d_ref.1, bf16[16,16,64]{2,1,0:T(8,128)(2,1)} %b_ref.3, bf16[16,64,64]{2,1,0:T(8,128)(2,1)} %t_in.1), custom_call_target="tpu_custom_call" | custom-call | flops 40000000 | bytes 500000 | tf_op jit(solution)/shard_map/pallas_call | solution.py:237
  11.7 16.5 %all_to_all.20.recv_ref = bf16[8,96,128]{2,1,0:T(8,128)(2,1)} all-to-all(bf16[8,96,128]{2,1,0:T(8,128)(2,1)} %shard_map.86), channel_id=1, replica_groups=mesh['x'=4,'z'=8,'core'=2,'y'=8] {'y'}, dimensions={0} | all-to-all | bytes 393216 | tf_op jit(solution)/shard_map/all_to_all | solution.py:277
  28.1 1.6 %shard_map.87 = (bf16[32,32,128]{2,1,0:T(8,128)(2,1)}, bf16[8,16,128]{2,1,0:T(8,128)(2,1)}, bf16[8,16,128]{2,1,0:T(8,128)(2,1)}) custom-call(bf16[8,96,128]{2,1,0:T(8,128)(2,1)} %all_to_all.20.recv_ref), custom_call_target="tpu_custom_call" | custom-call | flops 100000 | bytes 500000 | tf_op jit(solution)/shard_map/pallas_call | solution.py:237
  29.8 13.2 %all-to-all-start.1 = ((bf16[32,32,128]{2,1,0:T(8,128)(2,1)}), bf16[32,32,128]{2,1,0:T(8,128)(2,1)S(1)}, u32[]{:S(2)}, u32[]{:S(2)}) async-start(bf16[32,32,128]{2,1,0:T(8,128)(2,1)} %get-tuple-element.11), calls=%async_computation.1 | async-start | bytes 524288 | tf_op jit(solution)/shard_map/all_to_all | solution.py:248
  43.0 1.3 subtract_clamp_fusion.idx_ref
  44.3 6.1 %collective-permute-start = (bf16[8,16,128]{2,1,0:T(8,128)(2,1)}, bf16[8,16,128]{2,1,0:T(8,128)(2,1)S(1)}, u32[]{:S(2)}, u32[]{:S(2)}) collective-permute-start(bf16[8,16,128]{2,1,0:T(8,128)(2,1)} %get-tuple-element.12), channel_id=1, source_target_pairs={{0,8},{8,16},{16,24},{24,32},{32,40},{40,48},{48,56},{56,64},{64,7... | collective-permute-start | bytes 98312 | tf_op jit(solution)/shard_map/ppermute | solution.py:255
  50.4 1.9 %collective-permute-start.1 = (bf16[8,16,128]{2,1,0:T(8,128)(2,1)}, bf16[8,16,128]{2,1,0:T(8,128)(2,1)S(1)}, u32[]{:S(2)}, u32[]{:S(2)}) collective-permute-start(bf16[8,16,128]{2,1,0:T(8,128)(2,1)} %get-tuple-element.13), channel_id=1, source_target_pairs={{8,0},{16,8},{24,16},{32,24},{40,32},{48,40},{56,48},{64,56},{72,6... | collective-permute-start | bytes 98312 | tf_op jit(solution)/shard_map/ppermute | solution.py:255
  52.3 0.3 all-to-all-done.1
  52.6 6.2 %all-gather = bf16[64,32,128]{2,1,0:T(8,128)(2,1)} all-gather(bf16[32,32,128]{2,1,0:T(8,128)(2,1)S(1)} %all-to-all-done.1), channel_id=2, replica_groups=mesh['x'=4,'z'=8,'core'=2,'y'=8] {'core'}, dimensions={0}, use_global_device_ids=true | all-gather | bytes 786432 | tf_op jit(solution)/shard_map/all_gather | solution.py:281
  58.8 25.2 %all-gather.5.cloned.1.call-done = bf16[21184,128]{1,0:T(8,128)(2,1)} async-done(((bf16[2648,128]{1,0:T(8,128)(2,1)}), bf16[21184,128]{1,0:T(8,128)(2,1)}) %all-gather.5.cloned.1.call-update) | async-done | bytes 5423120 | tf_op jit(solution)/shard_map/all_gather | solution.py:270
  84.0 8.1 %shard_map.89 = (bf16[8,4,16,128]{3,2,1,0:T(8,128)(2,1)}, bf16[32,32,128]{2,1,0:T(8,128)(2,1)}, bf16[8,16,128]{2,1,0:T(8,128)(2,1)}, bf16[8,16,128]{2,1,0:T(8,12...) custom-call(s32[2,27]{1,0:T(2,128)} %far_ref.3, s32[16,9]{1,0:T(8,128)} %subtract_clamp_fusion.idx_ref, ...), custom_call_target="tpu_custom_call" | custom-call | flops 400000000 | bytes 8000000 | tf_op jit(solution)/shard_map/pallas_call | solution.py:237
  92.1 10.4 %all-to-all-start.2 = ((bf16[32,32,128]{2,1,0:T(8,128)(2,1)}), bf16[32,32,128]{2,1,0:T(8,128)(2,1)S(1)}, u32[]{:S(2)}, u32[]{:S(2)}) async-start(bf16[32,32,128]{2,1,0:T(8,128)(2,1)} %get-tuple-element.14), calls=%async_computation.2 | async-start | bytes 524288 | tf_op jit(solution)/shard_map/all_to_all | solution.py:248
  102.5 4.2 %collective-permute-start.2 = (bf16[8,16,128]{2,1,0:T(8,128)(2,1)}, bf16[8,16,128]{2,1,0:T(8,128)(2,1)S(1)}, u32[]{:S(2)}, u32[]{:S(2)}) collective-permute-start(bf16[8,16,128]{2,1,0:T(8,128)(2,1)} %get-tuple-element.18), channel_id=1, source_target_pairs={{0,8},{8,16},{16,24},{24,32},{32,40},{40,48},{48,56},{56,64},{64,7... | collective-permute-start | bytes 98312 | tf_op jit(solution)/shard_map/ppermute | solution.py:255
  106.7 1.9 %collective-permute-start.3 = (bf16[8,16,128]{2,1,0:T(8,128)(2,1)}, bf16[8,16,128]{2,1,0:T(8,128)(2,1)S(1)}, u32[]{:S(2)}, u32[]{:S(2)}) collective-permute-start(bf16[8,16,128]{2,1,0:T(8,128)(2,1)} %get-tuple-element.19), channel_id=1, source_target_pairs={{8,0},{16,8},{24,16},{32,24},{40,32},{48,40},{56,48},{64,56},{72,6... | collective-permute-start | bytes 98312 | tf_op jit(solution)/shard_map/ppermute | solution.py:255
  108.7 3.8 %collective-permute-done.3.hi_ref = bf16[8,16,128]{2,1,0:T(8,128)(2,1)S(1)} collective-permute-done((bf16[8,16,128]{2,1,0:T(8,128)(2,1)}, bf16[8,16,128]{2,1,0:T(8,128)(2,1)S(1)}, u32[]{:S(2)}, u32[]{:S(2)}) %collective-permute-start.3) | collective-permute-done | bytes 32800 | tf_op jit(solution)/shard_map/ppermute | solution.py:255
  112.5 0.6 copy-done.3
  113.1 5.1 %shard_map.90.near_ref = f32[4,128,128]{2,1,0:T(8,128)} custom-call(s32[16,9]{1,0:T(8,128)} %subtract_clamp_fusion.idx_ref, bf16[8,2648,128]{2,1,0:T(8,128)(2,1)} %bitcast.5, bf16[8,4,16,128]{3,2,1,0:T(8,128)(2,1)} %get-tuple-element.17.vec_ref.own_ref, bf16[8,16,128]{2,1,0:T(8,128)(2,1)} %copy-done.2, bf16[8,16,128]{2,1,0:T(8,128)(2,1)} %copy-done.3), custom_call_target="tpu_custom_call" | custom-call | flops 300000000 | bytes 6000000 | tf_op jit(solution)/shard_map/pallas_call | solution.py:237
  118.2 2.3 %all-gather.2 = bf16[64,32,128]{2,1,0:T(8,128)(2,1)} all-gather(bf16[32,32,128]{2,1,0:T(8,128)(2,1)S(1)} %all-to-all-done.2), channel_id=4, replica_groups=mesh['x'=4,'z'=8,'core'=2,'y'=8] {'core'}, dimensions={0}, use_global_device_ids=true | all-gather | bytes 786432 | tf_op jit(solution)/shard_map/all_gather | solution.py:315
  120.5 3.2 %shard_map.91 = bf16[8,2,4,16,128]{4,3,2,1,0:T(8,128)(2,1)} custom-call(s32[2,27]{1,0:T(2,128)} %far_ref.3, bf16[2,32,32,128]{3,2,1,0:T(8,128)(2,1)} %bitcast.6, bf16[2,128,864]{2,1,0:T(8,128)(2,1)} %get-tuple-element.15.cpl_ref, bf16[4,128,256]{2,1,0:T(8,128)(2,1)} %get-tuple-element.16.u_ref, f32[4,128,128]{2,1,0:T(8,128)} %shard_map.90.near_ref, ...), custom_call_target="tpu_custom_call" | custom-call | flops 100000000 | bytes 2000000 | tf_op jit(solution)/shard_map/pallas_call | solution.py:237
  123.7 16.3 %all_to_all.21.recv_ref = bf16[8,2,4,16,128]{4,3,2,1,0:T(8,128)(2,1)} all-to-all(bf16[8,2,4,16,128]{4,3,2,1,0:T(8,128)(2,1)} %shard_map.91), channel_id=1, replica_groups=mesh['x'=4,'z'=8,'core'=2,'y'=8] {'y'}, dimensions={0} | all-to-all | bytes 524288 | tf_op jit(solution)/shard_map/all_to_all | solution.py:322
  140.0 1.9 %shard_map.92 = (bf16[16,16,256]{2,1,0:T(8,128)(2,1)}, bf16[16,16,256]{2,1,0:T(8,128)(2,1)}) custom-call(bf16[8,2,4,16,128]{4,3,2,1,0:T(8,128)(2,1)} %all_to_all.21.recv_ref), custom_call_target="tpu_custom_call" | custom-call | bytes 600000 | tf_op jit(solution)/shard_map/pallas_call | solution.py:237
  (11 shorter events, 0.0 us)
Async XLA Ops:
  7.2 76.8 %all-gather.5.cloned.1.call-start = ((), (), s32[]{:S(2)}) async-start(), calls=%async_computation.4 | async-start | bytes 6100992 | tf_op jit(solution)/shard_map/all_gather | solution.py:270
  29.8 22.8 %all-to-all-start.1 = ((bf16[32,32,128]{2,1,0:T(8,128)(2,1)}), bf16[32,32,128]{2,1,0:T(8,128)(2,1)S(1)}, u32[]{:S(2)}, u32[]{:S(2)}) async-start(bf16[32,32,128]{2,1,0:T(8,128)(2,1)} %get-tuple-element.11), calls=%async_computation.1 | async-start | bytes 524288 | tf_op jit(solution)/shard_map/all_to_all | solution.py:248
  44.3 14.5 %collective-permute-start = (bf16[8,16,128]{2,1,0:T(8,128)(2,1)}, bf16[8,16,128]{2,1,0:T(8,128)(2,1)S(1)}, u32[]{:S(2)}, u32[]{:S(2)}) collective-permute-start(bf16[8,16,128]{2,1,0:T(8,128)(2,1)} %get-tuple-element.12), channel_id=1, source_target_pairs={{0,8},{8,16},{16,24},{24,32},{32,40},{40,48},{48,56},{56,64},{64,7... | collective-permute-start | bytes 98312 | tf_op jit(solution)/shard_map/ppermute | solution.py:255
  50.4 8.4 %collective-permute-start.1 = (bf16[8,16,128]{2,1,0:T(8,128)(2,1)}, bf16[8,16,128]{2,1,0:T(8,128)(2,1)S(1)}, u32[]{:S(2)}, u32[]{:S(2)}) collective-permute-start(bf16[8,16,128]{2,1,0:T(8,128)(2,1)} %get-tuple-element.13), channel_id=1, source_target_pairs={{8,0},{16,8},{24,16},{32,24},{40,32},{48,40},{56,48},{64,56},{72,6... | collective-permute-start | bytes 98312 | tf_op jit(solution)/shard_map/ppermute | solution.py:255
  58.8 25.2 %copy-start = (bf16[8,16,128]{2,1,0:T(8,128)(2,1)}, bf16[8,16,128]{2,1,0:T(8,128)(2,1)S(1)}, u32[]{:S(2)}) copy-start(bf16[8,16,128]{2,1,0:T(8,128)(2,1)S(1)} %collective-permute-done.lo_ref) | copy-start | bytes 98308
  58.8 25.2 %copy-start.1 = (bf16[8,16,128]{2,1,0:T(8,128)(2,1)}, bf16[8,16,128]{2,1,0:T(8,128)(2,1)S(1)}, u32[]{:S(2)}) copy-start(bf16[8,16,128]{2,1,0:T(8,128)(2,1)S(1)} %collective-permute-done.1.hi_ref) | copy-start | bytes 98308
  92.1 26.0 %all-to-all-start.2 = ((bf16[32,32,128]{2,1,0:T(8,128)(2,1)}), bf16[32,32,128]{2,1,0:T(8,128)(2,1)S(1)}, u32[]{:S(2)}, u32[]{:S(2)}) async-start(bf16[32,32,128]{2,1,0:T(8,128)(2,1)} %get-tuple-element.14), calls=%async_computation.2 | async-start | bytes 524288 | tf_op jit(solution)/shard_map/all_to_all | solution.py:248
  102.5 6.1 %collective-permute-start.2 = (bf16[8,16,128]{2,1,0:T(8,128)(2,1)}, bf16[8,16,128]{2,1,0:T(8,128)(2,1)S(1)}, u32[]{:S(2)}, u32[]{:S(2)}) collective-permute-start(bf16[8,16,128]{2,1,0:T(8,128)(2,1)} %get-tuple-element.18), channel_id=1, source_target_pairs={{0,8},{8,16},{16,24},{24,32},{32,40},{40,48},{48,56},{56,64},{64,7... | collective-permute-start | bytes 98312 | tf_op jit(solution)/shard_map/ppermute | solution.py:255
  106.7 5.7 %collective-permute-start.3 = (bf16[8,16,128]{2,1,0:T(8,128)(2,1)}, bf16[8,16,128]{2,1,0:T(8,128)(2,1)S(1)}, u32[]{:S(2)}, u32[]{:S(2)}) collective-permute-start(bf16[8,16,128]{2,1,0:T(8,128)(2,1)} %get-tuple-element.19), channel_id=1, source_target_pairs={{8,0},{16,8},{24,16},{32,24},{40,32},{48,40},{56,48},{64,56},{72,6... | collective-permute-start | bytes 98312 | tf_op jit(solution)/shard_map/ppermute | solution.py:255
  108.6 3.8 %copy-start.2 = (bf16[8,16,128]{2,1,0:T(8,128)(2,1)}, bf16[8,16,128]{2,1,0:T(8,128)(2,1)S(1)}, u32[]{:S(2)}) copy-start(bf16[8,16,128]{2,1,0:T(8,128)(2,1)S(1)} %collective-permute-done.2.lo_ref) | copy-start | bytes 98308
  112.4 0.6 copy-start.3
Sparse Core Ops, SparseCore 0:
  10.1 73.8 all-gather.4

commit v9 on v8

--- a/solution.py
+++ b/solution.py
@@ -1,3 +1,5 @@
+import functools
+
 import jax
 import jax.numpy as jnp
 from jax import lax
@@ -26,6 +28,7 @@
 CPL0 = BAS0 + LEAVES // 2 * ROWS
 HELD = CPL0 + FAR_K * 8
 HALF = FAR_K * 32
+CHUNKS = 4
 BATCH = 8
 CLUS = ("x", "z", "core")
 TOP = (((0,), (0,)), ((), ()))
@@ -65,13 +68,24 @@
     return moves
 
 
-def stack_kernel(near_ref, b_ref, c_ref, out_ref):
-    out_ref[:BAS0] = near_ref[...].reshape(BAS0, PANEL)
+def stack_kernel(near_ref, b_ref, c_ref, out_ref, near_scr, rest_scr, sems, out_sems):
+    size = BAS0 // CHUNKS
+    moves = fetch([(near_ref.at[pl.ds(size * n, size)], near_scr.at[n]) for n in range(CHUNKS)], sems)
     for m in range(LEAVES // 2):
-        row = BAS0 + ROWS * m
-        out_ref[row : row + ROWS] = jnp.concatenate([b_ref[2 * m], b_ref[2 * m + 1]], axis=1)
+        rest_scr[ROWS * m : ROWS * (m + 1)] = jnp.concatenate([b_ref[2 * m], b_ref[2 * m + 1]], axis=1)
     both = jnp.concatenate([c_ref[0].astype(F32), c_ref[1].astype(F32)], axis=2)
-    out_ref[CPL0:] = both.reshape(FAR_K * 8, 128).astype(BF)
+    rest_scr[CPL0 - BAS0 :] = both.reshape(FAR_K * 8, 128).astype(BF)
+    sends = [
+        pltpu.make_async_copy(near_scr.at[n], out_ref.at[pl.ds(size * n, size)], out_sems.at[n])
+        for n in range(CHUNKS)
+    ]
+    sends.append(pltpu.make_async_copy(rest_scr, out_ref.at[pl.ds(BAS0, HELD - BAS0)], out_sems.at[CHUNKS]))
+    sends[CHUNKS].start()
+    for n in range(CHUNKS):
+        moves[n].wait()
+        sends[n].start()
+    for send in sends:
+        send.wait()
 
 
 def prepare_kernel(d_ref, b_ref, t_ref, out_ref):
@@ -132,16 +146,16 @@
             v_scr[PACK * (start + n) + l] = tile[:, COLS * l : COLS * (l + 1)]
 
 
-def near_field(idx_ref, copies, near_scr, v_scr):
-    for start in range(0, LEAVES, BATCH):
-        for i in range(start, start + BATCH):
-            copies[i].wait()
+def near_field(idx_ref, copies, near_scr, v_scr, leaves=range(LEAVES), batch=BATCH):
+    for start in range(0, len(leaves), batch):
+        for n in range(start, start + batch):
+            copies[n].wait()
         cols = []
-        for i in range(start, start + BATCH):
-            parts = [near_scr[i, :, ROWS * k : ROWS * (k + 1), :].reshape(PANEL, PANEL) for k in range(NEAR_K)]
-            rhs = jnp.concatenate([v_scr[idx_ref[i, k]] for k in range(NEAR_K)], axis=0)
+        for n in range(start, start + batch):
+            parts = [near_scr[n, :, ROWS * k : ROWS * (k + 1), :].reshape(PANEL, PANEL) for k in range(NEAR_K)]
+            rhs = jnp.concatenate([v_scr[idx_ref[leaves[n], k]] for k in range(NEAR_K)], axis=0)
             cols.append(dot(jnp.concatenate(parts, axis=1), rhs))
-        for n in range(0, BATCH, PACK):
+        for n in range(0, batch, PACK):
             yield jnp.concatenate(cols[n : n + PACK], axis=1)
 
 
@@ -198,22 +212,25 @@
         side.wait()
 
 
-def near_kernel(idx_ref, w_ref, vec_ref, lo_ref, hi_ref, out_ref, near_scr, v_scr, sems):
-    copies = near_copies(w_ref, near_scr, sems, range(LEAVES))
-    for copy in copies[:BATCH]:
+def near_kernel(groups, idx_ref, w_ref, vec_ref, *refs):
+    *ends, out_ref, near_scr, v_scr, sems = refs
+    leaves = [i for g in groups for i in range(PACK * g, PACK * (g + 1))]
+    copies = near_copies(w_ref, near_scr, sems, leaves)
+    for copy in copies:
         copy.start()
-    tiles = [lo_ref[...]] + [vec_ref[:, g] for g in range(GROUPS)] + [hi_ref[...]]
-    unpack(0, [tile.reshape(PANEL, 128) for tile in tiles], v_scr)
-    for copy in copies[BATCH:]:
-        copy.start()
-    for g, near in enumerate(near_field(idx_ref, copies, near_scr, v_scr)):
-        out_ref[g] = near
-
-
-def last_kernel(far_ref, pc_ref, cpl_ref, u_ref, near_ref, own_ref, out_ref, rhs_scr):
+    tiles = [vec_ref[:, g] for g in range(GROUPS)]
+    unpack(1, [tile.reshape(PANEL, 128) for tile in tiles], v_scr)
+    for start, ref in zip((0, GROUPS + 1), ends):
+        unpack(start, [ref[...].reshape(PANEL, 128)], v_scr)
+    for n, near in enumerate(near_field(idx_ref, copies, near_scr, v_scr, leaves, PACK)):
+        out_ref[n] = near
+
+
+def last_kernel(far_ref, pc_ref, cpl_ref, u_ref, mid_ref, edge_ref, own_ref, out_ref, rhs_scr):
     coef = far_sums(far_ref, pc_ref, (cpl_ref[0], cpl_ref[1]), rhs_scr)
     for g in range(GROUPS):
-        res = (near_ref[g] + far_field(u_ref[g], coef[g // 2])).astype(BF)
+        near = mid_ref[g - 1] if 0 < g < GROUPS - 1 else edge_ref[g // (GROUPS - 1)]
+        res = (near + far_field(u_ref[g], coef[g // 2])).astype(BF)
         out_ref[:, 0, g] = own_ref[:, g]
         out_ref[:, 1, g] = res.reshape(SHARES, ROWS, 128)
 
@@ -264,9 +281,17 @@
     near_sems = pltpu.SemaphoreType.DMA((LEAVES,))
 
     mine = call(
-        stack_kernel, array(HELD, PANEL), [VMEM] * 3, [], 0, 1_400_000,
-        near_blocks, basis, jnp.swapaxes(coupling, 2, 3),
-    )
+        stack_kernel, (array(HELD, PANEL),), [ANY] + [VMEM] * 2,
+        [
+            pltpu.VMEM((CHUNKS, BAS0 // CHUNKS, PANEL), BF),
+            pltpu.VMEM((HELD - BAS0, PANEL), BF),
+            pltpu.SemaphoreType.DMA((CHUNKS,)),
+            pltpu.SemaphoreType.DMA((CHUNKS + 1,)),
+        ],
+        0, 1_400_000,
+        near_blocks.reshape(BAS0, PANEL), basis, jnp.swapaxes(coupling, 2, 3),
+        sides=1,
+    )[0]
     held = lax.all_gather(mine, "y", axis=0)
     near_idx = near_list - (lax.axis_index(CLUS) * LEAVES - NWIN)
     near_idx = jnp.clip(near_idx, 0, LEAVES + 2 * NWIN - 1)
@@ -275,9 +300,7 @@
         density, basis, transfer,
     )
     recv = lax.all_to_all(sent, "y", 0, 0)
-    parents, bottom, top = call(
-        parent_kernel, (spread_out, share, share), [VMEM], [], 100_000, 500_000, recv
-    )
+    parents, bottom, top = call(parent_kernel, (spread_out, share, share), [VMEM], [], 100_000, 500_000, recv)
     every = lax.all_gather(exchange(parents), "core", axis=0)
     low, high = halo(bottom, top)
     first, parents, bottom, top, cpl, u = call(
@@ -307,16 +330,27 @@
     )
     plane = exchange(parents)
     low, high = halo(bottom, top)
-    near = call(
-        near_kernel, array(GROUPS, PANEL, 128, dtype=F32), [SMEM, ANY] + [VMEM] * 3,
-        [near_scratch, vec_scratch, near_sems], 300_000_000, 6_000_000,
+    half = array(GROUPS // 2, PANEL, 128, dtype=F32)
+    half_scratch = [
+        pltpu.VMEM((LEAVES // 2, SHARES, NEAR_K * ROWS, PANEL), BF),
+        vec_scratch,
+        pltpu.SemaphoreType.DMA((LEAVES // 2,)),
+    ]
+    mid = call(
+        functools.partial(near_kernel, (1, 2)), half, [SMEM, ANY, VMEM],
+        half_scratch, 150_000_000, 3_000_000,
+        near_idx, held, first,
+    )
+    edge = call(
+        functools.partial(near_kernel, (0, 3)), half, [SMEM, ANY] + [VMEM] * 3,
+        half_scratch, 150_000_000, 3_000_000,
         near_idx, held, first, low, high,
     )
     every = lax.all_gather(plane, "core", axis=0)
     sent = call(
-        last_kernel, array(SHARES, 2, GROUPS, ROWS, 128), [SMEM] + [VMEM] * 5,
+        last_kernel, array(SHARES, 2, GROUPS, ROWS, 128), [SMEM] + [VMEM] * 6,
         [rhs_scratch], 100_000_000, 2_000_000,
-        far_list, every, cpl, u, near, first,
+        far_list, every, cpl, u, mid, edge, first,
     )
     out = array(LEAVES, ROWS, 256)
     return call(finish_kernel, (out, out), [VMEM], [], 0, 600_000, lax.all_to_all(sent, "y", 0, 0))

time: 150 us -> 151 us (level)
  waiting for transfers between devices: 29.3 us -> 24.4 us
  Pallas kernels: 24.4 us -> 28 us
    ppermute x2, waiting for transfers between devices: 3.79 us -> 0.01 us  [halo(): lax.ppermute(bottom, CLUS, backward)]
    pallas_call x7 -> x8, Pallas kernels: 24.4 us -> 28 us  [call(): pl.pallas_call(kernel, out_shape=outs, in_specs=ins, out_specs=VMEM if si...]
  transfers between devices with their start and end apart: 7 -> 7, of which waited for: 3 -> 1; matrix products, arithmetic and copies ran while one was open for 1% -> 1% of each run, Pallas kernels for 6% -> 8%
where the time goes in v9:
time: 151 us; the launch traced here: 149 us
  blocking collectives  41.4 us (27%)
  starting transfers between devices  38.1 us (25%)
  Pallas kernels  28 us (19%)
  waiting for transfers between devices  24.4 us (16%)
  between operations  14.2 us (9%)
    pallas_call x8, Pallas kernels, call(): pl.pallas_call(kernel, out_shape=outs, in_specs=ins, out_specs=VMEM if si...  28 us
    all_gather x1, waiting for transfers between devices, operator_twice(): held = lax.all_gather(mine, 'y', axis=0)  24.3 us
    all_to_all x2, starting transfers between devices, exchange(): return lax.all_to_all(values, ('x', 'z'), 0, 0)  23.3 us
    all_to_all x1, blocking collectives, operator_twice(): recv = lax.all_to_all(sent, 'y', 0, 0)  16.5 us
    all_to_all x1, blocking collectives, operator_twice(): lax.all_to_all(sent, 'y', 0, 0)  16.3 us
    ppermute x2, starting transfers between devices, halo(): lax.ppermute(top, CLUS, forward)  10.9 us
    all_gather x1, blocking collectives, operator_twice(): every = lax.all_gather(exchange(parents), 'core', axis=0)  6.33 us
    ppermute x2, starting transfers between devices, halo(): lax.ppermute(bottom, CLUS, backward)  3.84 us
  transfers between devices with their start and end apart: 7, of which 1 were waited for; matrix products, arithmetic and copies ran while one was open for 1% of the time, Pallas kernels for 8%

profile of v9, /device:TPU:1, one launch (start us, length us, event | category | flops | bytes accessed | tf_op | source)
XLA Modules:
  0.0 148.6 jit_solution(16654044435141797407)
XLA Ops:
  7.2 0.0 all-gather.5.cloned.1.call-start
  7.2 2.8 %shard_map.88 = bf16[2648,128]{1,0:T(8,128)(2,1)} custom-call(bf16[2304,128]{1,0:T(8,128)(2,1)} %bitcast.10, bf16[16,16,64]{2,1,0:T(8,128)(2,1)} %b_ref.3, bf16[2,27,8,64]{3,2,1,0:T(8,128)(2,1)} %bitcast.11), custom_call_target="tpu_custom_call" | custom-call | bytes 1400000 | tf_op jit(solution)/shard_map/pallas_call | solution.py:254
  10.1 2.4 %shard_map.86 = bf16[8,96,128]{2,1,0:T(8,128)(2,1)} custom-call(bf16[16,16,256]{2,1,0:T(8,128)(2,1)} %d_ref.1, bf16[16,16,64]{2,1,0:T(8,128)(2,1)} %b_ref.3, bf16[16,64,64]{2,1,0:T(8,128)(2,1)} %t_in.1), custom_call_target="tpu_custom_call" | custom-call | flops 40000000 | bytes 500000 | tf_op jit(solution)/shard_map/pallas_call | solution.py:254
  12.4 16.5 %all_to_all.20.recv_ref = bf16[8,96,128]{2,1,0:T(8,128)(2,1)} all-to-all(bf16[8,96,128]{2,1,0:T(8,128)(2,1)} %shard_map.86), channel_id=1, replica_groups=mesh['x'=4,'z'=8,'core'=2,'y'=8] {'y'}, dimensions={0} | all-to-all | bytes 393216 | tf_op jit(solution)/shard_map/all_to_all | solution.py:302
  28.9 1.6 %shard_map.87 = (bf16[32,32,128]{2,1,0:T(8,128)(2,1)}, bf16[8,16,128]{2,1,0:T(8,128)(2,1)}, bf16[8,16,128]{2,1,0:T(8,128)(2,1)}) custom-call(bf16[8,96,128]{2,1,0:T(8,128)(2,1)} %all_to_all.20.recv_ref), custom_call_target="tpu_custom_call" | custom-call | flops 100000 | bytes 500000 | tf_op jit(solution)/shard_map/pallas_call | solution.py:254
  30.6 13.2 %all-to-all-start.1 = ((bf16[32,32,128]{2,1,0:T(8,128)(2,1)}), bf16[32,32,128]{2,1,0:T(8,128)(2,1)S(1)}, u32[]{:S(2)}, u32[]{:S(2)}) async-start(bf16[32,32,128]{2,1,0:T(8,128)(2,1)} %get-tuple-element.11), calls=%async_computation.1 | async-start | bytes 524288 | tf_op jit(solution)/shard_map/all_to_all | solution.py:265
  43.7 1.3 subtract_clamp_fusion.idx_ref
  45.0 6.5 %collective-permute-start = (bf16[8,16,128]{2,1,0:T(8,128)(2,1)}, bf16[8,16,128]{2,1,0:T(8,128)(2,1)S(1)}, u32[]{:S(2)}, u32[]{:S(2)}) collective-permute-start(bf16[8,16,128]{2,1,0:T(8,128)(2,1)} %get-tuple-element.12), channel_id=1, source_target_pairs={{0,8},{8,16},{16,24},{24,32},{32,40},{40,48},{48,56},{56,64},{64,7... | collective-permute-start | bytes 98312 | tf_op jit(solution)/shard_map/ppermute | solution.py:272
  51.5 1.9 %collective-permute-start.1 = (bf16[8,16,128]{2,1,0:T(8,128)(2,1)}, bf16[8,16,128]{2,1,0:T(8,128)(2,1)S(1)}, u32[]{:S(2)}, u32[]{:S(2)}) collective-permute-start(bf16[8,16,128]{2,1,0:T(8,128)(2,1)} %get-tuple-element.13), channel_id=1, source_target_pairs={{8,0},{16,8},{24,16},{32,24},{40,32},{48,40},{56,48},{64,56},{72,6... | collective-permute-start | bytes 98312 | tf_op jit(solution)/shard_map/ppermute | solution.py:272
  53.4 0.0 all-to-all-done.1
  53.5 6.3 %all-gather = bf16[64,32,128]{2,1,0:T(8,128)(2,1)} all-gather(bf16[32,32,128]{2,1,0:T(8,128)(2,1)S(1)} %all-to-all-done.1), channel_id=2, replica_groups=mesh['x'=4,'z'=8,'core'=2,'y'=8] {'core'}, dimensions={0}, use_global_device_ids=true | all-gather | bytes 786432 | tf_op jit(solution)/shard_map/all_gather | solution.py:304
  59.8 24.3 %all-gather.5.cloned.1.call-done = bf16[21184,128]{1,0:T(8,128)(2,1)} async-done(((bf16[2648,128]{1,0:T(8,128)(2,1)}), bf16[21184,128]{1,0:T(8,128)(2,1)}) %all-gather.5.cloned.1.call-update) | async-done | bytes 5423120 | tf_op jit(solution)/shard_map/all_gather | solution.py:295
  84.1 8.1 %shard_map.89 = (bf16[8,4,16,128]{3,2,1,0:T(8,128)(2,1)}, bf16[32,32,128]{2,1,0:T(8,128)(2,1)}, bf16[8,16,128]{2,1,0:T(8,128)(2,1)}, bf16[8,16,128]{2,1,0:T(8,12...) custom-call(s32[2,27]{1,0:T(2,128)} %far_ref.3, s32[16,9]{1,0:T(8,128)} %subtract_clamp_fusion.idx_ref, ...), custom_call_target="tpu_custom_call" | custom-call | flops 400000000 | bytes 8000000 | tf_op jit(solution)/shard_map/pallas_call | solution.py:254
  92.2 10.2 %all-to-all-start.2 = ((bf16[32,32,128]{2,1,0:T(8,128)(2,1)}), bf16[32,32,128]{2,1,0:T(8,128)(2,1)S(1)}, u32[]{:S(2)}, u32[]{:S(2)}) async-start(bf16[32,32,128]{2,1,0:T(8,128)(2,1)} %get-tuple-element.14), calls=%async_computation.2 | async-start | bytes 524288 | tf_op jit(solution)/shard_map/all_to_all | solution.py:265
  102.4 4.4 %collective-permute-start.2 = (bf16[8,16,128]{2,1,0:T(8,128)(2,1)}, bf16[8,16,128]{2,1,0:T(8,128)(2,1)S(1)}, u32[]{:S(2)}, u32[]{:S(2)}) collective-permute-start(bf16[8,16,128]{2,1,0:T(8,128)(2,1)} %get-tuple-element.18), channel_id=1, source_target_pairs={{0,8},{8,16},{16,24},{24,32},{32,40},{40,48},{48,56},{56,64},{64,7... | collective-permute-start | bytes 98312 | tf_op jit(solution)/shard_map/ppermute | solution.py:272
  106.8 1.9 %collective-permute-start.3 = (bf16[8,16,128]{2,1,0:T(8,128)(2,1)}, bf16[8,16,128]{2,1,0:T(8,128)(2,1)S(1)}, u32[]{:S(2)}, u32[]{:S(2)}) collective-permute-start(bf16[8,16,128]{2,1,0:T(8,128)(2,1)} %get-tuple-element.19), channel_id=1, source_target_pairs={{8,0},{16,8},{24,16},{32,24},{40,32},{48,40},{56,48},{64,56},{72,6... | collective-permute-start | bytes 98312 | tf_op jit(solution)/shard_map/ppermute | solution.py:272
  108.8 4.0 %shard_map.90.mid_ref = f32[2,128,128]{2,1,0:T(8,128)} custom-call(s32[16,9]{1,0:T(8,128)} %subtract_clamp_fusion.idx_ref, bf16[8,2648,128]{2,1,0:T(8,128)(2,1)} %bitcast.6, bf16[8,4,16,128]{3,2,1,0:T(8,128)(2,1)} %get-tuple-element.17.vec_ref.own_ref), custom_call_target="tpu_custom_call" | custom-call | flops 150000000 | bytes 3000000 | tf_op jit(solution)/shard_map/pallas_call | solution.py:254
  112.8 0.6 copy-done.2
  113.4 0.6 copy-done.3
  114.0 4.0 %shard_map.91.edge_ref = f32[2,128,128]{2,1,0:T(8,128)} custom-call(s32[16,9]{1,0:T(8,128)} %subtract_clamp_fusion.idx_ref, bf16[8,2648,128]{2,1,0:T(8,128)(2,1)} %bitcast.7, bf16[8,4,16,128]{3,2,1,0:T(8,128)(2,1)} %get-tuple-element.17.vec_ref.own_ref, bf16[8,16,128]{2,1,0:T(8,128)(2,1)} %copy-done.2, bf16[8,16,128]{2,1,0:T(8,128)(2,1)} %copy-done.3), custom_call_target="tpu_custom_call" | custom-call | flops 150000000 | bytes 3000000 | tf_op jit(solution)/shard_map/pallas_call | solution.py:254
  118.0 2.3 %all-gather.2 = bf16[64,32,128]{2,1,0:T(8,128)(2,1)} all-gather(bf16[32,32,128]{2,1,0:T(8,128)(2,1)S(1)} %all-to-all-done.2), channel_id=4, replica_groups=mesh['x'=4,'z'=8,'core'=2,'y'=8] {'core'}, dimensions={0}, use_global_device_ids=true | all-gather | bytes 786432 | tf_op jit(solution)/shard_map/all_gather | solution.py:349
  120.3 3.3 %shard_map.92 = bf16[8,2,4,16,128]{4,3,2,1,0:T(8,128)(2,1)} custom-call(s32[2,27]{1,0:T(2,128)} %far_ref.3, bf16[2,32,32,128]{3,2,1,0:T(8,128)(2,1)} %bitcast.8, bf16[2,128,864]{2,1,0:T(8,128)(2,1)} %get-tuple-element.15.cpl_ref, bf16[4,128,256]{2,1,0:T(8,128)(2,1)} %get-tuple-element.16.u_ref, f32[2,128,128]{2,1,0:T(8,128)} %shard_map.90.mid_ref, ...), custom_call_target="tpu_custom_call" | custom-call | flops 100000000 | bytes 2000000 | tf_op jit(solution)/shard_map/pallas_call | solution.py:254
  123.6 16.3 %all_to_all.21.recv_ref = bf16[8,2,4,16,128]{4,3,2,1,0:T(8,128)(2,1)} all-to-all(bf16[8,2,4,16,128]{4,3,2,1,0:T(8,128)(2,1)} %shard_map.92), channel_id=1, replica_groups=mesh['x'=4,'z'=8,'core'=2,'y'=8] {'y'}, dimensions={0} | all-to-all | bytes 524288 | tf_op jit(solution)/shard_map/all_to_all | solution.py:356
  139.9 1.9 %shard_map.93 = (bf16[16,16,256]{2,1,0:T(8,128)(2,1)}, bf16[16,16,256]{2,1,0:T(8,128)(2,1)}) custom-call(bf16[8,2,4,16,128]{4,3,2,1,0:T(8,128)(2,1)} %all_to_all.21.recv_ref), custom_call_target="tpu_custom_call" | custom-call | bytes 600000 | tf_op jit(solution)/shard_map/pallas_call | solution.py:254
  (12 shorter events, 0.0 us)
Async XLA Ops:
  7.2 77.0 %all-gather.5.cloned.1.call-start = ((), (), s32[]{:S(2)}) async-start(), calls=%async_computation.4 | async-start | bytes 6100992 | tf_op jit(solution)/shard_map/all_gather | solution.py:295
  30.6 22.9 %all-to-all-start.1 = ((bf16[32,32,128]{2,1,0:T(8,128)(2,1)}), bf16[32,32,128]{2,1,0:T(8,128)(2,1)S(1)}, u32[]{:S(2)}, u32[]{:S(2)}) async-start(bf16[32,32,128]{2,1,0:T(8,128)(2,1)} %get-tuple-element.11), calls=%async_computation.1 | async-start | bytes 524288 | tf_op jit(solution)/shard_map/all_to_all | solution.py:265
  45.0 14.8 %collective-permute-start = (bf16[8,16,128]{2,1,0:T(8,128)(2,1)}, bf16[8,16,128]{2,1,0:T(8,128)(2,1)S(1)}, u32[]{:S(2)}, u32[]{:S(2)}) collective-permute-start(bf16[8,16,128]{2,1,0:T(8,128)(2,1)} %get-tuple-element.12), channel_id=1, source_target_pairs={{0,8},{8,16},{16,24},{24,32},{32,40},{40,48},{48,56},{56,64},{64,7... | collective-permute-start | bytes 98312 | tf_op jit(solution)/shard_map/ppermute | solution.py:272
  51.5 8.3 %collective-permute-start.1 = (bf16[8,16,128]{2,1,0:T(8,128)(2,1)}, bf16[8,16,128]{2,1,0:T(8,128)(2,1)S(1)}, u32[]{:S(2)}, u32[]{:S(2)}) collective-permute-start(bf16[8,16,128]{2,1,0:T(8,128)(2,1)} %get-tuple-element.13), channel_id=1, source_target_pairs={{8,0},{16,8},{24,16},{32,24},{40,32},{48,40},{56,48},{64,56},{72,6... | collective-permute-start | bytes 98312 | tf_op jit(solution)/shard_map/ppermute | solution.py:272
  59.8 24.3 %copy-start = (bf16[8,16,128]{2,1,0:T(8,128)(2,1)}, bf16[8,16,128]{2,1,0:T(8,128)(2,1)S(1)}, u32[]{:S(2)}) copy-start(bf16[8,16,128]{2,1,0:T(8,128)(2,1)S(1)} %collective-permute-done.lo_ref) | copy-start | bytes 98308
  59.8 24.3 %copy-start.1 = (bf16[8,16,128]{2,1,0:T(8,128)(2,1)}, bf16[8,16,128]{2,1,0:T(8,128)(2,1)S(1)}, u32[]{:S(2)}) copy-start(bf16[8,16,128]{2,1,0:T(8,128)(2,1)S(1)} %collective-permute-done.1.hi_ref) | copy-start | bytes 98308
  92.2 25.7 %all-to-all-start.2 = ((bf16[32,32,128]{2,1,0:T(8,128)(2,1)}), bf16[32,32,128]{2,1,0:T(8,128)(2,1)S(1)}, u32[]{:S(2)}, u32[]{:S(2)}) async-start(bf16[32,32,128]{2,1,0:T(8,128)(2,1)} %get-tuple-element.14), calls=%async_computation.2 | async-start | bytes 524288 | tf_op jit(solution)/shard_map/all_to_all | solution.py:265
  102.4 10.3 %collective-permute-start.2 = (bf16[8,16,128]{2,1,0:T(8,128)(2,1)}, bf16[8,16,128]{2,1,0:T(8,128)(2,1)S(1)}, u32[]{:S(2)}, u32[]{:S(2)}) collective-permute-start(bf16[8,16,128]{2,1,0:T(8,128)(2,1)} %get-tuple-element.18), channel_id=1, source_target_pairs={{0,8},{8,16},{16,24},{24,32},{32,40},{40,48},{48,56},{56,64},{64,7... | collective-permute-start | bytes 98312 | tf_op jit(solution)/shard_map/ppermute | solution.py:272
  106.8 5.9 %collective-permute-start.3 = (bf16[8,16,128]{2,1,0:T(8,128)(2,1)}, bf16[8,16,128]{2,1,0:T(8,128)(2,1)S(1)}, u32[]{:S(2)}, u32[]{:S(2)}) collective-permute-start(bf16[8,16,128]{2,1,0:T(8,128)(2,1)} %get-tuple-element.19), channel_id=1, source_target_pairs={{8,0},{16,8},{24,16},{32,24},{40,32},{48,40},{56,48},{64,56},{72,6... | collective-permute-start | bytes 98312 | tf_op jit(solution)/shard_map/ppermute | solution.py:272
  112.8 0.6 copy-start.2
  113.4 0.6 copy-start.3
Sparse Core Ops, SparseCore 0:
  10.2 73.8 all-gather.4
